TPU v7x, 32 devices: a whole 2x2x4 slice. The times are simulated.
32 devices in a mesh: seq: 16 (over z, y, core), head: 2 (over x).
Axes of the slice: x: 2, y: 2, z: 4, core: 2. Of those that a mesh axis runs over, the one named last changes fastest.
Arguments:
- projected: bfloat16 [16384, 4096], P(('seq', 'head')), may hold values from -6 to 6
- conv_weight: bfloat16 [4, 4096], P(None, 'head'), may hold values from -3 to 3
- log_gate: float32 [16, 16384], P('head', 'seq'), may hold values from -0.9 to 0
- write_rate: float32 [16, 16384], P('head', 'seq'), may hold values from 0 to 0.9
- norm_gain: float32 [128], replicated, may hold values from 0.5 to 1.5
Outputs:
- mixed_out: bfloat16 [16384, 2048], P(('seq', 'head'))
All inputs are finite; a program needn't handle non-finite values.
Results may differ from a plain program's by a relative error of at most 0.012.
Values may be sent and summed in bfloat16 or wider, within the bound.
No kernel may reach another device: no remote copies, remote signals or barrier semaphores. Data moves between devices by JAX's collectives and lax.ppermute only.
A program may use at most 64 MiB of HBM per device.

v0:
```python
import jax
import jax.numpy as jnp
from jax import lax
from jax.sharding import PartitionSpec as P

DK = 128
V_GROUP = 2
KW = 4
STRETCH = 128


PRECISE = lax.Precision.HIGHEST


def shifted(block, axis, distance):
    devices = range(lax.axis_size(axis))
    route = [(i - distance, i) for i in devices if i - distance in devices]
    return lax.ppermute(block, axis, route)


def prepare(key_rows, values, gates, rates):
    span = key_rows.shape[-2]
    width = key_rows.shape[-1]
    cumulative = jnp.cumsum(gates, axis=-1)
    index_of_row = lax.broadcasted_iota(jnp.int32, (span, span), 0)
    col_index = lax.broadcasted_iota(jnp.int32, (span, span), 1)
    inside_mask = index_of_row >= col_index
    below_mask = index_of_row > col_index
    spread = cumulative[..., :, None] - cumulative[..., None, :]
    decay_mat = jnp.where(inside_mask, jnp.exp(jnp.where(inside_mask, spread, 0.0)), 0.0)
    intersection = jnp.einsum("...td,...sd->...ts", key_rows, key_rows, precision=PRECISE)
    lower_part = jnp.where(below_mask, rates[..., :, None] * intersection * decay_mat, 0.0)
    system = lower_part + jnp.eye(span, dtype=jnp.float32)
    right_side = jnp.concatenate(
        [rates[..., None] * values, (rates * jnp.exp(cumulative))[..., None] * key_rows], axis=-1
    )
    solved = lax.linalg.triangular_solve(
        system, right_side, left_side=True, lower=True, unit_diagonal=True
    )
    return (cumulative, decay_mat, solved[..., :width], solved[..., width:])


def apply_state(queries, key_rows, cumulative, decay_mat, fresh, carried, state):
    written = fresh - jnp.einsum("...ce,...ef->...cf", carried, state, precision=PRECISE)
    scores = jnp.einsum("...td,...sd->...ts", queries, key_rows, precision=PRECISE) * decay_mat
    output = jnp.exp(cumulative)[..., None] * jnp.einsum(
        "...cd,...de->...ce", queries, state, precision=PRECISE
    )
    output = output + jnp.einsum("...ts,...se->...te", scores, written, precision=PRECISE)
    return (output, written)


def head_rows(convolved):
    count_rows = convolved.shape[0]
    grouped = convolved.astype(jnp.float32).reshape(count_rows, -1, 2 + V_GROUP, DK)
    queries = grouped[:, :, 0]
    key_rows = grouped[:, :, 1]
    key_rows = key_rows * lax.rsqrt(jnp.sum(key_rows * key_rows, axis=-1, keepdims=True) + 1e-06)
    queries = jnp.repeat(queries, V_GROUP, axis=1)
    key_rows = jnp.repeat(key_rows, V_GROUP, axis=1)
    values = grouped[:, :, 2:].reshape(count_rows, -1, DK)
    return (
        jnp.transpose(queries, (1, 0, 2)),
        jnp.transpose(key_rows, (1, 0, 2)),
        jnp.transpose(values, (1, 0, 2)),
    )


def normalize(output, norm_gain):
    return output * lax.rsqrt(jnp.mean(output * output, axis=-1, keepdims=True) + 1e-06) * norm_gain


def matmul_high(left, right):
    return jnp.einsum("...ij,...jk->...ik", left, right, precision=PRECISE)


def per_device(projected, conv_weight, log_gate, write_rate, norm_gain):
    local_rows = lax.all_to_all(projected, "head", split_axis=1, concat_axis=0, tiled=True)
    length = local_rows.shape[0]
    earlier = shifted(local_rows[length - (KW - 1) :], "seq", 1)
    padded = jnp.concatenate([earlier, local_rows], axis=0)
    weight = conv_weight.astype(jnp.float32)
    summed = padded[0:length].astype(jnp.float32) * weight[0]
    for start_displacement in range(1, KW):
        summed = (
            summed
            + padded[start_displacement : start_displacement + length].astype(jnp.float32)
            * weight[start_displacement]
        )
    convolved = jax.nn.silu(summed).astype(jnp.bfloat16)
    queries, key_rows, values = head_rows(convolved)
    heads = log_gate.shape[0]
    number = length // STRETCH
    queries = queries.reshape(heads, number, STRETCH, DK)
    key_rows = key_rows.reshape(heads, number, STRETCH, DK)
    values = values.reshape(heads, number, STRETCH, DK)
    gates = log_gate.reshape(heads, number, STRETCH)
    rates = write_rate.reshape(heads, number, STRETCH)
    cumulative, decay_mat, fresh, carried = prepare(key_rows, values, gates, rates)
    tail_decay = jnp.exp(cumulative[..., -1:] - cumulative)
    weighted = key_rows * tail_decay[..., None]
    identity = jnp.eye(DK, dtype=jnp.float32)
    transit = jnp.exp(cumulative[..., -1])[..., None, None] * identity - jnp.einsum(
        "...cd,...ce->...de", weighted, carried, precision=PRECISE
    )
    inject = jnp.einsum("...cd,...ce->...de", weighted, fresh, precision=PRECISE)
    block_transit = jnp.moveaxis(transit, 1, 0)
    block_inject = jnp.moveaxis(inject, 1, 0)
    zero_state = jnp.zeros((heads, DK, DK), jnp.float32)
    start_transit = jnp.broadcast_to(identity, (heads, DK, DK))

    def compose(carry, pieces):
        return (
            (matmul_high(pieces[0], carry[0]), matmul_high(pieces[0], carry[1]) + pieces[1]),
            None,
        )

    (device_transit, device_state), unused = lax.scan(
        compose, (start_transit, zero_state), (block_transit, block_inject)
    )

    def relay_step(position, incoming):
        outgoing = matmul_high(device_transit, incoming) + device_state
        return shifted(outgoing, "seq", 1)

    entering = lax.fori_loop(0, lax.axis_size("seq") - 1, relay_step, zero_state)

    def advance(state, pieces):
        return (matmul_high(pieces[0], state) + pieces[1], state)

    unused_end, starts = lax.scan(advance, entering, (block_transit, block_inject))
    starts = jnp.moveaxis(starts, 0, 1)
    output, written = apply_state(queries, key_rows, cumulative, decay_mat, fresh, carried, starts)
    normed = normalize(output, norm_gain).astype(jnp.bfloat16)
    arranged = jnp.transpose(normed.reshape(heads, length, DK), (1, 0, 2)).reshape(
        length, heads * DK
    )
    return lax.all_to_all(arranged, "head", split_axis=0, concat_axis=1, tiled=True)


def solution(mesh):
    in_specs = (P(("seq", "head"), None), P(None, "head"), P("head", "seq"), P("head", "seq"), P())
    out_specs = P(("seq", "head"), None)
    return jax.shard_map(
        per_device, mesh=mesh, in_specs=in_specs, out_specs=out_specs, check_vma=False
    )
```

profile of v0, /device:TPU:16, one launch (start us, length us, event | category | flops | bytes accessed | tf_op | source)
XLA Modules:
  0.0 1101.7 jit_solution(17238046256000215025)
XLA Ops:
  0.0 6.5 copy.30
  14.9 44.9 %all-to-all-done = bf16[512,2,2048]{0,2,1:T(8,128)(2,1)} async-done(((bf16[512,2,2048]{0,2,1:T(8,128)(2,1)}), bf16[512,2,2048]{0,2,1:T(8,128)(2,1)}, u32[]{:S(2)}, u32[]{:S(2)}) %all-to-all-start) | async-done | bytes 4194336 | tf_op jit(solution)/shard_map/all_to_all | solution.py:78
  72.9 15.1 %fusion.27 = f32[1024,2048]{1,0:T(8,128)} fusion(f32[2048]{0:T(1024)S(1)} %bitcast.140, bf16[1024,2048]{1,0:T(8,128)(2,1)} %bitcast.125, f32[2048]{0:T(1024)S(1)} %bitcast.139, bf16[3,2048]{1,0:T(4,128)(2,1)S(1)} %collective-permute-done.1, f32[2048]{0:T(1024)S(1)} %bitcast.138, f32[2048]{0:T(1024)S(1)} %bitcast.137), kind=kLoop, calls=%fused_computation.41 | loop fusion | flops 54525952 | bytes 12627968 | tf_op jit(solution)/shard_map/reshape | solution.py:55
  88.0 9.3 copy.32
  124.5 11.0 add_bitcast_fusion
  135.5 630.2 %custom-call.3 = f32[8,8,1,128,128]{3,4,2,1,0:T(8,128)} custom-call(f32[8,8,1,128,128]{4,3,2,1,0:T(8,128)} %add_bitcast_fusion), custom_call_target="InvertDiagBlocksLowerTriangular" | custom-call | tf_op jit(solution)/shard_map/triangular_solve | solution.py:37
  769.4 10.5 fusion.57
  782.4 11.4 %fusion.14 = f32[8,8,128,256]{3,2,1,0:T(8,128)S(1)} fusion(f32[8,8,128,128]{3,2,1,0:T(8,128)S(1)} %get-tuple-element.163, f32[8,8,128,128]{3,2,1,0:T(8,128)} %broadcast_multiply_fusion.1, f32[8,8,1,128,128]{3,4,2,1,0:T(8,128)} %custom-call.3), kind=kOutput, calls=%fused_computation.18 | convolution fusion | flops 3223322624 | bytes 20971520 | tf_op jit(solution)/shard_map/triangular_solve | solution.py:37
  793.8 7.5 fusion.35
  801.2 9.3 bitcast_subtract_fusion
  813.1 29.4 %while.40 = (s32[]{:T(128)}, f32[8,128,128]{2,1,0:T(8,128)S(1)}, f32[8,128,128]{2,1,0:T(8,128)S(1)}, f32[8,8,128,128]{3,2,1,0:T(8,128)}, f32[8,8,128,128]{3,2,1,0:T(8,128)}) while((s32[]{:T(128)}, f32[8,128,128]{2,1,0:T(8,128)S(1)}, f32[8,128,128]{2,1,0:T(8,128)S(1)}, f32[8,8,128,128]{3,2,1,0:T(8,128)}, ...), condition=%wide.region_3.4_spmd.clone.clone, body=%wide.region_2.3_spmd.clone.sunk.clone | while | flops 402915328 | bytes 5768786 | solution.py:118
  842.6 180.8 %while.38 = (s32[]{:T(128)}, f32[8,128,128]{2,1,0:T(8,128)S(1)}, f32[8,128,128]{2,1,0:T(8,128)S(1)}, f32[8,128,128]{2,1,0:T(8,128)S(1)}) while((s32[]{:T(128)}, f32[8,128,128]{2,1,0:T(8,128)S(1)}, f32[8,128,128]{2,1,0:T(8,128)S(1)}, f32[8,128,128]{2,1,0:T(8,128)S(1)}) %tuple.75), condition=%wide.region_5.6_spmd.clone, body=%wide.region_4.5_spmd.sunk.clone | while | flops 201457664 | bytes 4194397 | solution.py:126
  845.2 9.5 collective-permute-done
  857.2 9.5 collective-permute-done
  869.3 9.5 collective-permute-done
  881.3 9.5 collective-permute-done
  893.4 9.5 collective-permute-done
  905.4 9.5 collective-permute-done
  917.5 9.5 collective-permute-done
  929.5 9.5 collective-permute-done
  941.6 9.5 collective-permute-done
  953.6 9.5 collective-permute-done
  965.7 9.5 collective-permute-done
  977.8 9.5 collective-permute-done
  989.8 9.5 collective-permute-done
  1001.9 9.5 collective-permute-done
  1013.9 9.5 collective-permute-done
  1023.4 22.0 %while.39 = (s32[]{:T(128)}, f32[8,128,128]{2,1,0:T(8,128)S(1)}, f32[8,8,128,128]{3,2,1,0:T(8,128)}, f32[8,8,128,128]{3,2,1,0:T(8,128)}, f32[8,8,128,128]{3,2,1,0:T(8,128)}) while((s32[]{:T(128)}, f32[8,128,128]{2,1,0:T(8,128)S(1)}, f32[8,8,128,128]{3,2,1,0:T(8,128)}, f32[8,8,128,128]{3,2,1,0:T(8,128)}, ...), condition=%wide.region_7.8_spmd.clone, body=%wide.region_6.7_spmd.sunk.clone | while | flops 201457664 | bytes 4195401 | solution.py:131
  1045.4 6.9 fusion.31
  1052.3 8.4 fusion.24
  1060.7 7.7 multiply_reduce_fusion
  1073.6 21.4 %all_to_all.38 = bf16[2,512,1024]{2,1,0:T(8,128)(2,1)S(1)} all-to-all(bf16[2,512,1024]{2,1,0:T(8,128)(2,1)} %all_to_all.32), channel_id=1, replica_groups=mesh['seq'=16,'head'=2] {'head'}, dimensions={0} | all-to-all | bytes 4194304 | tf_op jit(solution)/shard_map/all_to_all | solution.py:138
  (150 shorter events, 158.0 us)
Async XLA Ops:
  6.5 5.8 copy-start.10
  6.5 8.3 copy-start.8
  6.5 8.4 copy-start.9
  6.5 53.4 %all-to-all-start = ((bf16[512,2,2048]{0,2,1:T(8,128)(2,1)}), bf16[512,2,2048]{0,2,1:T(8,128)(2,1)}, u32[]{:S(2)}, u32[]{:S(2)}) async-start(bf16[512,2,2048]{0,2,1:T(8,128)(2,1)} %bitcast.126), calls=%async_computation | async-start | bytes 8388608 | tf_op jit(solution)/shard_map/all_to_all | solution.py:78
  66.9 6.0 collective-permute-start.1
  118.0 4.3 copy-start.7
  122.5 1.9 copy-start.1
  765.7 3.7 copy-start.2
  766.0 13.9 %copy-start.3 = (f32[1024,4,2,128]{3,0,2,1:T(8,128)}, f32[1024,4,2,128]{3,0,2,1:T(8,128)S(1)}, u32[]{:S(2)}) copy-start(f32[1024,4,2,128]{3,0,2,1:T(8,128)S(1)} %broadcast_in_dim.44) | copy-start | bytes 12582916
  793.8 7.5 copy-start
  843.2 11.4 %collective-permute-start = (f32[8,128,128]{2,1,0:T(8,128)S(1)}, f32[8,128,128]{2,1,0:T(8,128)S(1)}, u32[]{:S(2)}, u32[]{:S(2)}) collective-permute-start(f32[8,128,128]{2,1,0:T(8,128)S(1)} %convolution_add_fusion.9), channel_id=1, source_target_pairs={{0,2},{2,4},{4,6},{6,8},{8,10},{10,12},{12,14},{14,16},{16,18},{18... | collective-permute-start | bytes 1572872 | tf_op jit(solution)/shard_map/while/body/eval_jaxpr/ppermute | solution.py:18
  855.3 11.4 %collective-permute-start = (f32[8,128,128]{2,1,0:T(8,128)S(1)}, f32[8,128,128]{2,1,0:T(8,128)S(1)}, u32[]{:S(2)}, u32[]{:S(2)}) collective-permute-start(f32[8,128,128]{2,1,0:T(8,128)S(1)} %convolution_add_fusion.9), channel_id=1, source_target_pairs={{0,2},{2,4},{4,6},{6,8},{8,10},{10,12},{12,14},{14,16},{16,18},{18... | collective-permute-start | bytes 1572872 | tf_op jit(solution)/shard_map/while/body/eval_jaxpr/ppermute | solution.py:18
  867.3 11.4 %collective-permute-start = (f32[8,128,128]{2,1,0:T(8,128)S(1)}, f32[8,128,128]{2,1,0:T(8,128)S(1)}, u32[]{:S(2)}, u32[]{:S(2)}) collective-permute-start(f32[8,128,128]{2,1,0:T(8,128)S(1)} %convolution_add_fusion.9), channel_id=1, source_target_pairs={{0,2},{2,4},{4,6},{6,8},{8,10},{10,12},{12,14},{14,16},{16,18},{18... | collective-permute-start | bytes 1572872 | tf_op jit(solution)/shard_map/while/body/eval_jaxpr/ppermute | solution.py:18
  879.4 11.4 %collective-permute-start = (f32[8,128,128]{2,1,0:T(8,128)S(1)}, f32[8,128,128]{2,1,0:T(8,128)S(1)}, u32[]{:S(2)}, u32[]{:S(2)}) collective-permute-start(f32[8,128,128]{2,1,0:T(8,128)S(1)} %convolution_add_fusion.9), channel_id=1, source_target_pairs={{0,2},{2,4},{4,6},{6,8},{8,10},{10,12},{12,14},{14,16},{16,18},{18... | collective-permute-start | bytes 1572872 | tf_op jit(solution)/shard_map/while/body/eval_jaxpr/ppermute | solution.py:18
  891.4 11.4 %collective-permute-start = (f32[8,128,128]{2,1,0:T(8,128)S(1)}, f32[8,128,128]{2,1,0:T(8,128)S(1)}, u32[]{:S(2)}, u32[]{:S(2)}) collective-permute-start(f32[8,128,128]{2,1,0:T(8,128)S(1)} %convolution_add_fusion.9), channel_id=1, source_target_pairs={{0,2},{2,4},{4,6},{6,8},{8,10},{10,12},{12,14},{14,16},{16,18},{18... | collective-permute-start | bytes 1572872 | tf_op jit(solution)/shard_map/while/body/eval_jaxpr/ppermute | solution.py:18
  903.5 11.4 %collective-permute-start = (f32[8,128,128]{2,1,0:T(8,128)S(1)}, f32[8,128,128]{2,1,0:T(8,128)S(1)}, u32[]{:S(2)}, u32[]{:S(2)}) collective-permute-start(f32[8,128,128]{2,1,0:T(8,128)S(1)} %convolution_add_fusion.9), channel_id=1, source_target_pairs={{0,2},{2,4},{4,6},{6,8},{8,10},{10,12},{12,14},{14,16},{16,18},{18... | collective-permute-start | bytes 1572872 | tf_op jit(solution)/shard_map/while/body/eval_jaxpr/ppermute | solution.py:18
  915.6 11.4 %collective-permute-start = (f32[8,128,128]{2,1,0:T(8,128)S(1)}, f32[8,128,128]{2,1,0:T(8,128)S(1)}, u32[]{:S(2)}, u32[]{:S(2)}) collective-permute-start(f32[8,128,128]{2,1,0:T(8,128)S(1)} %convolution_add_fusion.9), channel_id=1, source_target_pairs={{0,2},{2,4},{4,6},{6,8},{8,10},{10,12},{12,14},{14,16},{16,18},{18... | collective-permute-start | bytes 1572872 | tf_op jit(solution)/shard_map/while/body/eval_jaxpr/ppermute | solution.py:18
  927.6 11.4 %collective-permute-start = (f32[8,128,128]{2,1,0:T(8,128)S(1)}, f32[8,128,128]{2,1,0:T(8,128)S(1)}, u32[]{:S(2)}, u32[]{:S(2)}) collective-permute-start(f32[8,128,128]{2,1,0:T(8,128)S(1)} %convolution_add_fusion.9), channel_id=1, source_target_pairs={{0,2},{2,4},{4,6},{6,8},{8,10},{10,12},{12,14},{14,16},{16,18},{18... | collective-permute-start | bytes 1572872 | tf_op jit(solution)/shard_map/while/body/eval_jaxpr/ppermute | solution.py:18
  939.7 11.4 %collective-permute-start = (f32[8,128,128]{2,1,0:T(8,128)S(1)}, f32[8,128,128]{2,1,0:T(8,128)S(1)}, u32[]{:S(2)}, u32[]{:S(2)}) collective-permute-start(f32[8,128,128]{2,1,0:T(8,128)S(1)} %convolution_add_fusion.9), channel_id=1, source_target_pairs={{0,2},{2,4},{4,6},{6,8},{8,10},{10,12},{12,14},{14,16},{16,18},{18... | collective-permute-start | bytes 1572872 | tf_op jit(solution)/shard_map/while/body/eval_jaxpr/ppermute | solution.py:18
  951.7 11.4 %collective-permute-start = (f32[8,128,128]{2,1,0:T(8,128)S(1)}, f32[8,128,128]{2,1,0:T(8,128)S(1)}, u32[]{:S(2)}, u32[]{:S(2)}) collective-permute-start(f32[8,128,128]{2,1,0:T(8,128)S(1)} %convolution_add_fusion.9), channel_id=1, source_target_pairs={{0,2},{2,4},{4,6},{6,8},{8,10},{10,12},{12,14},{14,16},{16,18},{18... | collective-permute-start | bytes 1572872 | tf_op jit(solution)/shard_map/while/body/eval_jaxpr/ppermute | solution.py:18
  963.8 11.4 %collective-permute-start = (f32[8,128,128]{2,1,0:T(8,128)S(1)}, f32[8,128,128]{2,1,0:T(8,128)S(1)}, u32[]{:S(2)}, u32[]{:S(2)}) collective-permute-start(f32[8,128,128]{2,1,0:T(8,128)S(1)} %convolution_add_fusion.9), channel_id=1, source_target_pairs={{0,2},{2,4},{4,6},{6,8},{8,10},{10,12},{12,14},{14,16},{16,18},{18... | collective-permute-start | bytes 1572872 | tf_op jit(solution)/shard_map/while/body/eval_jaxpr/ppermute | solution.py:18
  975.8 11.4 %collective-permute-start = (f32[8,128,128]{2,1,0:T(8,128)S(1)}, f32[8,128,128]{2,1,0:T(8,128)S(1)}, u32[]{:S(2)}, u32[]{:S(2)}) collective-permute-start(f32[8,128,128]{2,1,0:T(8,128)S(1)} %convolution_add_fusion.9), channel_id=1, source_target_pairs={{0,2},{2,4},{4,6},{6,8},{8,10},{10,12},{12,14},{14,16},{16,18},{18... | collective-permute-start | bytes 1572872 | tf_op jit(solution)/shard_map/while/body/eval_jaxpr/ppermute | solution.py:18
  987.9 11.4 %collective-permute-start = (f32[8,128,128]{2,1,0:T(8,128)S(1)}, f32[8,128,128]{2,1,0:T(8,128)S(1)}, u32[]{:S(2)}, u32[]{:S(2)}) collective-permute-start(f32[8,128,128]{2,1,0:T(8,128)S(1)} %convolution_add_fusion.9), channel_id=1, source_target_pairs={{0,2},{2,4},{4,6},{6,8},{8,10},{10,12},{12,14},{14,16},{16,18},{18... | collective-permute-start | bytes 1572872 | tf_op jit(solution)/shard_map/while/body/eval_jaxpr/ppermute | solution.py:18
  999.9 11.4 %collective-permute-start = (f32[8,128,128]{2,1,0:T(8,128)S(1)}, f32[8,128,128]{2,1,0:T(8,128)S(1)}, u32[]{:S(2)}, u32[]{:S(2)}) collective-permute-start(f32[8,128,128]{2,1,0:T(8,128)S(1)} %convolution_add_fusion.9), channel_id=1, source_target_pairs={{0,2},{2,4},{4,6},{6,8},{8,10},{10,12},{12,14},{14,16},{16,18},{18... | collective-permute-start | bytes 1572872 | tf_op jit(solution)/shard_map/while/body/eval_jaxpr/ppermute | solution.py:18
  1012.0 11.4 %collective-permute-start = (f32[8,128,128]{2,1,0:T(8,128)S(1)}, f32[8,128,128]{2,1,0:T(8,128)S(1)}, u32[]{:S(2)}, u32[]{:S(2)}) collective-permute-start(f32[8,128,128]{2,1,0:T(8,128)S(1)} %convolution_add_fusion.9), channel_id=1, source_target_pairs={{0,2},{2,4},{4,6},{6,8},{8,10},{10,12},{12,14},{14,16},{16,18},{18... | collective-permute-start | bytes 1572872 | tf_op jit(solution)/shard_map/while/body/eval_jaxpr/ppermute | solution.py:18
  1045.4 6.9 copy-start.5
  1052.3 8.4 copy-start.4
  1052.3 8.4 copy-start.6
  1060.7 7.8 copy-start.11
where the time goes:
time: 1110 us; the launch traced here: 1100 us
  other arithmetic  660 us (59%)
  waiting for transfers between devices  191 us (17%)
  matrix products  125 us (11%)
  local copies, waits for them, and re-layouts  66.2 us (6%)
  starting transfers between devices  36.5 us (3%)
  blocking collectives  21.4 us (2%)
    another operation x4, other arithmetic, prepare(): lax.linalg.triangular_solve(system, right_side, left_side=True, lower=Tru...  630 us
    ppermute x16, waiting for transfers between devices, shifted(): return lax.ppermute(block, axis, route)  146 us
    dot_general x39, matrix products, matmul_high(): return jnp.einsum('...ij,...jk->...ik', left, right, precision=PRECISE)  52.7 us
    all_to_all x1, waiting for transfers between devices, per_device(): lax.all_to_all(projected, 'head', split_axis=1, concat_axis=0, tiled=True)  44.9 us
    ppermute x16, starting transfers between devices, shifted(): return lax.ppermute(block, axis, route)  30.7 us
  transfers between devices with their start and end apart: 17, of which 17 were waited for; matrix products, arithmetic and copies ran while one was open for 0% of the time, Pallas kernels for 0%

commit v1 on v0

v1 whole, which is shorter than its diff:
```python
import functools

import jax
import jax.numpy as jnp
from jax import lax
from jax.experimental import pallas as pl
from jax.experimental.pallas import tpu as pltpu
from jax.sharding import Mesh
from jax.sharding import PartitionSpec as P

DK = 128
V_GROUP = 2
KW = 4
STRETCH = 128
HALO = 8
BASE = 16
GROUP_CHANNELS = (2 + V_GROUP) * DK
ALL = ("outer", "inner", "head")
NEAR = ("inner", "head")

f32 = jnp.float32
bf16 = jnp.bfloat16


def product(left, right):
    return jnp.dot(left, right, preferred_element_type=f32)


def local_kernel(
    number, x_ref, halo_ref, weight_ref, gate_ref, rate_ref, summary_ref, out_ref, reach_ref, ext
):
    length = number * STRETCH
    ext[0:HALO] = halo_ref[...].astype(f32)
    ext[HALO:] = x_ref[...].astype(f32)
    weight = weight_ref[...].astype(f32)

    def convolved(c, segment):
        cols = slice(segment * DK, (segment + 1) * DK)
        start = c * STRETCH + HALO - (KW - 1)
        total = ext[start : start + STRETCH, cols] * weight[0:1, cols]
        for j in range(1, KW):
            total = total + ext[start + j : start + j + STRETCH, cols] * weight[j : j + 1, cols]
        half = 0.5 * total
        return (half + half * jnp.tanh(half)).astype(bf16)

    row = lax.broadcasted_iota(jnp.int32, (STRETCH, STRETCH), 0)
    col = lax.broadcasted_iota(jnp.int32, (STRETCH, STRETCH), 1)
    inside = row >= col
    below = row > col
    eye = jnp.where(row == col, 1.0, 0.0).astype(f32)

    gates = gate_ref[0]
    rates = rate_ref[0]
    units = gates.shape[0]
    lane = lax.broadcasted_iota(jnp.int32, gates.shape, 1)
    cumulative = gates
    for k in (1, 2, 4, 8, 16, 32, 64):
        cumulative = cumulative + jnp.where(lane >= k, pltpu.roll(cumulative, k, 1), 0.0)
    last = cumulative[:, STRETCH - 1 : STRETCH]
    grown = jnp.exp(cumulative)
    tail = jnp.exp(last - cumulative)
    columns = jnp.transpose(
        jnp.concatenate([cumulative, grown, rates], axis=0), (1, 0)
    )

    def column(kind, unit):
        at = kind * units + unit
        return columns[:, at : at + 1]

    queries, keys, values, key_inverse = [], [], {}, []
    lower, scores = {}, {}
    for c in range(number):
        q = convolved(c, 0)
        k = convolved(c, 1)
        queries.append(q)
        keys.append(k)
        gram = lax.dot_general(
            jnp.concatenate([k, q], axis=0), k, (((1,), (1,)), ((), ())), preferred_element_type=f32
        )
        diagonal = gram[:STRETCH] * eye
        inverse_row = lax.rsqrt(jnp.sum(diagonal, axis=0, keepdims=True) + 1e-06)
        inverse_col = lax.rsqrt(jnp.sum(diagonal, axis=1, keepdims=True) + 1e-06)
        key_inverse.append(inverse_row)
        key_gram = gram[:STRETCH] * inverse_row
        query_gram = gram[STRETCH:] * inverse_row
        for j in range(V_GROUP):
            unit = j * number + c
            values[unit] = convolved(c, 2 + j)
            spread = column(0, unit) - cumulative[unit : unit + 1]
            decay = jnp.exp(jnp.where(inside, spread, -1e30))
            lower[unit] = jnp.where(
                below, key_gram * decay * (column(2, unit) * inverse_col), 0.0
            )
            scores[unit] = (query_gram * decay).astype(bf16)

    blocks = STRETCH // BASE
    small_lane = lax.broadcasted_iota(jnp.int32, (BASE, STRETCH), 1)
    small_row = lax.broadcasted_iota(jnp.int32, (BASE, STRETCH), 0)
    owner = small_lane // BASE
    packed = []
    for unit in range(units):
        piece = lower[unit][0:BASE]
        for b in range(1, blocks):
            piece = jnp.where(owner == b, lower[unit][b * BASE : (b + 1) * BASE], piece)
        packed.append(piece)
    packed = jnp.concatenate(packed, axis=0)
    big_lane = lax.broadcasted_iota(jnp.int32, packed.shape, 1)
    group_start = (big_lane // BASE) * BASE
    start = jnp.where(small_lane % BASE == small_row, 1.0, 0.0).astype(f32)
    solved = jnp.broadcast_to(start[None], (units, BASE, STRETCH))
    for j in range(BASE - 1):
        spread_col = jnp.take_along_axis(packed, group_start + j, axis=1)
        solved = solved - spread_col.reshape(units, BASE, STRETCH) * solved[:, j : j + 1, :]

    recip = {}
    for unit in range(units):
        pieces = [jnp.where(owner == b, solved[unit], 0.0) for b in range(blocks)]
        rows_of_inverse = pieces
        size = BASE
        while size < STRETCH:
            per = size // BASE
            whole = jnp.concatenate(rows_of_inverse, axis=0).astype(bf16)
            odd = [b for b in range(blocks) if (b // per) % 2 == 1]
            crossing = []
            for b in odd:
                sibling = (b // per) - 1
                crossing.append(
                    jnp.where(
                        small_lane // size == sibling, lower[unit][b * BASE : (b + 1) * BASE], 0.0
                    )
                )
            first = product(jnp.concatenate(crossing, axis=0).astype(bf16), whole).astype(bf16)
            zero = jnp.zeros((BASE, STRETCH), bf16)
            laid = [zero] * blocks
            for i, b in enumerate(odd):
                laid[b] = first[i * BASE : (i + 1) * BASE]
            odd_rows = jnp.concatenate([rows_of_inverse[b] for b in odd], axis=0)
            second = product(odd_rows.astype(bf16), jnp.concatenate(laid, axis=0))
            updated = odd_rows - second
            rows_of_inverse = list(rows_of_inverse)
            for i, b in enumerate(odd):
                rows_of_inverse[b] = updated[i * BASE : (i + 1) * BASE]
            size *= 2
        recip[unit] = jnp.concatenate(rows_of_inverse, axis=0)

    for j in range(V_GROUP):
        joint = None
        for c in range(number):
            unit = j * number + c
            at = slice(unit, unit + 1)
            by_rate = recip[unit] * rates[at]
            fresh = product(by_rate.astype(bf16), values[unit])
            carried = product((by_rate * (grown[at] * key_inverse[c])).astype(bf16), keys[c])
            scaled = (
                jnp.transpose(keys[c].astype(f32), (1, 0)) * (key_inverse[c] * tail[at])
            ).astype(bf16)
            if joint is None:
                written = jnp.concatenate([fresh, -carried], axis=1)
                seen = jnp.concatenate(
                    [jnp.zeros((STRETCH, DK), f32), queries[c].astype(f32)], axis=1
                )
                previous = jnp.concatenate([jnp.zeros((DK, DK), f32), eye], axis=1)
            else:
                both = product(
                    jnp.concatenate([carried.astype(bf16), queries[c]], axis=0), joint.astype(bf16)
                )
                written = (
                    jnp.concatenate([fresh, jnp.zeros((STRETCH, DK), f32)], axis=1)
                    - both[:STRETCH]
                )
                seen = both[STRETCH:]
                previous = joint
            gained = product(
                jnp.concatenate([scores[unit], scaled], axis=0), written.astype(bf16)
            )
            result = seen * column(1, unit) + gained[:STRETCH]
            rows = slice(c * STRETCH, (c + 1) * STRETCH)
            cols = slice(j * DK, (j + 1) * DK)
            out_ref[rows, cols] = result[:, :DK]
            reach_ref[rows, cols] = result[:, DK:].astype(bf16)
            joint = previous * grown[at, STRETCH - 1 : STRETCH] + gained[STRETCH:]
        summary_ref[j, :, :DK] = joint[:, :DK].astype(bf16)
        summary_ref[j, :, DK:] = (joint[:, DK:] - eye).astype(bf16)


def local_stage(projected, halo, weight, gates, rates):
    length, channels = projected.shape
    key_heads = channels // GROUP_CHANNELS
    number = length // STRETCH
    heads = key_heads * V_GROUP
    units = V_GROUP * number
    return pl.pallas_call(
        functools.partial(local_kernel, number),
        grid=(key_heads,),
        in_specs=[
            pl.BlockSpec((length, GROUP_CHANNELS), lambda g: (0, g)),
            pl.BlockSpec((HALO, GROUP_CHANNELS), lambda g: (0, g)),
            pl.BlockSpec((KW, GROUP_CHANNELS), lambda g: (0, g)),
            pl.BlockSpec((1, units, STRETCH), lambda g: (g, 0, 0)),
            pl.BlockSpec((1, units, STRETCH), lambda g: (g, 0, 0)),
        ],
        out_specs=[
            pl.BlockSpec((V_GROUP, DK, 2 * DK), lambda g: (g, 0, 0)),
            pl.BlockSpec((length, V_GROUP * DK), lambda g: (0, g)),
            pl.BlockSpec((length, V_GROUP * DK), lambda g: (0, g)),
        ],
        out_shape=[
            jax.ShapeDtypeStruct((heads, DK, 2 * DK), bf16),
            jax.ShapeDtypeStruct((length, heads * DK), f32),
            jax.ShapeDtypeStruct((length, heads * DK), bf16),
        ],
        scratch_shapes=[pltpu.VMEM((HALO + length, GROUP_CHANNELS), f32)],
        compiler_params=pltpu.CompilerParams(vmem_limit_bytes=48 << 20),
        name="local_stage",
    )(
        projected,
        halo,
        weight,
        gates.reshape(key_heads, units, STRETCH),
        rates.reshape(key_heads, units, STRETCH),
    )


def chain_kernel(summary_ref, prefix_ref, total_ref):
    devices, heads = summary_ref.shape[0], summary_ref.shape[1]
    row = lax.broadcasted_iota(jnp.int32, (DK, DK), 0)
    col = lax.broadcasted_iota(jnp.int32, (DK, DK), 1)
    eye = jnp.where(row == col, 1.0, 0.0).astype(f32)
    for h in range(heads):
        joint = jnp.concatenate([jnp.zeros((DK, DK), f32), eye], axis=1)
        for d in range(devices):
            prefix_ref[d, h] = joint
            loss = summary_ref[d, h, :, DK:]
            high = joint.astype(bf16)
            low = (joint - high.astype(f32)).astype(bf16)
            joint = joint + (product(loss, high) + product(loss, low))
            joint = joint + jnp.concatenate(
                [summary_ref[d, h, :, :DK].astype(f32), jnp.zeros((DK, DK), f32)], axis=1
            )
        total_ref[h] = joint


def chain_stage(summary):
    devices, heads = summary.shape[:2]
    return pl.pallas_call(
        chain_kernel,
        out_shape=[
            jax.ShapeDtypeStruct((devices, heads, DK, 2 * DK), f32),
            jax.ShapeDtypeStruct((heads, DK, 2 * DK), f32),
        ],
        compiler_params=pltpu.CompilerParams(vmem_limit_bytes=48 << 20),
        name="chain_stage",
    )(summary)


def entry_kernel(prefix_ref, entering_ref, start_ref):
    devices, heads = prefix_ref.shape[0], prefix_ref.shape[1]
    for h in range(heads):
        entering = entering_ref[h]
        high = entering.astype(bf16)
        low = (entering - high.astype(f32)).astype(bf16)
        pair = jnp.concatenate([high, low], axis=1)
        for d in range(devices):
            both = product(prefix_ref[d, h, :, DK:].astype(bf16), pair)
            start_ref[d, h] = (
                prefix_ref[d, h, :, :DK] + (both[:, :DK] + both[:, DK:])
            ).astype(bf16)


def entry_stage(prefix, entering):
    devices, heads = prefix.shape[:2]
    return pl.pallas_call(
        entry_kernel,
        out_shape=jax.ShapeDtypeStruct((devices, heads, DK, DK), bf16),
        compiler_params=pltpu.CompilerParams(vmem_limit_bytes=48 << 20),
        name="entry_stage",
    )(prefix, entering)


def finish_kernel(local_ref, reach_ref, start_ref, gain_ref, out_ref):
    for h in range(start_ref.shape[0]):
        cols = slice(h * DK, (h + 1) * DK)
        result = local_ref[:, cols] + product(reach_ref[:, cols], start_ref[h])
        mean = jnp.mean(result * result, axis=1, keepdims=True)
        out_ref[:, cols] = (result * lax.rsqrt(mean + 1e-06) * gain_ref[...]).astype(bf16)


def finish_stage(local, reach, starts, gain):
    length, width = local.shape
    heads = starts.shape[0]
    step = 4
    return pl.pallas_call(
        finish_kernel,
        grid=(heads // step,),
        in_specs=[
            pl.BlockSpec((length, step * DK), lambda g: (0, g)),
            pl.BlockSpec((length, step * DK), lambda g: (0, g)),
            pl.BlockSpec((step, DK, DK), lambda g: (g, 0, 0)),
            pl.BlockSpec((1, DK), lambda g: (0, 0)),
        ],
        out_specs=pl.BlockSpec((length, step * DK), lambda g: (0, g)),
        out_shape=jax.ShapeDtypeStruct((length, width), bf16),
        compiler_params=pltpu.CompilerParams(vmem_limit_bytes=48 << 20),
        name="finish_stage",
    )(local, reach, starts, gain.reshape(1, DK))


def entering_state(total):
    outer = lax.axis_size("outer")
    if outer == 1:
        return jnp.zeros_like(total[..., :DK])
    if outer == 2:
        return lax.ppermute(total[..., :DK], "outer", [(0, 1)])
    everyone = lax.all_gather(total, "outer", axis=0)
    mine = lax.axis_index("outer")

    def step(i, state):
        piece = lax.dynamic_index_in_dim(everyone, i, 0, keepdims=False)
        moved = piece[..., :DK] + jnp.einsum(
            "hij,hjk->hik", piece[..., DK:], state, precision=lax.Precision.HIGHEST
        )
        return jnp.where(i < mine, moved, state)

    return lax.fori_loop(0, outer - 1, step, jnp.zeros_like(total[..., :DK]))


def per_device(projected, conv_weight, log_gate, write_rate, norm_gain):
    length = projected.shape[0]
    devices = lax.axis_size(ALL)
    parts = lax.axis_size("head")
    local_heads = log_gate.shape[0]
    width = conv_weight.shape[1]
    halo = lax.ppermute(
        projected[length - HALO :], ALL, [(i, i + 1) for i in range(devices - 1)]
    )
    both = jnp.stack([log_gate, write_rate]).reshape(2, local_heads, parts, length)
    both = jnp.moveaxis(both, 2, 0).reshape(parts, 2 * local_heads * length // DK, DK)
    taps = conv_weight.astype(f32).reshape(1, KW * width // DK, DK)
    packed = jnp.concatenate(
        [both, jnp.broadcast_to(taps, (parts,) + taps.shape[1:])], axis=1
    )
    packed = lax.all_to_all(packed, "head", 0, 0, tiled=True)
    split = both.shape[1]
    both = jnp.moveaxis(packed[:, :split].reshape(parts, 2, local_heads, length), 1, 0)
    both = both.reshape(2, parts * local_heads, length)
    weight = jnp.moveaxis(packed[:, split:].reshape(parts, KW, width), 0, 1)
    weight = weight.reshape(KW, parts * width)

    summary, local, reach = local_stage(projected, halo, weight, both[0], both[1])
    heads = summary.shape[0]
    near = lax.axis_size(NEAR)
    own = heads // near
    summary = lax.all_to_all(summary, NEAR, 0, 0, tiled=True)
    prefix, total = chain_stage(summary.reshape(near, own, DK, 2 * DK))
    starts = entry_stage(prefix, entering_state(total))
    starts = lax.all_to_all(starts.reshape(heads, DK, DK), NEAR, 0, 0, tiled=True)
    return finish_stage(local, reach, starts, norm_gain)


def solution(mesh):
    seq, head = mesh.shape["seq"], mesh.shape["head"]
    inner = max(1, 16 // head)
    while seq % inner:
        inner //= 2
    near = Mesh(mesh.devices.reshape(seq // inner, inner, head), ALL)
    in_specs = (
        P(ALL, None),
        P(None, "head"),
        P("head", ("outer", "inner")),
        P("head", ("outer", "inner")),
        P(),
    )
    return jax.shard_map(
        per_device, mesh=near, in_specs=in_specs, out_specs=P(ALL, None), check_vma=False
    )
```

time: 1110 us -> 129 us (0.12)
  other arithmetic: 660 us -> 1.45 us
  waiting for transfers between devices: 191 us -> 9.31 us
  matrix products: 125 us -> 0 us
  Pallas kernels: 0 us -> 74.6 us
  local copies, waits for them, and re-layouts: 66.2 us -> 1.66 us
  starting transfers between devices: 36.5 us -> 8.57 us
    another operation x5 -> x0, other arithmetic: 633 us -> none  [the longest x4 630 us: prepare(): lax.linalg.triangular_solve(system, right_side, left_side=True, lower=Tru...]
    ppermute x16 -> x2, waiting for transfers between devices: 146 us -> 9.31 us  [the longest x1 5.86 us: entering_state(): return lax.ppermute(total[..., :DK], 'outer', [(0, 1)])]
    dot_general x46 -> x0, matrix products: 114 us -> none  [the longest x39 52.7 us: matmul_high(): return jnp.einsum('...ij,...jk->...ik', left, right, precision=PRECISE)]
    pallas_call x0 -> x4, Pallas kernels: none -> 74.6 us  [the longest x1 66 us: local_stage(): pl.pallas_call(functools.partial(local_kernel, number), grid=(key_heads,)...]
    all_to_all x1, waiting for transfers between devices: 44.9 us -> 0.01 us  [per_device(): packed = lax.all_to_all(packed, 'head', 0, 0, tiled=True)]
    ppermute x16 -> x2, starting transfers between devices: 30.7 us -> 5.19 us  [the longest x1 3.9 us: per_device(): lax.ppermute(projected[length - HALO:], ALL, [(i, i + 1) for i in range(d...]
    reshape x4 -> x3, local copies, waits for them, and re-layouts: 16 us -> 0.04 us  [the longest x1 0.02 us: per_device(): weight = jnp.moveaxis(packed[:, split:].reshape(parts, KW, width), 0, 1)]
    reshape x1 -> x0, other arithmetic: 15.1 us -> none  [head_rows(): convolved.astype(jnp.float32).reshape(count_rows, -1, 2 + V_GROUP, DK)]
  transfers between devices with their start and end apart: 17 -> 3, of which waited for: 17 -> 2; matrix products, arithmetic and copies ran while one was open for 0% -> 1% of each run, Pallas kernels for 0% -> 0%
where the time goes in v1:
time: 129 us; the launch traced here: 128 us
  Pallas kernels  74.6 us (58%)
  blocking collectives  31.9 us (25%)
  waiting for transfers between devices  9.31 us (7%)
  starting transfers between devices  8.57 us (7%)
  local copies, waits for them, and re-layouts  1.66 us (1%)
  other arithmetic  1.45 us (1%)
    pallas_call x1, Pallas kernels, local_stage(): pl.pallas_call(functools.partial(local_kernel, number), grid=(key_heads,)...  66 us
    all_to_all x1, blocking collectives, per_device(): summary = lax.all_to_all(summary, NEAR, 0, 0, tiled=True)  18.6 us
    all_to_all x1, blocking collectives, per_device(): lax.all_to_all(starts.reshape(heads, DK, DK), NEAR, 0, 0, tiled=True)  13.3 us
    ppermute x1, waiting for transfers between devices, entering_state(): return lax.ppermute(total[..., :DK], 'outer', [(0, 1)])  5.86 us
    pallas_call x1, Pallas kernels, finish_stage(): pl.pallas_call(finish_kernel, grid=(heads // step,), in_specs=[pl.BlockSp...  5.14 us
    ppermute x1, starting transfers between devices, per_device(): lax.ppermute(projected[length - HALO:], ALL, [(i, i + 1) for i in range(d...  3.9 us
    ppermute x1, waiting for transfers between devices, per_device(): lax.ppermute(projected[length - HALO:], ALL, [(i, i + 1) for i in range(d...  3.45 us
    all_to_all x1, starting transfers between devices, per_device(): packed = lax.all_to_all(packed, 'head', 0, 0, tiled=True)  3.38 us
  transfers between devices with their start and end apart: 3, of which 2 were waited for; matrix products, arithmetic and copies ran while one was open for 1% of the time, Pallas kernels for 0%

profile of v1, /device:TPU:16, one launch (start us, length us, event | category | flops | bytes accessed | tf_op | source)
XLA Modules:
  0.0 127.6 jit_solution(10169616612569333260)
XLA Ops:
  0.0 0.7 reshape.40
  0.7 0.8 maximum_bitcast_fusion
  1.5 0.7 pad_maximum_fusion
  2.2 3.4 %all-to-all-start = ((f32[2,128,128]{2,1,0:T(8,128)}), f32[2,128,128]{2,1,0:T(8,128)S(1)}, u32[]{:S(2)}, u32[]{:S(2)}) async-start(f32[2,128,128]{2,1,0:T(8,128)} %pad_maximum_fusion), calls=%async_computation | async-start | bytes 262144 | tf_op jit(solution)/shard_map/all_to_all | solution.py:342
  5.6 0.8 slice.20
  6.4 3.9 %collective-permute-start = (bf16[8,4096]{1,0:T(8,128)(2,1)S(1)}, bf16[8,4096]{1,0:T(8,128)(2,1)S(1)}, u32[]{:S(2)}, u32[]{:S(2)}) collective-permute-start(bf16[8,4096]{1,0:T(8,128)(2,1)S(1)} %slice.20), channel_id=1, source_target_pairs={{0,1},{1,2},{2,3},{3,4},{4,5},{5,6},{6,7},{7,8},{8,9},{9,10},{10,1... | collective-permute-start | bytes 196616 | tf_op jit(solution)/shard_map/ppermute | solution.py:333
  10.3 0.0 all-to-all-done
  10.5 3.4 %collective-permute-done.halo_ref = bf16[8,4096]{1,0:T(8,128)(2,1)S(1)} collective-permute-done((bf16[8,4096]{1,0:T(8,128)(2,1)S(1)}, bf16[8,4096]{1,0:T(8,128)(2,1)S(1)}, u32[]{:S(2)}, u32[]{:S(2)}) %collective-permute-start) | collective-permute-done | bytes 65568 | tf_op jit(solution)/shard_map/ppermute | solution.py:333
  13.9 66.0 %local_stage.1 = (bf16[16,128,256]{2,1,0:T(8,128)(2,1)S(1)}, f32[512,2048]{1,0:T(8,128)}, bf16[512,2048]{1,0:T(8,128)(2,1)S(1)}) custom-call(bf16[512,4096]{1,0:T(8,128)(2,1)} %x_ref.1, bf16[8,4096]{1,0:T(8,128)(2,1)S(1)} %collective-permute-done.halo_ref, f32[4,4096]{1,0:T(4,128)S(1)} %bitcast.27, f32[8,8,128]{2,1,0:T(8,128)S(1)} %reshape_squeeze.6.gate_ref, ...), custom_call_target="tpu_custom_call" | custom-call | tf_op jit(solution)/shard_map/local_stage/pallas_call | solution.py:192
  79.9 18.6 %all_to_all.15 = bf16[16,128,256]{2,1,0:T(8,128)(2,1)S(1)} all-to-all(bf16[16,128,256]{2,1,0:T(8,128)(2,1)S(1)} %get-tuple-element.12), channel_id=1, replica_groups=mesh['outer'=2,'inner'=8,'head'=2] {'inner','head'}, dimensions={0} | all-to-all | bytes 2097152 | tf_op jit(solution)/shard_map/all_to_all | solution.py:353
  98.6 3.0 %chain_stage.1 = (f32[16,1,128,256]{3,2,1,0:T(8,128)S(1)}, f32[1,128,256]{2,1,0:T(8,128)S(1)}) custom-call(bf16[16,1,128,256]{3,2,1,0:T(8,128)(2,1)S(1)} %bitcast.25), custom_call_target="tpu_custom_call" | custom-call | tf_op jit(solution)/shard_map/chain_stage/pallas_call | solution.py:245
  101.6 0.0 copy-start
  101.6 1.3 %collective-permute-start.1 = (f32[1,128,128]{2,1,0:T(8,128)S(1)}, f32[1,128,128]{2,1,0:T(8,128)S(1)}, u32[]{:S(2)}, u32[]{:S(2)}) collective-permute-start(f32[1,128,128]{2,1,0:T(8,128)S(1)} %slice.25), channel_id=1, source_target_pairs={{0,16},{1,17},{2,18},{3,19},{4,20},{5,21},{6,22},{7,23},{8,24},{9,... | collective-permute-start | bytes 196616 | tf_op jit(solution)/shard_map/ppermute | solution.py:313
  102.9 5.9 %collective-permute-done.1.entering_ref = f32[1,128,128]{2,1,0:T(8,128)S(1)} collective-permute-done((f32[1,128,128]{2,1,0:T(8,128)S(1)}, f32[1,128,128]{2,1,0:T(8,128)S(1)}, u32[]{:S(2)}, u32[]{:S(2)}) %collective-permute-start.1) | collective-permute-done | bytes 65568 | tf_op jit(solution)/shard_map/ppermute | solution.py:313
  108.8 0.4 entry_stage.1
  109.2 13.3 %all_to_all.16.start_ref = bf16[16,128,128]{2,1,0:T(8,128)(2,1)S(1)} all-to-all(bf16[16,128,128]{2,1,0:T(8,128)(2,1)S(1)} %bitcast.26), channel_id=1, replica_groups=mesh['outer'=2,'inner'=8,'head'=2] {'inner','head'}, dimensions={0} | all-to-all | bytes 1048576 | tf_op jit(solution)/shard_map/all_to_all | solution.py:356
  122.5 0.0 copy-done
  122.5 5.1 %finish_stage.1 = bf16[512,2048]{1,0:T(8,128)(2,1)} custom-call(f32[512,2048]{1,0:T(8,128)} %get-tuple-element.10.local_ref, bf16[512,2048]{1,0:T(8,128)(2,1)S(1)} %get-tuple-element.11.reach_ref, bf16[16,128,128]{2,1,0:T(8,128)(2,1)S(1)} %all_to_all.16.start_ref, f32[1,128]{1,0:T(1,128)S(1)} %bitcast.28), custom_call_target="tpu_custom_call" | custom-call | tf_op jit(solution)/shard_map/finish_stage/pallas_call | solution.py:292
  (9 shorter events, 0.1 us)
Async XLA Ops:
  2.2 8.1 %all-to-all-start = ((f32[2,128,128]{2,1,0:T(8,128)}), f32[2,128,128]{2,1,0:T(8,128)S(1)}, u32[]{:S(2)}, u32[]{:S(2)}) async-start(f32[2,128,128]{2,1,0:T(8,128)} %pad_maximum_fusion), calls=%async_computation | async-start | bytes 262144 | tf_op jit(solution)/shard_map/all_to_all | solution.py:342
  6.4 7.5 %collective-permute-start = (bf16[8,4096]{1,0:T(8,128)(2,1)S(1)}, bf16[8,4096]{1,0:T(8,128)(2,1)S(1)}, u32[]{:S(2)}, u32[]{:S(2)}) collective-permute-start(bf16[8,4096]{1,0:T(8,128)(2,1)S(1)} %slice.20), channel_id=1, source_target_pairs={{0,1},{1,2},{2,3},{3,4},{4,5},{5,6},{6,7},{7,8},{8,9},{9,10},{10,1... | collective-permute-start | bytes 196616 | tf_op jit(solution)/shard_map/ppermute | solution.py:333
  101.6 20.9 %copy-start = (f32[128]{0:T(128)S(1)}, f32[128]{0:T(128)}, u32[]{:S(2)}) copy-start(f32[128]{0:T(128)} %param.9) | copy-start | bytes 1540
  101.6 7.2 %collective-permute-start.1 = (f32[1,128,128]{2,1,0:T(8,128)S(1)}, f32[1,128,128]{2,1,0:T(8,128)S(1)}, u32[]{:S(2)}, u32[]{:S(2)}) collective-permute-start(f32[1,128,128]{2,1,0:T(8,128)S(1)} %slice.25), channel_id=1, source_target_pairs={{0,16},{1,17},{2,18},{3,19},{4,20},{5,21},{6,22},{7,23},{8,24},{9,... | collective-permute-start | bytes 196616 | tf_op jit(solution)/shard_map/ppermute | solution.py:313

commit v2 on v1

v2 whole, which is shorter than its diff:
```python
import functools

import jax
import jax.numpy as jnp
from jax import lax
from jax.experimental import pallas as pl
from jax.experimental.pallas import tpu as pltpu
from jax.sharding import Mesh
from jax.sharding import PartitionSpec as P

DK = 128
V_GROUP = 2
KW = 4
STRETCH = 128
HALO = 8
BASE = 16
SEGMENTS = 2 + V_GROUP
VMEM_BYTES = 56 << 20
GROUP_CHANNELS = (2 + V_GROUP) * DK
ALL = ("outer", "inner", "head")
NEAR = ("inner", "head")

f32 = jnp.float32
bf16 = jnp.bfloat16


def product(left, right):
    return jnp.dot(left, right, preferred_element_type=f32)


def extend(ext, halo_ref, x_ref, cols):
    ext[0:HALO, cols] = halo_ref[:, cols].astype(f32)
    ext[HALO:, cols] = x_ref[:, cols].astype(f32)


def convolved(ext, cols, taps, c):
    start = c * STRETCH + HALO - (KW - 1)
    total = ext[start : start + STRETCH, cols] * taps[0:1]
    for j in range(1, KW):
        total = total + ext[start + j : start + j + STRETCH, cols] * taps[j : j + 1]
    half = 0.5 * total
    return (half + half * jnp.tanh(half)).astype(bf16)


def running_sum(gates):
    lane = lax.broadcasted_iota(jnp.int32, gates.shape, 1)
    total = gates
    for k in (1, 2, 4, 8, 16, 32, 64):
        total = total + jnp.where(lane >= k, pltpu.roll(total, k, 1), 0.0)
    return total


def square_iotas():
    row = lax.broadcasted_iota(jnp.int32, (STRETCH, STRETCH), 0)
    col = lax.broadcasted_iota(jnp.int32, (STRETCH, STRETCH), 1)
    return row, col


def block_inverses(lower):
    units = len(lower)
    blocks = STRETCH // BASE
    small_lane = lax.broadcasted_iota(jnp.int32, (BASE, STRETCH), 1)
    small_row = lax.broadcasted_iota(jnp.int32, (BASE, STRETCH), 0)
    owner = small_lane // BASE
    packed = []
    for unit in range(units):
        piece = lower[unit][0:BASE]
        for b in range(1, blocks):
            piece = jnp.where(owner == b, lower[unit][b * BASE : (b + 1) * BASE], piece)
        packed.append(piece)
    packed = jnp.concatenate(packed, axis=0)
    group_start = (lax.broadcasted_iota(jnp.int32, packed.shape, 1) // BASE) * BASE
    start = jnp.where(small_lane % BASE == small_row, 1.0, 0.0).astype(f32)
    solved = jnp.broadcast_to(start[None], (units, BASE, STRETCH))
    for j in range(BASE - 1):
        spread_col = jnp.take_along_axis(packed, group_start + j, axis=1)
        solved = solved - spread_col.reshape(units, BASE, STRETCH) * solved[:, j : j + 1, :]

    rows = [
        [jnp.where(owner == b, solved[unit], 0.0) for b in range(blocks)] for unit in range(units)
    ]
    size = BASE
    while size < STRETCH:
        per = size // BASE
        odd = [b for b in range(blocks) if (b // per) % 2 == 1]
        firsts = []
        for unit in range(units):
            crossing = [
                jnp.where(
                    small_lane // size == (b // per) - 1,
                    lower[unit][b * BASE : (b + 1) * BASE],
                    0.0,
                )
                for b in odd
            ]
            firsts.append(
                product(
                    jnp.concatenate(crossing, axis=0).astype(bf16),
                    jnp.concatenate(rows[unit], axis=0).astype(bf16),
                ).astype(bf16)
            )
        for unit in range(units):
            laid = [jnp.zeros((BASE, STRETCH), bf16)] * blocks
            for i, b in enumerate(odd):
                laid[b] = firsts[unit][i * BASE : (i + 1) * BASE]
            odd_rows = jnp.concatenate([rows[unit][b] for b in odd], axis=0)
            updated = odd_rows - product(odd_rows.astype(bf16), jnp.concatenate(laid, axis=0))
            for i, b in enumerate(odd):
                rows[unit][b] = updated[i * BASE : (i + 1) * BASE]
        size *= 2
    return [jnp.concatenate(rows[unit], axis=0) for unit in range(units)]


def pack_kernel(parts, at_ref, x_ref, gate_ref, rate_ref, taps_ref, packed_ref, halo_ref):
    heads = gate_ref.shape[0]
    length = gate_ref.shape[1] // parts
    number = length // STRETCH
    segments = taps_ref.shape[1] // DK
    halo_ref[...] = x_ref[...]
    for i in range(packed_ref.shape[0]):
        part = at_ref[i]
        for c in range(number):
            lanes = pl.ds(pl.multiple_of(part * length + c * STRETCH, STRETCH), STRETCH)
            rows = slice(c * heads, (c + 1) * heads)
            packed_ref[i, rows] = gate_ref[:, lanes]
            rows = slice((number + c) * heads, (number + c + 1) * heads)
            packed_ref[i, rows] = rate_ref[:, lanes]
        base = 2 * number * heads
        for segment in range(segments):
            rows = slice(base + segment * KW, base + (segment + 1) * KW)
            packed_ref[i, rows] = taps_ref[:, segment * DK : (segment + 1) * DK].astype(f32)


def pack_stage(order, parts, projected, log_gate, write_rate, conv_weight):
    length, channels = projected.shape
    heads = log_gate.shape[0]
    rows = 2 * (length // STRETCH) * heads + conv_weight.shape[1] // DK * KW
    count = order.shape[0]
    whole = lambda shape: pl.BlockSpec(shape, lambda i, at: (0,) * len(shape))
    return pl.pallas_call(
        functools.partial(pack_kernel, parts),
        grid_spec=pltpu.PrefetchScalarGridSpec(
            num_scalar_prefetch=1,
            grid=(1,),
            in_specs=[
                pl.BlockSpec((HALO, channels), lambda i, at: (length // HALO - 1, 0)),
                whole(log_gate.shape),
                whole(write_rate.shape),
                whole(conv_weight.shape),
            ],
            out_specs=[whole((count, rows, DK)), whole((HALO, channels))],
        ),
        out_shape=[
            jax.ShapeDtypeStruct((count, rows, DK), f32),
            jax.ShapeDtypeStruct((HALO, channels), bf16),
        ],
        name="pack_stage",
    )(order, projected, log_gate, write_rate, conv_weight)


def local_kernel(number, into, part_ref, x_ref, halo_ref, pack_ref, *refs):
    summary_ref, written_ref, joint_ref, key_ref, norm_ref, ext = refs[into:]
    key_heads = key_ref.shape[1] // DK
    heads = key_heads * V_GROUP
    units = heads * number
    row, col = square_iotas()
    below = row > col
    eye = jnp.where(row == col, 1.0, 0.0).astype(f32)

    rates = pack_ref[0, units : 2 * units]
    cumulative = running_sum(pack_ref[0, 0:units])
    grown = jnp.exp(cumulative)
    tail = jnp.exp(cumulative[:, STRETCH - 1 : STRETCH] - cumulative)
    columns = jnp.transpose(jnp.concatenate([cumulative, rates], axis=0), (1, 0))
    where = [(c, g) for g in range(key_heads) for c in range(number)]

    def units_of(c, g):
        return [(j, c * heads + g * V_GROUP + j) for j in range(V_GROUP)]

    def channels(c, g, kind):
        segment = g * SEGMENTS + kind
        cols = slice(segment * DK, (segment + 1) * DK)
        if c == 0:
            extend(ext, halo_ref, x_ref, cols)
        at = 2 * units + segment * KW
        return convolved(ext, cols, pack_ref[0, at : at + KW], c)

    keys, inverses, lower = {}, {}, [None] * units
    for c, g in where:
        k = channels(c, g, 1)
        keys[c, g] = k
        key_ref[c * STRETCH : (c + 1) * STRETCH, g * DK : (g + 1) * DK] = k
        gram = lax.dot_general(k, k, (((1,), (1,)), ((), ())), preferred_element_type=f32)
        diagonal = gram * eye
        inverse_row = lax.rsqrt(jnp.sum(diagonal, axis=0, keepdims=True) + 1e-06)
        inverse_col = lax.rsqrt(jnp.sum(diagonal, axis=1, keepdims=True) + 1e-06)
        inverses[c, g] = inverse_row
        norm_ref[g, c : c + 1] = inverse_row
        gram = gram * inverse_row
        for j, unit in units_of(c, g):
            spread = columns[:, unit : unit + 1] - cumulative[unit : unit + 1]
            decay = jnp.exp(jnp.where(below, spread, -1e30))
            lower[unit] = gram * decay * (columns[:, units + unit : units + unit + 1] * inverse_col)

    solved = block_inverses(lower)

    fresh, carried, scaled = [None] * units, [None] * units, [None] * units
    for c, g in where:
        turned = jnp.transpose(keys[c, g].astype(f32), (1, 0)) * inverses[c, g]
        for j, unit in units_of(c, g):
            at = slice(unit, unit + 1)
            by_rate = solved[unit] * rates[at]
            fresh[unit] = product(by_rate.astype(bf16), channels(c, g, 2 + j))
            by_rate = by_rate * (grown[at] * inverses[c, g])
            carried[unit] = product(by_rate.astype(bf16), keys[c, g])
            scaled[unit] = (turned * tail[at]).astype(bf16)

    nothing = jnp.zeros((STRETCH, DK), f32)
    joint = [jnp.concatenate([jnp.zeros((DK, DK), f32), eye], axis=1)] * heads
    for c in range(number):
        for head in range(heads):
            unit = c * heads + head
            if c == 0:
                written = jnp.concatenate([fresh[unit], -carried[unit]], axis=1)
            else:
                start = joint[head].astype(bf16)
                joint_ref[c, head] = start
                written = jnp.concatenate([fresh[unit], nothing], axis=1) - product(
                    carried[unit].astype(bf16), start
                )
            written = written.astype(bf16)
            written_ref[c, head] = written
            decay = grown[unit : unit + 1, STRETCH - 1 : STRETCH]
            joint[head] = joint[head] * decay + product(scaled[unit], written)
    for head in range(heads):
        summary_ref[head, :, :DK] = joint[head][:, :DK].astype(bf16)
        summary_ref[head, :, DK:] = (joint[head][:, DK:] - eye).astype(bf16)


def pack_row(pack, index):
    return pl.BlockSpec((1,) + pack.shape[1:], lambda i, part: (index, 0, 0))


def local_stage(part, parts, projected, halo, packs, index, into=()):
    length, channels = projected.shape
    number = length // STRETCH
    width = channels // parts
    all_key_heads = channels // GROUP_CHANNELS
    all_heads = all_key_heads * V_GROUP
    key_heads = all_key_heads // parts
    heads = all_heads // parts
    per_unit = pl.BlockSpec((number, heads, STRETCH, 2 * DK), lambda i, part: (0, part[0], 0, 0))
    inputs = (part, projected, halo, packs)
    return pl.pallas_call(
        functools.partial(local_kernel, number, len(into)),
        grid_spec=pltpu.PrefetchScalarGridSpec(
            num_scalar_prefetch=1,
            grid=(1,),
            in_specs=[
                pl.BlockSpec((length, width), lambda i, part: (0, part[0])),
                pl.BlockSpec((HALO, width), lambda i, part: (0, part[0])),
                pack_row(packs, index),
            ]
            + [pl.BlockSpec(memory_space=pl.ANY)] * len(into),
            out_specs=[
                pl.BlockSpec((heads, DK, 2 * DK), lambda i, part: (part[0], 0, 0)),
                per_unit,
                per_unit,
                pl.BlockSpec((length, key_heads * DK), lambda i, part: (0, part[0])),
                pl.BlockSpec((key_heads, number, STRETCH), lambda i, part: (part[0], 0, 0)),
            ],
            scratch_shapes=[pltpu.VMEM((HALO + length, width), f32)],
        ),
        out_shape=[
            jax.ShapeDtypeStruct((all_heads, DK, 2 * DK), bf16),
            jax.ShapeDtypeStruct((number, all_heads, STRETCH, 2 * DK), bf16),
            jax.ShapeDtypeStruct((number, all_heads, STRETCH, 2 * DK), bf16),
            jax.ShapeDtypeStruct((length, all_key_heads * DK), bf16),
            jax.ShapeDtypeStruct((all_key_heads, number, STRETCH), f32),
        ],
        input_output_aliases={len(inputs) + i: i for i in range(len(into))},
        compiler_params=pltpu.CompilerParams(vmem_limit_bytes=VMEM_BYTES),
        name="local_stage",
    )(*inputs, *into)


def reading_kernel(number, part_ref, *refs):
    key_heads = refs[-3].shape[1] // (V_GROUP * DK)
    x_refs, halo_refs = refs[:key_heads], refs[key_heads : 2 * key_heads]
    pack_ref, key_ref, norm_ref, written_ref, joint_ref = refs[2 * key_heads : 2 * key_heads + 5]
    out_ref, reach_ref, ext = refs[-3:]
    heads = key_heads * V_GROUP
    units = heads * number
    row, col = square_iotas()
    inside = row >= col
    cumulative = running_sum(pack_ref[0, 0:units])
    columns = jnp.transpose(cumulative, (1, 0))
    whole = slice(0, DK)
    for g in range(key_heads):
        extend(ext.at[g], halo_refs[g], x_refs[g], whole)
        at = 2 * units + g * SEGMENTS * KW
        for c in range(number):
            rows = slice(c * STRETCH, (c + 1) * STRETCH)
            query = convolved(ext.at[g], whole, pack_ref[0, at : at + KW], c)
            gram = lax.dot_general(
                query,
                key_ref[rows, g * DK : (g + 1) * DK],
                (((1,), (1,)), ((), ())),
                preferred_element_type=f32,
            )
            gram = gram * norm_ref[g, c : c + 1]
            for j in range(V_GROUP):
                head = g * V_GROUP + j
                unit = c * heads + head
                sum_here = columns[:, unit : unit + 1]
                decay = jnp.exp(jnp.where(inside, sum_here - cumulative[unit : unit + 1], -1e30))
                result = product((gram * decay).astype(bf16), written_ref[c, head])
                grown = jnp.exp(sum_here)
                cols = slice(head * DK, (head + 1) * DK)
                if c == 0:
                    reached = result[:, DK:] + grown * query.astype(f32)
                else:
                    result = result + grown * product(query, joint_ref[c, head])
                    reached = result[:, DK:]
                out_ref[rows, cols] = result[:, :DK]
                reach_ref[rows, cols] = reached.astype(bf16)


def reading_stage(part, parts, projected, halo, packs, index, kept, into=()):
    written, joints, keys, norms = kept
    length, channels = projected.shape
    number = length // STRETCH
    all_key_heads = channels // GROUP_CHANNELS
    key_heads = all_key_heads // parts
    heads = key_heads * V_GROUP
    per_unit = pl.BlockSpec((number, heads, STRETCH, 2 * DK), lambda i, part: (0, part[0], 0, 0))
    per_head = pl.BlockSpec((length, heads * DK), lambda i, part: (0, part[0]))
    query = lambda g: lambda i, part: (0, (part[0] * key_heads + g) * SEGMENTS)
    inputs = (part,) + (projected,) * key_heads + (halo,) * key_heads
    inputs += (packs, keys, norms, written, joints)
    width = all_key_heads * V_GROUP * DK
    return pl.pallas_call(
        functools.partial(reading_kernel, number),
        grid_spec=pltpu.PrefetchScalarGridSpec(
            num_scalar_prefetch=1,
            grid=(1,),
            in_specs=[pl.BlockSpec((length, DK), query(g)) for g in range(key_heads)]
            + [pl.BlockSpec((HALO, DK), query(g)) for g in range(key_heads)]
            + [
                pack_row(packs, index),
                pl.BlockSpec((length, key_heads * DK), lambda i, part: (0, part[0])),
                pl.BlockSpec((key_heads, number, STRETCH), lambda i, part: (part[0], 0, 0)),
                per_unit,
                per_unit,
            ]
            + [pl.BlockSpec(memory_space=pl.ANY)] * len(into),
            out_specs=[per_head, per_head],
            scratch_shapes=[pltpu.VMEM((key_heads, HALO + length, DK), f32)],
        ),
        out_shape=[
            jax.ShapeDtypeStruct((length, width), f32),
            jax.ShapeDtypeStruct((length, width), bf16),
        ],
        input_output_aliases={len(inputs) + i: i for i in range(len(into))},
        compiler_params=pltpu.CompilerParams(vmem_limit_bytes=VMEM_BYTES),
        name="reading_stage",
    )(*inputs, *into)


def chain_kernel(summary_ref, prefix_ref, total_ref):
    devices, heads = summary_ref.shape[0], summary_ref.shape[1]
    row = lax.broadcasted_iota(jnp.int32, (DK, DK), 0)
    col = lax.broadcasted_iota(jnp.int32, (DK, DK), 1)
    eye = jnp.where(row == col, 1.0, 0.0).astype(f32)
    for h in range(heads):
        joint = jnp.concatenate([jnp.zeros((DK, DK), f32), eye], axis=1)
        for d in range(devices):
            prefix_ref[d, h] = joint
            loss = summary_ref[d, h, :, DK:]
            high = joint.astype(bf16)
            low = (joint - high.astype(f32)).astype(bf16)
            joint = joint + (product(loss, high) + product(loss, low))
            joint = joint + jnp.concatenate(
                [summary_ref[d, h, :, :DK].astype(f32), jnp.zeros((DK, DK), f32)], axis=1
            )
        total_ref[h] = joint


def chain_stage(summary):
    devices, heads = summary.shape[:2]
    return pl.pallas_call(
        chain_kernel,
        out_shape=[
            jax.ShapeDtypeStruct((devices, heads, DK, 2 * DK), f32),
            jax.ShapeDtypeStruct((heads, DK, 2 * DK), f32),
        ],
        compiler_params=pltpu.CompilerParams(vmem_limit_bytes=48 << 20),
        name="chain_stage",
    )(summary)


def entry_kernel(prefix_ref, entering_ref, start_ref):
    devices, heads = prefix_ref.shape[0], prefix_ref.shape[1]
    for h in range(heads):
        entering = entering_ref[h]
        high = entering.astype(bf16)
        low = (entering - high.astype(f32)).astype(bf16)
        pair = jnp.concatenate([high, low], axis=1)
        for d in range(devices):
            both = product(prefix_ref[d, h, :, DK:].astype(bf16), pair)
            start_ref[d, h] = (
                prefix_ref[d, h, :, :DK] + (both[:, :DK] + both[:, DK:])
            ).astype(bf16)


def entry_stage(prefix, entering):
    devices, heads = prefix.shape[:2]
    return pl.pallas_call(
        entry_kernel,
        out_shape=jax.ShapeDtypeStruct((devices, heads, DK, DK), bf16),
        compiler_params=pltpu.CompilerParams(vmem_limit_bytes=48 << 20),
        name="entry_stage",
    )(prefix, entering)


def finish_kernel(local_ref, reach_ref, start_ref, gain_ref, out_ref):
    for h in range(start_ref.shape[0]):
        cols = slice(h * DK, (h + 1) * DK)
        result = local_ref[:, cols] + product(reach_ref[:, cols], start_ref[h])
        mean = jnp.mean(result * result, axis=1, keepdims=True)
        out_ref[:, cols] = (result * lax.rsqrt(mean + 1e-06) * gain_ref[...]).astype(bf16)


def finish_stage(local, reach, starts, gain):
    length, width = local.shape
    heads = starts.shape[0]
    step = 4
    return pl.pallas_call(
        finish_kernel,
        grid=(heads // step,),
        in_specs=[
            pl.BlockSpec((length, step * DK), lambda g: (0, g)),
            pl.BlockSpec((length, step * DK), lambda g: (0, g)),
            pl.BlockSpec((step, DK, DK), lambda g: (g, 0, 0)),
            pl.BlockSpec((1, DK), lambda g: (0, 0)),
        ],
        out_specs=pl.BlockSpec((length, step * DK), lambda g: (0, g)),
        out_shape=jax.ShapeDtypeStruct((length, width), bf16),
        compiler_params=pltpu.CompilerParams(vmem_limit_bytes=48 << 20),
        name="finish_stage",
    )(local, reach, starts, gain.reshape(1, DK))


def entering_state(total):
    outer = lax.axis_size("outer")
    if outer == 1:
        return jnp.zeros_like(total[..., :DK])
    if outer == 2:
        return lax.ppermute(total[..., :DK], "outer", [(0, 1)])
    everyone = lax.all_gather(total, "outer", axis=0)
    mine = lax.axis_index("outer")

    def step(i, state):
        piece = lax.dynamic_index_in_dim(everyone, i, 0, keepdims=False)
        moved = piece[..., :DK] + jnp.einsum(
            "hij,hjk->hik", piece[..., DK:], state, precision=lax.Precision.HIGHEST
        )
        return jnp.where(i < mine, moved, state)

    return lax.fori_loop(0, outer - 1, step, jnp.zeros_like(total[..., :DK]))


def per_device(projected, conv_weight, log_gate, write_rate, norm_gain):
    devices = lax.axis_size(ALL)
    parts = lax.axis_size("head")
    route = [(i, i + 1) for i in range(devices - 1)]
    mine = lax.axis_index("head").astype(jnp.int32)
    if parts == 2:
        order = jnp.stack([mine, 1 - mine])
        packs, tail = pack_stage(order, parts, projected, log_gate, write_rate, conv_weight)
        halo = lax.ppermute(tail, ALL, route)
        theirs = lax.ppermute(packs[1:], "head", [(0, 1), (1, 0)])
        pieces = [(order[:1], packs, 0), (order[1:], theirs, 0)]
    else:
        order = jnp.arange(parts, dtype=jnp.int32)
        packs, tail = pack_stage(order, parts, projected, log_gate, write_rate, conv_weight)
        halo = lax.ppermute(tail, ALL, route)
        packs = lax.all_to_all(packs, "head", 0, 0, tiled=True)
        pieces = [(order[p : p + 1], packs, p) for p in range(parts)]

    made = ()
    for part, pack, index in pieces:
        made = local_stage(part, parts, projected, halo, pack, index, made)
    summary, *kept = made
    heads = summary.shape[0]
    near = lax.axis_size(NEAR)
    own = heads // near
    summary = lax.all_to_all(summary, NEAR, 0, 0, tiled=True)
    read = ()
    early = max(1, len(pieces) // 2)
    for part, pack, index in pieces[:early]:
        read = reading_stage(part, parts, projected, halo, pack, index, kept, read)
    summary, read = lax.optimization_barrier((summary, read))
    prefix, total = chain_stage(summary.reshape(near, own, DK, 2 * DK))
    starts = entry_stage(prefix, entering_state(total))
    starts, read = lax.optimization_barrier((starts, read))
    starts = lax.all_to_all(starts.reshape(heads, DK, DK), NEAR, 0, 0, tiled=True)
    for part, pack, index in pieces[early:]:
        read = reading_stage(part, parts, projected, halo, pack, index, kept, read)
    local, reach = read
    return finish_stage(local, reach, starts, norm_gain)


def solution(mesh):
    seq, head = mesh.shape["seq"], mesh.shape["head"]
    inner = max(1, 16 // head)
    while seq % inner:
        inner //= 2
    near = Mesh(mesh.devices.reshape(seq // inner, inner, head), ALL)
    in_specs = (
        P(ALL, None),
        P(None, "head"),
        P("head", ("outer", "inner")),
        P("head", ("outer", "inner")),
        P(),
    )
    return jax.shard_map(
        per_device, mesh=near, in_specs=in_specs, out_specs=P(ALL, None), check_vma=False
    )
```

time: 129 us -> 93.6 us (0.73)
  blocking collectives: 31.9 us -> 0 us
  Pallas kernels: 74.6 us -> 55.7 us
  waiting for transfers between devices: 9.31 us -> 18.7 us
  starting transfers between devices: 8.57 us -> 13.6 us
  local copies, waits for them, and re-layouts: 1.66 us -> 3.71 us
    all_to_all x2 -> x0, blocking collectives: 31.9 us -> none  [the longest x1 18.6 us: per_device(): summary = lax.all_to_all(summary, NEAR, 0, 0, tiled=True)]
    pallas_call x1 -> x5, Pallas kernels: 66 us -> 46.4 us  [the longest x2 29.7 us: local_stage(): pl.pallas_call(functools.partial(local_kernel, number, len(into)), grid_s...]
    all_to_all x1 -> x2, waiting for transfers between devices: 0.01 us -> 9.55 us  [the longest x1 7.61 us: per_device(): summary = lax.all_to_all(summary, NEAR, 0, 0, tiled=True)]
    all_to_all x1 -> x2, starting transfers between devices: 3.38 us -> 8.89 us  [the longest x1 5.01 us: per_device(): lax.all_to_all(starts.reshape(heads, DK, DK), NEAR, 0, 0, tiled=True)]
    unnamed x2 -> x8, local copies, waits for them, and re-layouts: 0.01 us -> 2.86 us
    ppermute x1 -> x2, starting transfers between devices: 3.9 us -> 3.4 us  [the longest x1 3.39 us: per_device(): halo = lax.ppermute(tail, ALL, route)]
    ppermute x1 -> x2, waiting for transfers between devices: 3.45 us -> 3.33 us  [the longest x1 3.33 us: per_device(): halo = lax.ppermute(tail, ALL, route)]
  transfers between devices with their start and end apart: 3 -> 5, of which waited for: 2 -> 4; matrix products, arithmetic and copies ran while one was open for 1% -> 1% of each run, Pallas kernels for 0% -> 32%
where the time goes in v2:
time: 93.6 us; the launch traced here: 92.5 us
  Pallas kernels  55.7 us (60%)
  waiting for transfers between devices  18.7 us (20%)
  starting transfers between devices  13.6 us (15%)
  local copies, waits for them, and re-layouts  3.71 us (4%)
    pallas_call x2, Pallas kernels, local_stage(): pl.pallas_call(functools.partial(local_kernel, number, len(into)), grid_s...  29.7 us
    pallas_call x2, Pallas kernels, reading_stage(): pl.pallas_call(functools.partial(reading_kernel, number), grid_spec=pltpu...  14.4 us
    all_to_all x1, waiting for transfers between devices, per_device(): summary = lax.all_to_all(summary, NEAR, 0, 0, tiled=True)  7.61 us
    ppermute x1, waiting for transfers between devices, entering_state(): return lax.ppermute(total[..., :DK], 'outer', [(0, 1)])  5.86 us
    pallas_call x1, Pallas kernels, finish_stage(): pl.pallas_call(finish_kernel, grid=(heads // step,), in_specs=[pl.BlockSp...  5.13 us
    all_to_all x1, starting transfers between devices, per_device(): lax.all_to_all(starts.reshape(heads, DK, DK), NEAR, 0, 0, tiled=True)  5.01 us
    all_to_all x1, starting transfers between devices, per_device(): summary = lax.all_to_all(summary, NEAR, 0, 0, tiled=True)  3.88 us
    ppermute x1, starting transfers between devices, per_device(): halo = lax.ppermute(tail, ALL, route)  3.39 us
  transfers between devices with their start and end apart: 5, of which 4 were waited for; matrix products, arithmetic and copies ran while one was open for 1% of the time, Pallas kernels for 32%

profile of v2, /device:TPU:16, one launch (start us, length us, event | category | flops | bytes accessed | tf_op | source)
XLA Modules:
  0.0 92.5 jit_solution(8318663007842754402)
XLA Ops:
  0.0 0.6 pad_add_fusion.at_ref
  0.6 2.2 %pack_stage.1 = (f32[2,128,128]{2,1,0:T(8,128)}, bf16[8,4096]{1,0:T(8,128)(2,1)}) custom-call(s32[2]{0:T(128)} %pad_add_fusion.at_ref, bf16[512,4096]{1,0:T(8,128)(2,1)} %refs_3_.3, f32[8,1024]{1,0:T(8,128)} %gate_ref.1, f32[8,1024]{1,0:T(8,128)} %rate_ref.1, bf16[4,2048]{1,0:T(4,128)(2,1)} %taps_ref.1), custom_call_target="tpu_custom_call" | custom-call | tf_op jit(solution)/shard_map/pack_stage/pallas_call | solution.py:140
  2.9 3.4 %collective-permute-start = (bf16[8,4096]{1,0:T(8,128)(2,1)}, bf16[8,4096]{1,0:T(8,128)(2,1)S(1)}, u32[]{:S(2)}, u32[]{:S(2)}) collective-permute-start(bf16[8,4096]{1,0:T(8,128)(2,1)} %get-tuple-element.29), channel_id=1, source_target_pairs={{0,1},{1,2},{2,3},{3,4},{4,5},{5,6},{6,7},{7,8},{8,9},{9,10},{10,1... | collective-permute-start | bytes 196616 | tf_op jit(solution)/shard_map/ppermute | solution.py:481
  6.3 0.8 slice.6
  7.1 0.0 collective-permute-start.1
  7.1 3.3 %collective-permute-done.halo_ref.refs_4_.refs_5_.refs_6_.refs_7_ = bf16[8,4096]{1,0:T(8,128)(2,1)S(1)} collective-permute-done((bf16[8,4096]{1,0:T(8,128)(2,1)}, bf16[8,4096]{1,0:T(8,128)(2,1)S(1)}, u32[]{:S(2)}, u32[]{:S(2)}) %collective-permute-start) | collective-permute-done | bytes 65568 | tf_op jit(solution)/shard_map/ppermute | solution.py:481
  10.4 0.0 copy-start.2
  10.4 0.6 copy-done.2
  11.1 14.8 %local_stage.2 = (bf16[16,128,256]{2,1,0:T(8,128)(2,1)}, bf16[4,16,128,256]{3,2,1,0:T(8,128)(2,1)}, bf16[4,16,128,256]{3,2,1,0:T(8,128)(2,1)}, bf16[512,1024]{1,0:T(8,128)(2,1)}, f32[8,4,128]{2,1,0:T(4,128)}) custom-call(s32[1]{0:T(128)} %bitcast.1.part_ref, bf16[512,4096]{1,0:T(8,128)(2,1)} %refs_3_.3, bf16[8,4096]{1,0:T(8,128)(2,1)} %copy-done.2, ...), custom_call_target="tpu_custom_call" | custom-call | tf_op jit(solution)/shard_map/local_stage/pallas_call | solution.py:254
  25.9 0.0 collective-permute-done.1.pack_ref.refs_8_
  25.9 0.0 copy-start.3
  25.9 0.6 copy-done.3
  26.5 14.9 %local_stage.3 = (bf16[16,128,256]{2,1,0:T(8,128)(2,1)}, bf16[4,16,128,256]{3,2,1,0:T(8,128)(2,1)}, bf16[4,16,128,256]{3,2,1,0:T(8,128)(2,1)}, bf16[512,1024]{1,0:T(8,128)(2,1)}, f32[8,4,128]{2,1,0:T(4,128)}) custom-call(s32[1]{0:T(128)} %bitcast.part_ref, ...), custom_call_target="tpu_custom_call", output_to_operand_aliasing={{0}: (4, {}), {1}: (5, {}), {2}: (6, {}), {3}: (7, {}), {4}... | custom-call | tf_op jit(solution)/shard_map/local_stage/pallas_call | solution.py:254
  41.4 3.9 %all-to-all-start = ((bf16[16,128,256]{2,1,0:T(8,128)(2,1)}), bf16[16,128,256]{2,1,0:T(8,128)(2,1)S(1)}, u32[]{:S(2)}, u32[]{:S(2)}) async-start(bf16[16,128,256]{2,1,0:T(8,128)(2,1)} %get-tuple-element.40), calls=%async_computation | async-start | bytes 2097152 | tf_op jit(solution)/shard_map/all_to_all | solution.py:498
  45.3 7.2 %reading_stage.2 = (f32[512,2048]{1,0:T(8,128)}, bf16[512,2048]{1,0:T(8,128)(2,1)}) custom-call(s32[1]{0:T(128)} %bitcast.1.part_ref, bf16[512,4096]{1,0:T(8,128)(2,1)} %refs_3_.3, bf16[512,4096]{1,0:T(8,128)(2,1)} %refs_3_.3, bf16[512,4096]{1,0:T(8,128)(2,1)} %refs_3_.3, bf16[512,4096]{1,0:T(8,128)(2,1)} %refs_3_.3, bf16[8,4096]{1,0:T(8,128)(2,1)} %copy-done.2, ...), custom_call_target="tpu_custom_call" | custom-call | tf_op jit(solution)/shard_map/reading_stage/pallas_call | solution.py:342
  52.5 7.6 %all-to-all-done = bf16[16,128,256]{2,1,0:T(8,128)(2,1)S(1)} async-done(((bf16[16,128,256]{2,1,0:T(8,128)(2,1)}), bf16[16,128,256]{2,1,0:T(8,128)(2,1)S(1)}, u32[]{:S(2)}, u32[]{:S(2)}) %all-to-all-start) | async-done | bytes 1048608 | tf_op jit(solution)/shard_map/all_to_all | solution.py:498
  60.1 3.0 %chain_stage.1 = (f32[16,1,128,256]{3,2,1,0:T(8,128)S(1)}, f32[1,128,256]{2,1,0:T(8,128)S(1)}) custom-call(bf16[16,1,128,256]{3,2,1,0:T(8,128)(2,1)S(1)} %bitcast.5), custom_call_target="tpu_custom_call" | custom-call | tf_op jit(solution)/shard_map/chain_stage/pallas_call | solution.py:391
  63.1 1.3 %collective-permute-start.2 = (f32[1,128,128]{2,1,0:T(8,128)S(1)}, f32[1,128,128]{2,1,0:T(8,128)S(1)}, u32[]{:S(2)}, u32[]{:S(2)}) collective-permute-start(f32[1,128,128]{2,1,0:T(8,128)S(1)} %slice.7), channel_id=1, source_target_pairs={{0,16},{1,17},{2,18},{3,19},{4,20},{5,21},{6,22},{7,23},{8,24},{9,... | collective-permute-start | bytes 196616 | tf_op jit(solution)/shard_map/ppermute | solution.py:459
  64.4 5.9 %collective-permute-done.2.entering_ref = f32[1,128,128]{2,1,0:T(8,128)S(1)} collective-permute-done((f32[1,128,128]{2,1,0:T(8,128)S(1)}, f32[1,128,128]{2,1,0:T(8,128)S(1)}, u32[]{:S(2)}, u32[]{:S(2)}) %collective-permute-start.2) | collective-permute-done | bytes 65568 | tf_op jit(solution)/shard_map/ppermute | solution.py:459
  70.3 1.3 %entry_stage.1 = bf16[16,1,128,128]{3,2,1,0:T(8,128)(2,1)} custom-call(f32[16,1,128,256]{3,2,1,0:T(8,128)S(1)} %get-tuple-element.44.prefix_ref, f32[1,128,128]{2,1,0:T(8,128)S(1)} %collective-permute-done.2.entering_ref), custom_call_target="tpu_custom_call" | custom-call | tf_op jit(solution)/shard_map/entry_stage/pallas_call | solution.py:418
  71.6 5.0 %all-to-all-start.1 = ((bf16[16,128,128]{2,1,0:T(8,128)(2,1)}), bf16[16,128,128]{2,1,0:T(8,128)(2,1)S(1)}, u32[]{:S(2)}, u32[]{:S(2)}) async-start(bf16[16,128,128]{2,1,0:T(8,128)(2,1)} %bitcast.3), calls=%async_computation.1 | async-start | bytes 1048576 | tf_op jit(solution)/shard_map/all_to_all | solution.py:507
  76.6 0.0 copy-start.1
  76.6 7.2 %reading_stage.3 = (f32[512,2048]{1,0:T(8,128)}, bf16[512,2048]{1,0:T(8,128)(2,1)}) custom-call(s32[1]{0:T(128)} %bitcast.part_ref, bf16[512,4096]{1,0:T(8,128)(2,1)} %refs_3_.3, bf16[512,4096]{1,0:T(8,128)(2,1)} %refs_3_.3, bf16[512,4096]{1,0:T(8,128)(2,1)} %refs_3_.3, bf16[512,4096]{1,0:T(8,128)(2,1)} %refs_3_.3, ...), custom_call_target="tpu_custom_call", output_to_operand_aliasing={{0}: (14, {}), {1}: (15, {})} | custom-call | tf_op jit(solution)/shard_map/reading_stage/pallas_call | solution.py:342
  83.8 1.9 %all-to-all-done.1.start_ref = bf16[16,128,128]{2,1,0:T(8,128)(2,1)S(1)} async-done(((bf16[16,128,128]{2,1,0:T(8,128)(2,1)}), bf16[16,128,128]{2,1,0:T(8,128)(2,1)S(1)}, u32[]{:S(2)}, u32[]{:S(2)}) %all-to-all-start.1) | async-done | bytes 524320 | tf_op jit(solution)/shard_map/all_to_all | solution.py:507
  85.7 0.0 copy-done.1
  85.8 0.0 copy-start
  85.8 1.6 %copy-done = bf16[512,2048]{1,0:T(8,128)(2,1)S(1)} copy-done((bf16[512,2048]{1,0:T(8,128)(2,1)S(1)}, bf16[512,2048]{1,0:T(8,128)(2,1)}, u32[]{:S(2)}) %copy-start) | copy-done | bytes 2097176
  87.3 5.1 %finish_stage.1 = bf16[512,2048]{1,0:T(8,128)(2,1)} custom-call(f32[512,2048]{1,0:T(8,128)} %get-tuple-element.50.local_ref, bf16[512,2048]{1,0:T(8,128)(2,1)S(1)} %copy-done, bf16[16,128,128]{2,1,0:T(8,128)(2,1)S(1)} %all-to-all-done.1.start_ref, f32[1,128]{1,0:T(1,128)S(1)} %bitcast.6), custom_call_target="tpu_custom_call" | custom-call | tf_op jit(solution)/shard_map/finish_stage/pallas_call | solution.py:438
  (1 shorter events, 0.0 us)
Async XLA Ops:
  2.9 7.6 %collective-permute-start = (bf16[8,4096]{1,0:T(8,128)(2,1)}, bf16[8,4096]{1,0:T(8,128)(2,1)S(1)}, u32[]{:S(2)}, u32[]{:S(2)}) collective-permute-start(bf16[8,4096]{1,0:T(8,128)(2,1)} %get-tuple-element.29), channel_id=1, source_target_pairs={{0,1},{1,2},{2,3},{3,4},{4,5},{5,6},{6,7},{7,8},{8,9},{9,10},{10,1... | collective-permute-start | bytes 196616 | tf_op jit(solution)/shard_map/ppermute | solution.py:481
  7.1 18.8 %collective-permute-start.1 = (f32[1,128,128]{2,1,0:T(8,128)S(1)}, f32[1,128,128]{2,1,0:T(8,128)S(1)}, u32[]{:S(2)}, u32[]{:S(2)}) collective-permute-start(f32[1,128,128]{2,1,0:T(8,128)S(1)} %slice.6), channel_id=1, source_target_pairs={{0,1},{1,0},{2,3},{3,2},{4,5},{5,4},{6,7},{7,6},{8,9},{9,8},{10,11... | collective-permute-start | bytes 196616 | tf_op jit(solution)/shard_map/ppermute | solution.py:482
  10.4 0.6 copy-start.2
  25.9 0.6 copy-start.3
  41.4 18.7 %all-to-all-start = ((bf16[16,128,256]{2,1,0:T(8,128)(2,1)}), bf16[16,128,256]{2,1,0:T(8,128)(2,1)S(1)}, u32[]{:S(2)}, u32[]{:S(2)}) async-start(bf16[16,128,256]{2,1,0:T(8,128)(2,1)} %get-tuple-element.40), calls=%async_computation | async-start | bytes 2097152 | tf_op jit(solution)/shard_map/all_to_all | solution.py:498
  63.1 7.2 %collective-permute-start.2 = (f32[1,128,128]{2,1,0:T(8,128)S(1)}, f32[1,128,128]{2,1,0:T(8,128)S(1)}, u32[]{:S(2)}, u32[]{:S(2)}) collective-permute-start(f32[1,128,128]{2,1,0:T(8,128)S(1)} %slice.7), channel_id=1, source_target_pairs={{0,16},{1,17},{2,18},{3,19},{4,20},{5,21},{6,22},{7,23},{8,24},{9,... | collective-permute-start | bytes 196616 | tf_op jit(solution)/shard_map/ppermute | solution.py:459
  71.6 14.2 %all-to-all-start.1 = ((bf16[16,128,128]{2,1,0:T(8,128)(2,1)}), bf16[16,128,128]{2,1,0:T(8,128)(2,1)S(1)}, u32[]{:S(2)}, u32[]{:S(2)}) async-start(bf16[16,128,128]{2,1,0:T(8,128)(2,1)} %bitcast.3), calls=%async_computation.1 | async-start | bytes 1048576 | tf_op jit(solution)/shard_map/all_to_all | solution.py:507
  76.6 9.2 %copy-start.1 = (f32[128]{0:T(128)S(1)}, f32[128]{0:T(128)}, u32[]{:S(2)}) copy-start(f32[128]{0:T(128)} %param.9) | copy-start | bytes 1540
  85.8 1.6 %copy-start = (bf16[512,2048]{1,0:T(8,128)(2,1)S(1)}, bf16[512,2048]{1,0:T(8,128)(2,1)}, u32[]{:S(2)}) copy-start(bf16[512,2048]{1,0:T(8,128)(2,1)} %get-tuple-element.51.reach_ref) | copy-start | bytes 6291460

commit v3 on v2

v3 whole, which is shorter than its diff:
```python
import functools

import jax
import jax.numpy as jnp
from jax import lax
from jax.experimental import pallas as pl
from jax.experimental.pallas import tpu as pltpu
from jax.sharding import Mesh
from jax.sharding import PartitionSpec as P

DK = 128
V_GROUP = 2
KW = 4
STRETCH = 128
HALO = 8
BASE = 16
SEGMENTS = 2 + V_GROUP
GROUP_CHANNELS = (2 + V_GROUP) * DK
ALL = ("outer", "inner", "head")
NEAR = ("inner", "head")

f32 = jnp.float32
bf16 = jnp.bfloat16


VMEM = pl.BlockSpec(memory_space=pltpu.VMEM)
SMEM = pl.BlockSpec(memory_space=pltpu.SMEM)
FAR = pl.BlockSpec(memory_space=pltpu.HBM)


def near(array):
    return pltpu.with_memory_space_constraint(array, pltpu.VMEM)


def far(array):
    return pltpu.with_memory_space_constraint(array, pltpu.HBM)


def product(left, right):
    return jnp.dot(left, right, preferred_element_type=f32)


def part_at(first, step, parts):
    return lax.rem(first + step, parts)


def lanes_of(start):
    return pl.ds(pl.multiple_of(start, DK), DK)


def convolved(ext, cols, taps, c):
    start = c * STRETCH + HALO - (KW - 1)
    total = ext[start : start + STRETCH, cols] * taps[0:1]
    for j in range(1, KW):
        total = total + ext[start + j : start + j + STRETCH, cols] * taps[j : j + 1]
    half = 0.5 * total
    return (half + half * jnp.tanh(half)).astype(bf16)


def running_sum(gates):
    lane = lax.broadcasted_iota(jnp.int32, gates.shape, 1)
    total = gates
    for k in (1, 2, 4, 8, 16, 32, 64):
        total = total + jnp.where(lane >= k, pltpu.roll(total, k, 1), 0.0)
    return total


def square_iotas():
    row = lax.broadcasted_iota(jnp.int32, (STRETCH, STRETCH), 0)
    col = lax.broadcasted_iota(jnp.int32, (STRETCH, STRETCH), 1)
    return row, col


def block_inverses(lower):
    units = len(lower)
    blocks = STRETCH // BASE
    small_lane = lax.broadcasted_iota(jnp.int32, (BASE, STRETCH), 1)
    small_row = lax.broadcasted_iota(jnp.int32, (BASE, STRETCH), 0)
    owner = small_lane // BASE
    packed = []
    for unit in range(units):
        piece = lower[unit][0:BASE]
        for b in range(1, blocks):
            piece = jnp.where(owner == b, lower[unit][b * BASE : (b + 1) * BASE], piece)
        packed.append(piece)
    packed = jnp.concatenate(packed, axis=0)
    group_start = (lax.broadcasted_iota(jnp.int32, packed.shape, 1) // BASE) * BASE
    start = jnp.where(small_lane % BASE == small_row, 1.0, 0.0).astype(f32)
    solved = jnp.broadcast_to(start[None], (units, BASE, STRETCH))
    for j in range(BASE - 1):
        spread_col = jnp.take_along_axis(packed, group_start + j, axis=1)
        solved = solved - spread_col.reshape(units, BASE, STRETCH) * solved[:, j : j + 1, :]

    rows = [
        [jnp.where(owner == b, solved[unit], 0.0) for b in range(blocks)] for unit in range(units)
    ]
    size = BASE
    while size < STRETCH:
        per = size // BASE
        odd = [b for b in range(blocks) if (b // per) % 2 == 1]
        firsts = []
        for unit in range(units):
            crossing = [
                jnp.where(
                    small_lane // size == (b // per) - 1,
                    lower[unit][b * BASE : (b + 1) * BASE],
                    0.0,
                )
                for b in odd
            ]
            firsts.append(
                product(
                    jnp.concatenate(crossing, axis=0).astype(bf16),
                    jnp.concatenate(rows[unit], axis=0).astype(bf16),
                ).astype(bf16)
            )
        for unit in range(units):
            laid = [jnp.zeros((BASE, STRETCH), bf16)] * blocks
            for i, b in enumerate(odd):
                laid[b] = firsts[unit][i * BASE : (i + 1) * BASE]
            odd_rows = jnp.concatenate([rows[unit][b] for b in odd], axis=0)
            updated = odd_rows - product(odd_rows.astype(bf16), jnp.concatenate(laid, axis=0))
            for i, b in enumerate(odd):
                rows[unit][b] = updated[i * BASE : (i + 1) * BASE]
        size *= 2
    return [jnp.concatenate(rows[unit], axis=0) for unit in range(units)]


def pack_kernel(parts, first_ref, x_ref, gate_ref, rate_ref, taps_ref, halo_ref, *pack_refs):
    heads = gate_ref.shape[0]
    length = gate_ref.shape[1] // parts
    number = length // STRETCH
    segments = taps_ref.shape[1] // DK
    halo_ref[...] = x_ref[...]
    base = 2 * number * heads
    slots = [(ref, i) for ref in pack_refs for i in range(ref.shape[0])]
    for step, (ref, i) in enumerate(slots):
        first = part_at(first_ref[0], step, parts) * length
        for c in range(number):
            lanes = lanes_of(first + c * STRETCH)
            ref[i, c * heads : (c + 1) * heads] = gate_ref[:, lanes]
            ref[i, (number + c) * heads : (number + c + 1) * heads] = rate_ref[:, lanes]
        for segment in range(segments):
            rows = slice(base + segment * KW, base + (segment + 1) * KW)
            ref[i, rows] = taps_ref[:, segment * DK : (segment + 1) * DK].astype(f32)


def pack_stage(first, stacks, parts, projected, log_gate, write_rate, conv_weight):
    length, channels = projected.shape
    heads = log_gate.shape[0]
    rows = 2 * (length // STRETCH) * heads + conv_weight.shape[1] // DK * KW
    whole = lambda array: pl.BlockSpec(array.shape, lambda i: (0, 0))
    return pl.pallas_call(
        functools.partial(pack_kernel, parts),
        grid=(1,),
        in_specs=[
            SMEM,
            pl.BlockSpec((HALO, channels), lambda i: (length // HALO - 1, 0)),
            whole(log_gate),
            whole(write_rate),
            whole(conv_weight),
        ],
        out_specs=[VMEM] * (1 + len(stacks)),
        out_shape=[pltpu.VMEM((HALO, channels), bf16)]
        + [pltpu.VMEM((count, rows, DK), f32) for count in stacks],
        compiler_params=pltpu.CompilerParams(vmem_limit_bytes=2 << 20),
        name="pack_stage",
    )(first, far(projected), far(log_gate), far(write_rate), far(conv_weight))


def local_kernel(number, parts, stacks, first_ref, x_ref, halo_ref, *refs):
    pack_refs, refs = refs[: len(stacks)], refs[len(stacks) :]
    summary_out, written_out, joint_out, key_out, norm_ref = refs[:5]
    pack, blocks, ext, summaries, writtens, joints, keys_held, in_sems, out_sems = refs[5:]
    step = pl.program_id(0)
    slot = lax.rem(step, 2)
    part = part_at(first_ref[0], step, parts)
    key_heads = norm_ref.shape[1]
    width = key_heads * GROUP_CHANNELS
    heads = key_heads * V_GROUP
    units = heads * number
    block, summary_ref, written_ref = blocks.at[slot], summaries.at[slot], writtens.at[slot]
    joint_ref, key_ref = joints.at[slot], keys_held.at[slot]

    def arriving(at):
        here = lax.rem(at, 2)
        base = part_at(first_ref[0], at, parts) * width
        used = (SEGMENTS - 1) * DK
        copies = []
        for g in range(key_heads):
            source = pl.ds(pl.multiple_of(base + (g * SEGMENTS + 1) * DK, DK), used)
            target = pl.ds((g * SEGMENTS + 1) * DK, used)
            copies.append(
                pltpu.make_async_copy(
                    x_ref.at[:, source], blocks.at[here, :, target], in_sems.at[here, g]
                )
            )
        return copies

    def leaving(at):
        here = lax.rem(at, 2)
        place = pl.ds(part_at(first_ref[0], at, parts) * heads, heads)
        pairs = [(keys_held.at[here], key_out.at[at]), (summaries.at[here], summary_out.at[place])]
        pairs += [(writtens.at[here, c], written_out.at[at, c]) for c in range(number)]
        pairs += [(joints.at[here, c - 1], joint_out.at[at, c]) for c in range(1, number)]
        return [
            pltpu.make_async_copy(source, target, out_sems.at[here, i])
            for i, (source, target) in enumerate(pairs)
        ]

    @pl.when(step == 0)
    def _():
        for copy in arriving(step):
            copy.start()

    @pl.when(step + 1 < pl.num_programs(0))
    def _():
        for copy in arriving(step + 1):
            copy.start()

    coming, going = arriving(step), leaving(step)
    entries = [(ref, i) for ref in pack_refs for i in range(ref.shape[0])]
    for n, (ref, i) in enumerate(entries):

        @pl.when(step == n)
        def _():
            pack[...] = ref[i]

    row, col = square_iotas()
    below = row > col
    eye = jnp.where(row == col, 1.0, 0.0).astype(f32)

    rates = pack[units : 2 * units]
    cumulative = running_sum(pack[0:units])
    grown = jnp.exp(cumulative)
    tail = jnp.exp(cumulative[:, STRETCH - 1 : STRETCH] - cumulative)
    columns = jnp.transpose(jnp.concatenate([cumulative, rates], axis=0), (1, 0))
    where = [(c, g) for g in range(key_heads) for c in range(number)]

    def units_of(c, g):
        return [(j, c * heads + g * V_GROUP + j) for j in range(V_GROUP)]

    def channels(c, g, kind):
        segment = g * SEGMENTS + kind
        cols = slice(segment * DK, (segment + 1) * DK)
        if c == 0:
            ext[0:HALO, cols] = halo_ref[:, lanes_of(part * width + segment * DK)].astype(f32)
            ext[HALO:, cols] = block[:, cols].astype(f32)
        at = 2 * units + segment * KW
        return convolved(ext, cols, pack[at : at + KW], c)

    keys, inverses, lower = {}, {}, [None] * units
    for c, g in where:
        if c == 0:
            coming[g].wait()
        k = channels(c, g, 1)
        keys[c, g] = k
        key_ref[c * STRETCH : (c + 1) * STRETCH, g * DK : (g + 1) * DK] = k
        gram = lax.dot_general(k, k, (((1,), (1,)), ((), ())), preferred_element_type=f32)
        diagonal = gram * eye
        inverse_row = lax.rsqrt(jnp.sum(diagonal, axis=0, keepdims=True) + 1e-06)
        inverse_col = lax.rsqrt(jnp.sum(diagonal, axis=1, keepdims=True) + 1e-06)
        inverses[c, g] = inverse_row
        norm_ref[0, g, c : c + 1] = inverse_row
        gram = gram * inverse_row
        for j, unit in units_of(c, g):
            spread = columns[:, unit : unit + 1] - cumulative[unit : unit + 1]
            decay = jnp.exp(jnp.where(below, spread, -1e30))
            lower[unit] = gram * decay * (columns[:, units + unit : units + unit + 1] * inverse_col)

    going[0].start()
    solved = block_inverses(lower)

    fresh, carried, scaled = [None] * units, [None] * units, [None] * units
    for c, g in where:
        turned = jnp.transpose(keys[c, g].astype(f32), (1, 0)) * inverses[c, g]
        for j, unit in units_of(c, g):
            at = slice(unit, unit + 1)
            by_rate = solved[unit] * rates[at]
            fresh[unit] = product(by_rate.astype(bf16), channels(c, g, 2 + j))
            by_rate = by_rate * (grown[at] * inverses[c, g])
            carried[unit] = product(by_rate.astype(bf16), keys[c, g])
            scaled[unit] = (turned * tail[at]).astype(bf16)

    nothing = jnp.zeros((STRETCH, DK), f32)
    joint = [jnp.concatenate([jnp.zeros((DK, DK), f32), eye], axis=1)] * heads
    for c in range(number):
        for head in range(heads):
            unit = c * heads + head
            if c == 0:
                written = jnp.concatenate([fresh[unit], -carried[unit]], axis=1)
            else:
                start = joint[head].astype(bf16)
                joint_ref[c - 1, head] = start
                written = jnp.concatenate([fresh[unit], nothing], axis=1) - product(
                    carried[unit].astype(bf16), start
                )
            written = written.astype(bf16)
            written_ref[c, head] = written
            decay = grown[unit : unit + 1, STRETCH - 1 : STRETCH]
            joint[head] = joint[head] * decay + product(scaled[unit], written)
        going[2 + c].start()
        if c > 0:
            going[1 + number + c].start()
    for head in range(heads):
        summary_ref[head, :, :DK] = joint[head][:, :DK].astype(bf16)
        summary_ref[head, :, DK:] = (joint[head][:, DK:] - eye).astype(bf16)
    going[1].start()

    @pl.when(step > 0)
    def _():
        for copy in leaving(step - 1):
            copy.wait()

    @pl.when(step + 1 == pl.num_programs(0))
    def _():
        for copy in going:
            copy.wait()


def local_stage(first, parts, projected, halo, packs):
    length, channels = projected.shape
    number = length // STRETCH
    width = channels // parts
    key_heads = width // GROUP_CHANNELS
    heads = key_heads * V_GROUP
    per_unit = (number, heads, STRETCH, 2 * DK)
    later = (max(1, number - 1), heads, STRETCH, 2 * DK)
    return pl.pallas_call(
        functools.partial(local_kernel, number, parts, tuple(p.shape[0] for p in packs)),
        grid=(parts,),
        in_specs=[SMEM, FAR] + [VMEM] * (1 + len(packs)),
        out_specs=[FAR] * 4
        + [pl.BlockSpec((1, key_heads, number, STRETCH), lambda p: (p, 0, 0, 0))],
        out_shape=[
            pltpu.HBM((heads * parts, DK, 2 * DK), bf16),
            pltpu.HBM((parts,) + per_unit, bf16),
            pltpu.HBM((parts,) + per_unit, bf16),
            pltpu.HBM((parts, length, key_heads * DK), bf16),
            jax.ShapeDtypeStruct((parts, key_heads, number, STRETCH), f32),
        ],
        scratch_shapes=[
            pltpu.VMEM(packs[0].shape[1:], f32),
            pltpu.VMEM((2, length, width), bf16),
            pltpu.VMEM((HALO + length, width), f32),
            pltpu.VMEM((2, heads, DK, 2 * DK), bf16),
            pltpu.VMEM((2,) + per_unit, bf16),
            pltpu.VMEM((2,) + later, bf16),
            pltpu.VMEM((2, length, key_heads * DK), bf16),
            pltpu.SemaphoreType.DMA((2, key_heads)),
            pltpu.SemaphoreType.DMA((2, 2 * number + 1)),
        ],
        compiler_params=pltpu.CompilerParams(vmem_limit_bytes=44 << 20),
        name="local_stage",
    )(first, far(projected), near(halo), *(near(p) for p in packs))


def reading_kernel(number, index, first_ref, x_ref, halo_ref, pack_ref, *refs):
    written_ref, joint_ref, key_ref, norm_ref, out_ref, reach_ref, ext = refs
    heads = pl.num_programs(0) * V_GROUP
    g = pl.program_id(0)
    units = heads * number
    row, col = square_iotas()
    inside = row >= col
    gates = [
        pack_ref[index, pl.ds(c * heads + g * V_GROUP, V_GROUP)] for c in range(number)
    ]
    cumulative = running_sum(jnp.concatenate(gates, axis=0))
    columns = jnp.transpose(cumulative, (1, 0))
    ext[0:HALO] = halo_ref[...].astype(f32)
    ext[HALO:] = x_ref[...].astype(f32)
    taps = pack_ref[index, pl.ds(2 * units + g * SEGMENTS * KW, KW)]
    for c in range(number):
        rows = slice(c * STRETCH, (c + 1) * STRETCH)
        query = convolved(ext, slice(0, DK), taps, c)
        gram = lax.dot_general(
            query, key_ref[0, rows], (((1,), (1,)), ((), ())), preferred_element_type=f32
        )
        gram = gram * norm_ref[0, pl.ds(g, 1), c]
        for j in range(V_GROUP):
            unit = c * V_GROUP + j
            sum_here = columns[:, unit : unit + 1]
            decay = jnp.exp(jnp.where(inside, sum_here - cumulative[unit : unit + 1], -1e30))
            result = product((gram * decay).astype(bf16), written_ref[0, c, j])
            grown = jnp.exp(sum_here)
            if c == 0:
                reached = result[:, DK:] + grown * query.astype(f32)
            else:
                result = result + grown * product(query, joint_ref[0, c, j])
                reached = result[:, DK:]
            out_ref[j, rows] = result[:, :DK].astype(bf16)
            reach_ref[j, rows] = reached.astype(bf16)


def reading_stage(first, step, parts, projected, halo, packs, index, kept):
    length, channels = projected.shape
    number = length // STRETCH
    key_heads = channels // parts // GROUP_CHANNELS
    heads = key_heads * V_GROUP
    written, joints, keys, norms = kept
    query = lambda g, first: (0, (part_at(first[0], step, parts) * key_heads + g) * SEGMENTS)
    per_unit = pl.BlockSpec(
        (1, number, V_GROUP, STRETCH, 2 * DK), lambda g, first: (step, 0, g, 0, 0)
    )
    per_head = pl.BlockSpec((V_GROUP, length, DK), lambda g, first: (g, 0, 0))
    return pl.pallas_call(
        functools.partial(reading_kernel, number, index),
        grid_spec=pltpu.PrefetchScalarGridSpec(
            num_scalar_prefetch=1,
            grid=(key_heads,),
            in_specs=[
                pl.BlockSpec((length, DK), query),
                pl.BlockSpec((HALO, DK), query),
                pl.BlockSpec(packs.shape, lambda g, first: (0, 0, 0)),
                per_unit,
                per_unit,
                pl.BlockSpec((1, length, DK), lambda g, first: (step, 0, g)),
                pl.BlockSpec((1,) + norms.shape[1:], lambda g, first: (step, 0, 0, 0)),
            ],
            out_specs=[per_head, per_head],
            scratch_shapes=[pltpu.VMEM((HALO + length, DK), f32)],
        ),
        out_shape=[pltpu.HBM((heads, length, DK), bf16)] * 2,
        compiler_params=pltpu.CompilerParams(vmem_limit_bytes=12 << 20),
        name="reading_stage",
    )(first, far(projected), halo, packs, far(written), far(joints), far(keys), norms)


def advance(joint, loss, gain):
    high = joint.astype(bf16)
    low = (joint - high.astype(f32)).astype(bf16)
    return joint + (product(loss, high) + product(loss, low)) + gain


def chain_kernel(run, summary_ref, state_ref, loss_ref, sub_ref, total_ref):
    devices, heads = summary_ref.shape[0], summary_ref.shape[1]
    row, col = square_iotas()
    eye = jnp.where(row == col, 1.0, 0.0).astype(f32)
    nothing = jnp.zeros((DK, DK), f32)
    start = jnp.concatenate([nothing, eye], axis=1)
    for h in range(heads):
        joint = [start] * (devices // run)
        for k in range(run):
            for i in range(devices // run):
                d = i * run + k
                state_ref[d, h] = joint[i][:, :DK]
                loss_ref[d, h] = (joint[i][:, DK:] - eye).astype(bf16)
                gain = jnp.concatenate([summary_ref[d, h, :, :DK].astype(f32), nothing], axis=1)
                joint[i] = advance(joint[i], summary_ref[d, h, :, DK:], gain)
        total = joint[0]
        for i in range(devices // run):
            sub_ref[i, h] = joint[i]
            if i > 0:
                gain = jnp.concatenate([joint[i][:, :DK], nothing], axis=1)
                total = advance(total, (joint[i][:, DK:] - eye).astype(bf16), gain)
        total_ref[h] = total


def chain_stage(summary):
    devices, heads = summary.shape[:2]
    run = 4 if devices % 4 == 0 else devices
    return pl.pallas_call(
        functools.partial(chain_kernel, run),
        in_specs=[VMEM],
        out_specs=[VMEM] * 4,
        out_shape=[
            pltpu.VMEM((devices, heads, DK, DK), f32),
            pltpu.VMEM((devices, heads, DK, DK), bf16),
            pltpu.VMEM((devices // run, heads, DK, 2 * DK), f32),
            pltpu.VMEM((heads, DK, 2 * DK), f32),
        ],
        compiler_params=pltpu.CompilerParams(vmem_limit_bytes=12 << 20),
        name="chain_stage",
    )(near(summary))


def entry_kernel(state_ref, loss_ref, sub_ref, entering_ref, start_ref):
    devices, heads = state_ref.shape[0], state_ref.shape[1]
    runs = sub_ref.shape[0]
    run = devices // runs
    row, col = square_iotas()
    eye = jnp.where(row == col, 1.0, 0.0).astype(f32)
    for h in range(heads):
        entering = [entering_ref[h]]
        for i in range(runs - 1):
            loss = (sub_ref[i, h, :, DK:] - eye).astype(bf16)
            entering.append(advance(entering[i], loss, sub_ref[i, h, :, :DK]))
        for d in range(devices):
            start = advance(entering[d // run], loss_ref[d, h], state_ref[d, h])
            start_ref[d, h] = start.astype(bf16)


def entry_stage(states, losses, subs, entering):
    devices, heads = states.shape[:2]
    return pl.pallas_call(
        entry_kernel,
        in_specs=[VMEM] * 4,
        out_specs=VMEM,
        out_shape=jax.ShapeDtypeStruct((devices, heads, DK, DK), bf16),
        compiler_params=pltpu.CompilerParams(vmem_limit_bytes=12 << 20),
        name="entry_stage",
    )(states, losses, subs, near(entering))


def finish_kernel(batch, first_ref, start_ref, gain_ref, *refs):
    reads, refs = refs[:-7], refs[-7:]
    out_ref, gain, held_local, held_reach, done, in_sems, out_sems = refs
    parts = len(reads) // 2
    heads = reads[0].shape[0]
    arriving, leaving = [], []
    for p in range(parts):
        for b in range(heads // batch):
            at = pl.ds(b * batch, batch)
            into = pl.ds(p * heads + b * batch, batch)
            n = len(arriving)
            arriving.append(
                (
                    pltpu.make_async_copy(
                        reads[2 * p].at[at], held_local.at[into], in_sems.at[0, n]
                    ),
                    pltpu.make_async_copy(
                        reads[2 * p + 1].at[at], held_reach.at[into], in_sems.at[1, n]
                    ),
                )
            )
            for copy in arriving[-1]:
                copy.start()
    gain_copy = pltpu.make_async_copy(gain_ref, gain, in_sems.at[0, len(arriving)])
    gain_copy.start()
    gain_copy.wait()
    for p in range(parts):
        part = part_at(first_ref[0], p, parts)
        for b in range(heads // batch):
            n = len(leaving)
            for copy in arriving[n]:
                copy.wait()
            for k in range(batch):
                h = p * heads + b * batch + k
                start = start_ref[part * heads + b * batch + k]
                result = held_local[h].astype(f32) + product(held_reach[h], start)
                mean = jnp.mean(result * result, axis=1, keepdims=True)
                scaled = result * lax.rsqrt(mean + 1e-06) * gain[...]
                done[:, h * DK : (h + 1) * DK] = scaled.astype(bf16)
            width = batch * DK
            to = pl.ds(pl.multiple_of((part * heads + b * batch) * DK, DK), width)
            leaving.append(
                pltpu.make_async_copy(
                    done.at[:, pl.ds(n * width, width)], out_ref.at[:, to], out_sems.at[n]
                )
            )
            leaving[-1].start()
    for copy in leaving:
        copy.wait()


def finish_stage(first, reads, starts, gain):
    heads, length, _ = reads[0][0].shape
    all_heads = starts.shape[0]
    batch = 2
    return pl.pallas_call(
        functools.partial(finish_kernel, batch),
        in_specs=[SMEM, VMEM, FAR] + [FAR] * (2 * len(reads)),
        out_specs=FAR,
        out_shape=pltpu.HBM((length, all_heads * DK), bf16),
        scratch_shapes=[
            pltpu.VMEM((1, DK), f32),
            pltpu.VMEM((all_heads, length, DK), bf16),
            pltpu.VMEM((all_heads, length, DK), bf16),
            pltpu.VMEM((length, all_heads * DK), bf16),
            pltpu.SemaphoreType.DMA((2, all_heads // batch + 1)),
            pltpu.SemaphoreType.DMA((all_heads // batch,)),
        ],
        compiler_params=pltpu.CompilerParams(vmem_limit_bytes=16 << 20),
        name="finish_stage",
    )(first, near(starts), far(gain.reshape(1, DK)), *(far(a) for read in reads for a in read))


def entering_state(total):
    outer = lax.axis_size("outer")
    if outer == 1:
        return jnp.zeros_like(total[..., :DK])
    if outer == 2:
        return lax.ppermute(total[..., :DK], "outer", [(0, 1)])
    everyone = lax.all_gather(total, "outer", axis=0)
    mine = lax.axis_index("outer")

    def step(i, state):
        piece = lax.dynamic_index_in_dim(everyone, i, 0, keepdims=False)
        moved = piece[..., :DK] + jnp.einsum(
            "hij,hjk->hik", piece[..., DK:], state, precision=lax.Precision.HIGHEST
        )
        return jnp.where(i < mine, moved, state)

    return lax.fori_loop(0, outer - 1, step, jnp.zeros_like(total[..., :DK]))


def per_device(projected, conv_weight, log_gate, write_rate, norm_gain):
    devices = lax.axis_size(ALL)
    parts = lax.axis_size("head")
    route = [(i, i + 1) for i in range(devices - 1)]
    arguments = (projected, log_gate, write_rate, conv_weight)
    if parts == 2:
        first = lax.axis_index("head").astype(jnp.int32).reshape(1)
        tail, mine, theirs = pack_stage(first, (1, 1), parts, *arguments)
        halo = lax.ppermute(tail, ALL, route)
        packs = [mine, lax.ppermute(theirs, "head", [(0, 1), (1, 0)])]
    else:
        first = jnp.zeros((1,), jnp.int32)
        tail, mine = pack_stage(first, (parts,), parts, *arguments)
        halo = lax.ppermute(tail, ALL, route)
        packs = [lax.all_to_all(mine, "head", 0, 0, tiled=True)]
    entries = [(pack, i) for pack in packs for i in range(pack.shape[0])]

    summary, *kept = local_stage(first, parts, projected, halo, packs)
    heads = summary.shape[0]
    members = lax.axis_size(NEAR)
    own = heads // members
    summary = lax.all_to_all(summary, NEAR, 0, 0, tiled=True)
    early = max(1, parts // 2)

    def reading(step):
        return reading_stage(first, step, parts, projected, halo, *entries[step], kept)

    reads = [reading(step) for step in range(early)]
    summary, reads = lax.optimization_barrier((summary, reads))
    *prefix, total = chain_stage(summary.reshape(members, own, DK, 2 * DK))
    starts = entry_stage(*prefix, entering_state(total))
    starts = lax.all_to_all(starts.reshape(heads, DK, DK), NEAR, 0, 0, tiled=True)
    reads += [reading(step) for step in range(early, parts)]
    return finish_stage(first, reads, starts, norm_gain)


def solution(mesh):
    seq, head = mesh.shape["seq"], mesh.shape["head"]
    inner = max(1, 16 // head)
    while seq % inner:
        inner //= 2
    layered = Mesh(mesh.devices.reshape(seq // inner, inner, head), ALL)
    in_specs = (
        P(ALL, None),
        P(None, "head"),
        P("head", ("outer", "inner")),
        P("head", ("outer", "inner")),
        P(),
    )
    return jax.shard_map(
        per_device, mesh=layered, in_specs=in_specs, out_specs=P(ALL, None), check_vma=False
    )
```

time: 93.6 us -> 83.4 us (0.89)
  Pallas kernels: 55.7 us -> 48.8 us
  local copies, waits for them, and re-layouts: 3.71 us -> 0.01 us
    pallas_call x8 -> x7, Pallas kernels: 55.7 us -> 48.8 us  [the longest x1 24.1 us: local_stage(): pl.pallas_call(functools.partial(local_kernel, number, parts, tuple((p.sh...]
    unnamed x8 -> x0, local copies, waits for them, and re-layouts: 2.86 us -> none
  transfers between devices with their start and end apart: 5 -> 5, of which waited for: 4 -> 5; matrix products, arithmetic and copies ran while one was open for 1% -> 0% of each run, Pallas kernels for 32% -> 18%
where the time goes in v3:
time: 83.4 us; the launch traced here: 82.2 us
  Pallas kernels  48.8 us (59%)
  waiting for transfers between devices  19.3 us (23%)
  starting transfers between devices  13.8 us (17%)
    pallas_call x1, Pallas kernels, local_stage(): pl.pallas_call(functools.partial(local_kernel, number, parts, tuple((p.sh...  24.1 us
    pallas_call x2, Pallas kernels, reading_stage(): pl.pallas_call(functools.partial(reading_kernel, number, index), grid_spe...  15 us
    all_to_all x1, waiting for transfers between devices, per_device(): summary = lax.all_to_all(summary, NEAR, 0, 0, tiled=True)  7.31 us
    ppermute x1, waiting for transfers between devices, entering_state(): return lax.ppermute(total[..., :DK], 'outer', [(0, 1)])  5.86 us
    pallas_call x1, Pallas kernels, finish_stage(): pl.pallas_call(functools.partial(finish_kernel, batch), in_specs=[SMEM, V...  5.86 us
    all_to_all x1, starting transfers between devices, per_device(): lax.all_to_all(starts.reshape(heads, DK, DK), NEAR, 0, 0, tiled=True)  5 us
    all_to_all x1, starting transfers between devices, per_device(): summary = lax.all_to_all(summary, NEAR, 0, 0, tiled=True)  4.05 us
    ppermute x1, waiting for transfers between devices, per_device(): halo = lax.ppermute(tail, ALL, route)  3.95 us
  transfers between devices with their start and end apart: 5, of which 5 were waited for; matrix products, arithmetic and copies ran while one was open for 0% of the time, Pallas kernels for 18%

profile of v3, /device:TPU:16, one launch (start us, length us, event | category | flops | bytes accessed | tf_op | source)
XLA Modules:
  0.0 82.2 jit_solution(14335352302851124636)
XLA Ops:
  0.0 0.9 %pack_stage.1 = (bf16[8,4096]{1,0:T(8,128)(2,1)S(1)}, f32[1,128,128]{2,1,0:T(8,128)S(1)}, f32[1,128,128]{2,1,0:T(8,128)S(1)}) custom-call(s32[1]{0:T(128)} %bitcast.first_ref, bf16[512,4096]{1,0:T(8,128)(2,1)} %x_ref.7, f32[8,1024]{1,0:T(8,128)} %gate_ref.1, f32[8,1024]{1,0:T(8,128)} %rate_ref.1, bf16[4,2048]{1,0:T(4,128)(2,1)} %taps_ref.1), custom_call_target="tpu_custom_call" | custom-call | tf_op jit(solution)/shard_map/pack_stage/pallas_call | solution.py:153
  0.9 3.4 %collective-permute-start = (bf16[8,4096]{1,0:T(8,128)(2,1)S(1)}, bf16[8,4096]{1,0:T(8,128)(2,1)S(1)}, u32[]{:S(2)}, u32[]{:S(2)}) collective-permute-start(bf16[8,4096]{1,0:T(8,128)(2,1)S(1)} %get-tuple-element.24), channel_id=1, source_target_pairs={{0,1},{1,2},{2,3},{3,4},{4,5},{5,6},{6,7},{7,8},{8,9},{9,10},{10,1... | collective-permute-start | bytes 196616 | tf_op jit(solution)/shard_map/ppermute | solution.py:605
  4.3 0.1 collective-permute-start.1
  4.4 3.9 %collective-permute-done.halo_ref = bf16[8,4096]{1,0:T(8,128)(2,1)S(1)} collective-permute-done((bf16[8,4096]{1,0:T(8,128)(2,1)S(1)}, bf16[8,4096]{1,0:T(8,128)(2,1)S(1)}, u32[]{:S(2)}, u32[]{:S(2)}) %collective-permute-start) | collective-permute-done | bytes 65568 | tf_op jit(solution)/shard_map/ppermute | solution.py:605
  8.3 0.5 collective-permute-done.1.refs_1_.pack_ref
  8.8 24.1 %local_stage.1 = (bf16[16,128,256]{2,1,0:T(8,128)(2,1)}, bf16[2,4,8,128,256]{4,3,2,1,0:T(8,128)(2,1)}, bf16[2,4,8,128,256]{4,3,2,1,0:T(8,128)(2,1)}, bf16[2,512,512]{2,1,0:T(8,128)(2,1)}, f32[2,4,4,128]{3,2,1,0:T(4,128)S(1)}) custom-call(s32[1]{0:T(128)} %bitcast.first_ref, bf16[512,4096]{1,0:T(8,128)(2,1)} %x_ref.7, ...), custom_call_target="tpu_custom_call" | custom-call | tf_op jit(solution)/shard_map/local_stage/pallas_call | solution.py:329
  32.9 4.0 %all-to-all-start = ((bf16[16,128,256]{2,1,0:T(8,128)(2,1)}), bf16[16,128,256]{2,1,0:T(8,128)(2,1)S(1)}, u32[]{:S(2)}, u32[]{:S(2)}) async-start(bf16[16,128,256]{2,1,0:T(8,128)(2,1)} %get-tuple-element.27), calls=%async_computation | async-start | bytes 2097152 | tf_op jit(solution)/shard_map/all_to_all | solution.py:618
  37.0 7.5 %reading_stage.2 = (bf16[8,512,128]{2,1,0:T(8,128)(2,1)}, bf16[8,512,128]{2,1,0:T(8,128)(2,1)}) custom-call(s32[1]{0:T(128)} %bitcast.first_ref, bf16[512,4096]{1,0:T(8,128)(2,1)} %x_ref.7, bf16[8,4096]{1,0:T(8,128)(2,1)S(1)} %collective-permute-done.halo_ref, f32[1,128,128]{2,1,0:T(8,128)S(1)} %get-tuple-element.25.refs_0_.pack_ref, ...), custom_call_target="tpu_custom_call" | custom-call | tf_op jit(solution)/shard_map/reading_stage/pallas_call | solution.py:406
  44.5 7.3 %all-to-all-done = bf16[16,128,256]{2,1,0:T(8,128)(2,1)S(1)} async-done(((bf16[16,128,256]{2,1,0:T(8,128)(2,1)}), bf16[16,128,256]{2,1,0:T(8,128)(2,1)S(1)}, u32[]{:S(2)}, u32[]{:S(2)}) %all-to-all-start) | async-done | bytes 1048608 | tf_op jit(solution)/shard_map/all_to_all | solution.py:618
  51.8 1.4 %chain_stage.1 = (f32[16,1,128,128]{3,2,1,0:T(8,128)S(1)}, bf16[16,1,128,128]{3,2,1,0:T(8,128)(2,1)S(1)}, f32[4,1,128,256]{3,2,1,0:T(8,128)S(1)}, f32[1,128,256]{2,1,0:T(8,128)S(1)}) custom-call(bf16[16,1,128,256]{3,2,1,0:T(8,128)(2,1)S(1)} %bitcast.4), custom_call_target="tpu_custom_call" | custom-call | tf_op jit(solution)/shard_map/chain_stage/pallas_call | solution.py:462
  53.2 1.3 %collective-permute-start.2 = (f32[1,128,128]{2,1,0:T(8,128)S(1)}, f32[1,128,128]{2,1,0:T(8,128)S(1)}, u32[]{:S(2)}, u32[]{:S(2)}) collective-permute-start(f32[1,128,128]{2,1,0:T(8,128)S(1)} %slice.3), channel_id=1, source_target_pairs={{0,16},{1,17},{2,18},{3,19},{4,20},{5,21},{6,22},{7,23},{8,24},{9,... | collective-permute-start | bytes 196616 | tf_op jit(solution)/shard_map/ppermute | solution.py:583
  54.5 5.9 %collective-permute-done.2.entering_ref = f32[1,128,128]{2,1,0:T(8,128)S(1)} collective-permute-done((f32[1,128,128]{2,1,0:T(8,128)S(1)}, f32[1,128,128]{2,1,0:T(8,128)S(1)}, u32[]{:S(2)}, u32[]{:S(2)}) %collective-permute-start.2) | collective-permute-done | bytes 65568 | tf_op jit(solution)/shard_map/ppermute | solution.py:583
  60.4 1.5 %entry_stage.1 = bf16[16,1,128,128]{3,2,1,0:T(8,128)(2,1)} custom-call(f32[16,1,128,128]{3,2,1,0:T(8,128)S(1)} %get-tuple-element.35.state_ref, bf16[16,1,128,128]{3,2,1,0:T(8,128)(2,1)S(1)} %get-tuple-element.36.loss_ref, f32[4,1,128,256]{3,2,1,0:T(8,128)S(1)} %get-tuple-element.37.sub_ref, f32[1,128,128]{2,1,0:T(8,128)S(1)} %collective-permute-done.2.entering_ref), custom_call_target="tpu_custom_call" | custom-call | tf_op jit(solution)/shard_map/entry_stage/pallas_call | solution.py:495
  62.0 5.0 %all-to-all-start.1 = ((bf16[16,128,128]{2,1,0:T(8,128)(2,1)}), bf16[16,128,128]{2,1,0:T(8,128)(2,1)S(1)}, u32[]{:S(2)}, u32[]{:S(2)}) async-start(bf16[16,128,128]{2,1,0:T(8,128)(2,1)} %bitcast.2), calls=%async_computation.1 | async-start | bytes 1048576 | tf_op jit(solution)/shard_map/all_to_all | solution.py:628
  67.0 7.5 %reading_stage.3 = (bf16[8,512,128]{2,1,0:T(8,128)(2,1)}, bf16[8,512,128]{2,1,0:T(8,128)(2,1)}) custom-call(s32[1]{0:T(128)} %bitcast.first_ref, bf16[512,4096]{1,0:T(8,128)(2,1)} %x_ref.7, bf16[8,4096]{1,0:T(8,128)(2,1)S(1)} %collective-permute-done.halo_ref, f32[1,128,128]{2,1,0:T(8,128)S(1)} %collective-permute-done.1.refs_1_.pack_ref, ...), custom_call_target="tpu_custom_call" | custom-call | tf_op jit(solution)/shard_map/reading_stage/pallas_call | solution.py:406
  74.5 1.7 %all-to-all-done.1.start_ref = bf16[16,128,128]{2,1,0:T(8,128)(2,1)S(1)} async-done(((bf16[16,128,128]{2,1,0:T(8,128)(2,1)}), bf16[16,128,128]{2,1,0:T(8,128)(2,1)S(1)}, u32[]{:S(2)}, u32[]{:S(2)}) %all-to-all-start.1) | async-done | bytes 524320 | tf_op jit(solution)/shard_map/all_to_all | solution.py:628
  76.1 5.9 %finish_stage.1 = bf16[512,2048]{1,0:T(8,128)(2,1)} custom-call(s32[1]{0:T(128)} %bitcast.first_ref, bf16[16,128,128]{2,1,0:T(8,128)(2,1)S(1)} %all-to-all-done.1.start_ref, f32[1,128]{1,0:T(1,128)} %bitcast.5, bf16[8,512,128]{2,1,0:T(8,128)(2,1)} %get-tuple-element.39.refs_0_, bf16[8,512,128]{2,1,0:T(8,128)(2,1)} %get-tuple-element.40.refs_1_, ...), custom_call_target="tpu_custom_call" | custom-call | tf_op jit(solution)/shard_map/finish_stage/pallas_call | solution.py:560
  (1 shorter events, 0.0 us)
Async XLA Ops:
  0.9 7.4 %collective-permute-start = (bf16[8,4096]{1,0:T(8,128)(2,1)S(1)}, bf16[8,4096]{1,0:T(8,128)(2,1)S(1)}, u32[]{:S(2)}, u32[]{:S(2)}) collective-permute-start(bf16[8,4096]{1,0:T(8,128)(2,1)S(1)} %get-tuple-element.24), channel_id=1, source_target_pairs={{0,1},{1,2},{2,3},{3,4},{4,5},{5,6},{6,7},{7,8},{8,9},{9,10},{10,1... | collective-permute-start | bytes 196616 | tf_op jit(solution)/shard_map/ppermute | solution.py:605
  4.3 4.5 %collective-permute-start.1 = (f32[1,128,128]{2,1,0:T(8,128)S(1)}, f32[1,128,128]{2,1,0:T(8,128)S(1)}, u32[]{:S(2)}, u32[]{:S(2)}) collective-permute-start(f32[1,128,128]{2,1,0:T(8,128)S(1)} %get-tuple-element.26), channel_id=1, source_target_pairs={{0,1},{1,0},{2,3},{3,2},{4,5},{5,4},{6,7},{7,6},{8,9},{9,8},{10,11... | collective-permute-start | bytes 196616 | tf_op jit(solution)/shard_map/ppermute | solution.py:606
  32.9 18.9 %all-to-all-start = ((bf16[16,128,256]{2,1,0:T(8,128)(2,1)}), bf16[16,128,256]{2,1,0:T(8,128)(2,1)S(1)}, u32[]{:S(2)}, u32[]{:S(2)}) async-start(bf16[16,128,256]{2,1,0:T(8,128)(2,1)} %get-tuple-element.27), calls=%async_computation | async-start | bytes 2097152 | tf_op jit(solution)/shard_map/all_to_all | solution.py:618
  53.2 7.2 %collective-permute-start.2 = (f32[1,128,128]{2,1,0:T(8,128)S(1)}, f32[1,128,128]{2,1,0:T(8,128)S(1)}, u32[]{:S(2)}, u32[]{:S(2)}) collective-permute-start(f32[1,128,128]{2,1,0:T(8,128)S(1)} %slice.3), channel_id=1, source_target_pairs={{0,16},{1,17},{2,18},{3,19},{4,20},{5,21},{6,22},{7,23},{8,24},{9,... | collective-permute-start | bytes 196616 | tf_op jit(solution)/shard_map/ppermute | solution.py:583
  62.0 14.2 %all-to-all-start.1 = ((bf16[16,128,128]{2,1,0:T(8,128)(2,1)}), bf16[16,128,128]{2,1,0:T(8,128)(2,1)S(1)}, u32[]{:S(2)}, u32[]{:S(2)}) async-start(bf16[16,128,128]{2,1,0:T(8,128)(2,1)} %bitcast.2), calls=%async_computation.1 | async-start | bytes 1048576 | tf_op jit(solution)/shard_map/all_to_all | solution.py:628

commit v4 on v3

--- a/solution.py
+++ b/solution.py
@@ -23,6 +23,7 @@
 bf16 = jnp.bfloat16
 
 
+LOG2E = 1.4426950408889634
 VMEM = pl.BlockSpec(memory_space=pltpu.VMEM)
 SMEM = pl.BlockSpec(memory_space=pltpu.SMEM)
 FAR = pl.BlockSpec(memory_space=pltpu.HBM)
@@ -83,13 +84,20 @@
         for b in range(1, blocks):
             piece = jnp.where(owner == b, lower[unit][b * BASE : (b + 1) * BASE], piece)
         packed.append(piece)
-    packed = jnp.concatenate(packed, axis=0)
-    group_start = (lax.broadcasted_iota(jnp.int32, packed.shape, 1) // BASE) * BASE
+    half = BASE // 2
+    upper = jnp.concatenate([piece[:half] for piece in packed], axis=0)
+    under = jnp.concatenate([piece[half:] for piece in packed], axis=0)
+    group_start = (lax.broadcasted_iota(jnp.int32, upper.shape, 1) // BASE) * BASE
     start = jnp.where(small_lane % BASE == small_row, 1.0, 0.0).astype(f32)
-    solved = jnp.broadcast_to(start[None], (units, BASE, STRETCH))
+    shape = (units, half, STRETCH)
+    top = jnp.broadcast_to(start[None, :half], shape)
+    bottom = jnp.broadcast_to(start[None, half:], shape)
     for j in range(BASE - 1):
-        spread_col = jnp.take_along_axis(packed, group_start + j, axis=1)
-        solved = solved - spread_col.reshape(units, BASE, STRETCH) * solved[:, j : j + 1, :]
+        pivot = top[:, j : j + 1, :] if j < half else bottom[:, j - half : j - half + 1, :]
+        if j < half - 1:
+            top = top - jnp.take_along_axis(upper, group_start + j, axis=1).reshape(shape) * pivot
+        bottom = bottom - jnp.take_along_axis(under, group_start + j, axis=1).reshape(shape) * pivot
+    solved = [jnp.concatenate([top[unit], bottom[unit]], axis=0) for unit in range(units)]
 
     rows = [
         [jnp.where(owner == b, solved[unit], 0.0) for b in range(blocks)] for unit in range(units)
@@ -168,64 +176,12 @@
     )(first, far(projected), far(log_gate), far(write_rate), far(conv_weight))
 
 
-def local_kernel(number, parts, stacks, first_ref, x_ref, halo_ref, *refs):
-    pack_refs, refs = refs[: len(stacks)], refs[len(stacks) :]
-    summary_out, written_out, joint_out, key_out, norm_ref = refs[:5]
-    pack, blocks, ext, summaries, writtens, joints, keys_held, in_sems, out_sems = refs[5:]
-    step = pl.program_id(0)
-    slot = lax.rem(step, 2)
-    part = part_at(first_ref[0], step, parts)
+def local_body(number, part, halo_ref, pack, block, ext, kept, norm_ref, arrived, ready):
+    key_ref, summary_ref, written_ref, joint_ref = kept
     key_heads = norm_ref.shape[1]
     width = key_heads * GROUP_CHANNELS
     heads = key_heads * V_GROUP
     units = heads * number
-    block, summary_ref, written_ref = blocks.at[slot], summaries.at[slot], writtens.at[slot]
-    joint_ref, key_ref = joints.at[slot], keys_held.at[slot]
-
-    def arriving(at):
-        here = lax.rem(at, 2)
-        base = part_at(first_ref[0], at, parts) * width
-        used = (SEGMENTS - 1) * DK
-        copies = []
-        for g in range(key_heads):
-            source = pl.ds(pl.multiple_of(base + (g * SEGMENTS + 1) * DK, DK), used)
-            target = pl.ds((g * SEGMENTS + 1) * DK, used)
-            copies.append(
-                pltpu.make_async_copy(
-                    x_ref.at[:, source], blocks.at[here, :, target], in_sems.at[here, g]
-                )
-            )
-        return copies
-
-    def leaving(at):
-        here = lax.rem(at, 2)
-        place = pl.ds(part_at(first_ref[0], at, parts) * heads, heads)
-        pairs = [(keys_held.at[here], key_out.at[at]), (summaries.at[here], summary_out.at[place])]
-        pairs += [(writtens.at[here, c], written_out.at[at, c]) for c in range(number)]
-        pairs += [(joints.at[here, c - 1], joint_out.at[at, c]) for c in range(1, number)]
-        return [
-            pltpu.make_async_copy(source, target, out_sems.at[here, i])
-            for i, (source, target) in enumerate(pairs)
-        ]
-
-    @pl.when(step == 0)
-    def _():
-        for copy in arriving(step):
-            copy.start()
-
-    @pl.when(step + 1 < pl.num_programs(0))
-    def _():
-        for copy in arriving(step + 1):
-            copy.start()
-
-    coming, going = arriving(step), leaving(step)
-    entries = [(ref, i) for ref in pack_refs for i in range(ref.shape[0])]
-    for n, (ref, i) in enumerate(entries):
-
-        @pl.when(step == n)
-        def _():
-            pack[...] = ref[i]
-
     row, col = square_iotas()
     below = row > col
     eye = jnp.where(row == col, 1.0, 0.0).astype(f32)
@@ -234,7 +190,8 @@
     cumulative = running_sum(pack[0:units])
     grown = jnp.exp(cumulative)
     tail = jnp.exp(cumulative[:, STRETCH - 1 : STRETCH] - cumulative)
-    columns = jnp.transpose(jnp.concatenate([cumulative, rates], axis=0), (1, 0))
+    bits = cumulative * LOG2E
+    columns = jnp.transpose(bits + jnp.log2(rates), (1, 0))
     where = [(c, g) for g in range(key_heads) for c in range(number)]
 
     def units_of(c, g):
@@ -252,23 +209,22 @@
     keys, inverses, lower = {}, {}, [None] * units
     for c, g in where:
         if c == 0:
-            coming[g].wait()
+            arrived(g)
         k = channels(c, g, 1)
         keys[c, g] = k
         key_ref[c * STRETCH : (c + 1) * STRETCH, g * DK : (g + 1) * DK] = k
         gram = lax.dot_general(k, k, (((1,), (1,)), ((), ())), preferred_element_type=f32)
         diagonal = gram * eye
-        inverse_row = lax.rsqrt(jnp.sum(diagonal, axis=0, keepdims=True) + 1e-06)
-        inverse_col = lax.rsqrt(jnp.sum(diagonal, axis=1, keepdims=True) + 1e-06)
-        inverses[c, g] = inverse_row
-        norm_ref[0, g, c : c + 1] = inverse_row
-        gram = gram * inverse_row
+        sum_row = jnp.sum(diagonal, axis=0, keepdims=True) + 1e-06
+        sum_col = jnp.sum(diagonal, axis=1, keepdims=True) + 1e-06
+        inverses[c, g] = lax.rsqrt(sum_row)
+        log_row, log_col = -0.5 * jnp.log2(sum_row), -0.5 * jnp.log2(sum_col)
+        norm_ref[0, g, c : c + 1] = log_row
         for j, unit in units_of(c, g):
-            spread = columns[:, unit : unit + 1] - cumulative[unit : unit + 1]
-            decay = jnp.exp(jnp.where(below, spread, -1e30))
-            lower[unit] = gram * decay * (columns[:, units + unit : units + unit + 1] * inverse_col)
-
-    going[0].start()
+            spread = (columns[:, unit : unit + 1] + log_col) - (bits[unit : unit + 1] - log_row)
+            lower[unit] = gram * jnp.exp2(jnp.where(below, spread, -1e30))
+
+    ready(0)
     solved = block_inverses(lower)
 
     fresh, carried, scaled = [None] * units, [None] * units, [None] * units
@@ -299,13 +255,137 @@
             written_ref[c, head] = written
             decay = grown[unit : unit + 1, STRETCH - 1 : STRETCH]
             joint[head] = joint[head] * decay + product(scaled[unit], written)
-        going[2 + c].start()
+        ready(2 + c)
         if c > 0:
-            going[1 + number + c].start()
+            ready(1 + number + c)
     for head in range(heads):
         summary_ref[head, :, :DK] = joint[head][:, :DK].astype(bf16)
         summary_ref[head, :, DK:] = (joint[head][:, DK:] - eye).astype(bf16)
-    going[1].start()
+    ready(1)
+
+
+def channel_copies(base, key_heads, x_ref, block, sems):
+    used = (SEGMENTS - 1) * DK
+    copies = []
+    for g in range(key_heads):
+        source = pl.ds(pl.multiple_of(base + (g * SEGMENTS + 1) * DK, DK), used)
+        target = pl.ds((g * SEGMENTS + 1) * DK, used)
+        copies.append(
+            pltpu.make_async_copy(x_ref.at[:, source], block.at[:, target], sems.at[g])
+        )
+    return copies
+
+
+def kept_copies(number, step, place, kept, outs, sems):
+    key_ref, summary_ref, written_ref, joint_ref = kept
+    pairs = [(key_ref, outs[3].at[step]), (summary_ref, outs[0].at[place])]
+    pairs += [(written_ref.at[c], outs[1].at[step, c]) for c in range(number)]
+    pairs += [(joint_ref.at[c - 1], outs[2].at[step, c]) for c in range(1, number)]
+    return [
+        pltpu.make_async_copy(source, target, sems.at[i]) for i, (source, target) in enumerate(pairs)
+    ]
+
+
+def first_kernel(number, parts, first_ref, x_ref, halo_ref, pack_ref, *refs):
+    kept, (norm_ref, other, block, ext, sems, other_sems) = refs[:4], refs[4:]
+    key_heads = norm_ref.shape[1]
+    width = key_heads * GROUP_CHANNELS
+    part, next_part = part_at(first_ref[0], 0, parts), part_at(first_ref[0], 1, parts)
+    coming = channel_copies(part * width, key_heads, x_ref, block, sems)
+    others = channel_copies(next_part * width, key_heads, x_ref, other, other_sems)
+    for copy in coming + others:
+        copy.start()
+    local_body(
+        number,
+        part,
+        halo_ref,
+        pack_ref.at[0],
+        block,
+        ext,
+        kept,
+        norm_ref,
+        lambda g: coming[g].wait(),
+        lambda i: None,
+    )
+    for copy in others:
+        copy.wait()
+
+
+def second_kernel(number, parts, first_ref, halo_ref, pack_ref, block, *refs):
+    before, outs, norm_ref, (ext, *kept, before_sems, sems) = refs[:4], refs[4:8], refs[8], refs[9:]
+    heads = norm_ref.shape[1] * V_GROUP
+    old, part = part_at(first_ref[0], 0, parts), part_at(first_ref[0], 1, parts)
+    leaving = kept_copies(number, 0, pl.ds(old * heads, heads), before, outs, before_sems)
+    for copy in leaving:
+        copy.start()
+    going = kept_copies(number, 1, pl.ds(part * heads, heads), kept, outs, sems)
+    local_body(
+        number,
+        part,
+        halo_ref,
+        pack_ref.at[0],
+        block,
+        ext,
+        kept,
+        norm_ref,
+        lambda g: None,
+        lambda i: going[i].start(),
+    )
+    for copy in leaving + going:
+        copy.wait()
+
+
+def local_kernel(number, parts, stacks, first_ref, x_ref, halo_ref, *refs):
+    pack_refs, refs = refs[: len(stacks)], refs[len(stacks) :]
+    outs, norm_ref = refs[:4], refs[4]
+    pack, blocks, ext, *held, in_sems, out_sems = refs[5:]
+    step = pl.program_id(0)
+    key_heads = norm_ref.shape[1]
+    width = key_heads * GROUP_CHANNELS
+    heads = key_heads * V_GROUP
+
+    def arriving(at):
+        here = lax.rem(at, 2)
+        base = part_at(first_ref[0], at, parts) * width
+        return channel_copies(base, key_heads, x_ref, blocks.at[here], in_sems.at[here])
+
+    def leaving(at):
+        here = lax.rem(at, 2)
+        place = pl.ds(part_at(first_ref[0], at, parts) * heads, heads)
+        kept = [ref.at[here] for ref in held]
+        return kept_copies(number, at, place, kept, outs, out_sems.at[here])
+
+    @pl.when(step == 0)
+    def _():
+        for copy in arriving(step):
+            copy.start()
+
+    @pl.when(step + 1 < pl.num_programs(0))
+    def _():
+        for copy in arriving(step + 1):
+            copy.start()
+
+    coming, going = arriving(step), leaving(step)
+    entries = [(ref, i) for ref in pack_refs for i in range(ref.shape[0])]
+    for n, (ref, i) in enumerate(entries):
+
+        @pl.when(step == n)
+        def _():
+            pack[...] = ref[i]
+
+    slot = lax.rem(step, 2)
+    local_body(
+        number,
+        part_at(first_ref[0], step, parts),
+        halo_ref,
+        pack,
+        blocks.at[slot],
+        ext,
+        [ref.at[slot] for ref in held],
+        norm_ref,
+        lambda g: coming[g].wait(),
+        lambda i: going[i].start(),
+    )
 
     @pl.when(step > 0)
     def _():
@@ -316,6 +396,25 @@
     def _():
         for copy in going:
             copy.wait()
+
+
+def kept_scratch(number, heads, length):
+    return [
+        ((length, heads // V_GROUP * DK), bf16),
+        ((heads, DK, 2 * DK), bf16),
+        ((number, heads, STRETCH, 2 * DK), bf16),
+        ((max(1, number - 1), heads, STRETCH, 2 * DK), bf16),
+    ]
+
+
+def kept_arrays(parts, number, heads, length):
+    per_unit = (parts, number, heads, STRETCH, 2 * DK)
+    return [
+        pltpu.HBM((heads * parts, DK, 2 * DK), bf16),
+        pltpu.HBM(per_unit, bf16),
+        pltpu.HBM(per_unit, bf16),
+        pltpu.HBM((parts, length, heads // V_GROUP * DK), bf16),
+    ]
 
 
 def local_stage(first, parts, projected, halo, packs):
@@ -324,35 +423,57 @@
     width = channels // parts
     key_heads = width // GROUP_CHANNELS
     heads = key_heads * V_GROUP
-    per_unit = (number, heads, STRETCH, 2 * DK)
-    later = (max(1, number - 1), heads, STRETCH, 2 * DK)
-    return pl.pallas_call(
+    scratch = kept_scratch(number, heads, length)
+    kept = kept_arrays(parts, number, heads, length)
+    norms = (1, key_heads, number, STRETCH)
+    ext = pltpu.VMEM((HALO + length, width), f32)
+    results = 2 * number + 1
+    if len(packs) == 2:
+        *before, norm, block = pl.pallas_call(
+            functools.partial(first_kernel, number, parts),
+            in_specs=[SMEM, FAR, VMEM, VMEM],
+            out_specs=[VMEM] * 6,
+            out_shape=[pltpu.VMEM(*shape) for shape in scratch]
+            + [pltpu.VMEM(norms, f32), pltpu.VMEM((length, width), bf16)],
+            scratch_shapes=[
+                pltpu.VMEM((length, width), bf16),
+                ext,
+                pltpu.SemaphoreType.DMA((key_heads,)),
+                pltpu.SemaphoreType.DMA((key_heads,)),
+            ],
+            compiler_params=pltpu.CompilerParams(vmem_limit_bytes=24 << 20),
+            name="first_stage",
+        )(first, far(projected), near(halo), near(packs[0]))
+        *made, other_norm = pl.pallas_call(
+            functools.partial(second_kernel, number, parts),
+            in_specs=[SMEM] + [VMEM] * 7,
+            out_specs=[FAR] * 4 + [VMEM],
+            out_shape=kept + [pltpu.VMEM(norms, f32)],
+            scratch_shapes=[ext]
+            + [pltpu.VMEM(*shape) for shape in scratch]
+            + [pltpu.SemaphoreType.DMA((results,))] * 2,
+            compiler_params=pltpu.CompilerParams(vmem_limit_bytes=24 << 20),
+            name="second_stage",
+        )(first, near(halo), near(packs[1]), block, *before)
+        return *made, [(norm, 0), (other_norm, 0)]
+    *made, norm = pl.pallas_call(
         functools.partial(local_kernel, number, parts, tuple(p.shape[0] for p in packs)),
         grid=(parts,),
         in_specs=[SMEM, FAR] + [VMEM] * (1 + len(packs)),
-        out_specs=[FAR] * 4
-        + [pl.BlockSpec((1, key_heads, number, STRETCH), lambda p: (p, 0, 0, 0))],
-        out_shape=[
-            pltpu.HBM((heads * parts, DK, 2 * DK), bf16),
-            pltpu.HBM((parts,) + per_unit, bf16),
-            pltpu.HBM((parts,) + per_unit, bf16),
-            pltpu.HBM((parts, length, key_heads * DK), bf16),
-            jax.ShapeDtypeStruct((parts, key_heads, number, STRETCH), f32),
-        ],
+        out_specs=[FAR] * 4 + [pl.BlockSpec(norms, lambda p: (p, 0, 0, 0))],
+        out_shape=kept + [jax.ShapeDtypeStruct((parts,) + norms[1:], f32)],
         scratch_shapes=[
             pltpu.VMEM(packs[0].shape[1:], f32),
             pltpu.VMEM((2, length, width), bf16),
-            pltpu.VMEM((HALO + length, width), f32),
-            pltpu.VMEM((2, heads, DK, 2 * DK), bf16),
-            pltpu.VMEM((2,) + per_unit, bf16),
-            pltpu.VMEM((2,) + later, bf16),
-            pltpu.VMEM((2, length, key_heads * DK), bf16),
+            ext,
+            *(pltpu.VMEM((2,) + shape, dtype) for shape, dtype in scratch),
             pltpu.SemaphoreType.DMA((2, key_heads)),
-            pltpu.SemaphoreType.DMA((2, 2 * number + 1)),
+            pltpu.SemaphoreType.DMA((2, results)),
         ],
         compiler_params=pltpu.CompilerParams(vmem_limit_bytes=44 << 20),
         name="local_stage",
     )(first, far(projected), near(halo), *(near(p) for p in packs))
+    return *made, [(norm, p) for p in range(parts)]
 
 
 def reading_kernel(number, index, first_ref, x_ref, halo_ref, pack_ref, *refs):
@@ -366,7 +487,8 @@
         pack_ref[index, pl.ds(c * heads + g * V_GROUP, V_GROUP)] for c in range(number)
     ]
     cumulative = running_sum(jnp.concatenate(gates, axis=0))
-    columns = jnp.transpose(cumulative, (1, 0))
+    bits = cumulative * LOG2E
+    columns = jnp.transpose(bits, (1, 0))
     ext[0:HALO] = halo_ref[...].astype(f32)
     ext[HALO:] = x_ref[...].astype(f32)
     taps = pack_ref[index, pl.ds(2 * units + g * SEGMENTS * KW, KW)]
@@ -376,13 +498,14 @@
         gram = lax.dot_general(
             query, key_ref[0, rows], (((1,), (1,)), ((), ())), preferred_element_type=f32
         )
-        gram = gram * norm_ref[0, pl.ds(g, 1), c]
+        log_row = norm_ref[0, pl.ds(g, 1), c]
         for j in range(V_GROUP):
             unit = c * V_GROUP + j
             sum_here = columns[:, unit : unit + 1]
-            decay = jnp.exp(jnp.where(inside, sum_here - cumulative[unit : unit + 1], -1e30))
+            spread = sum_here - (bits[unit : unit + 1] - log_row)
+            decay = jnp.exp2(jnp.where(inside, spread, -1e30))
             result = product((gram * decay).astype(bf16), written_ref[0, c, j])
-            grown = jnp.exp(sum_here)
+            grown = jnp.exp2(sum_here)
             if c == 0:
                 reached = result[:, DK:] + grown * query.astype(f32)
             else:
@@ -398,6 +521,7 @@
     key_heads = channels // parts // GROUP_CHANNELS
     heads = key_heads * V_GROUP
     written, joints, keys, norms = kept
+    norm, norm_at = norms[step]
     query = lambda g, first: (0, (part_at(first[0], step, parts) * key_heads + g) * SEGMENTS)
     per_unit = pl.BlockSpec(
         (1, number, V_GROUP, STRETCH, 2 * DK), lambda g, first: (step, 0, g, 0, 0)
@@ -415,7 +539,7 @@
                 per_unit,
                 per_unit,
                 pl.BlockSpec((1, length, DK), lambda g, first: (step, 0, g)),
-                pl.BlockSpec((1,) + norms.shape[1:], lambda g, first: (step, 0, 0, 0)),
+                pl.BlockSpec((1,) + norm.shape[1:], lambda g, first: (norm_at, 0, 0, 0)),
             ],
             out_specs=[per_head, per_head],
             scratch_shapes=[pltpu.VMEM((HALO + length, DK), f32)],
@@ -423,7 +547,7 @@
         out_shape=[pltpu.HBM((heads, length, DK), bf16)] * 2,
         compiler_params=pltpu.CompilerParams(vmem_limit_bytes=12 << 20),
         name="reading_stage",
-    )(first, far(projected), halo, packs, far(written), far(joints), far(keys), norms)
+    )(first, far(projected), halo, packs, far(written), far(joints), far(keys), norm)
 
 
 def advance(joint, loss, gain):
@@ -508,6 +632,8 @@
     parts = len(reads) // 2
     heads = reads[0].shape[0]
     arriving, leaving = [], []
+    gain_copy = pltpu.make_async_copy(gain_ref, gain, in_sems.at[0, out_sems.shape[0]])
+    gain_copy.start()
     for p in range(parts):
         for b in range(heads // batch):
             at = pl.ds(b * batch, batch)
@@ -525,8 +651,6 @@
             )
             for copy in arriving[-1]:
                 copy.start()
-    gain_copy = pltpu.make_async_copy(gain_ref, gain, in_sems.at[0, len(arriving)])
-    gain_copy.start()
     gain_copy.wait()
     for p in range(parts):
         part = part_at(first_ref[0], p, parts)

time: 83.4 us -> 80.8 us (0.969)
  Pallas kernels: 48.8 us -> 47 us
    pallas_call x1 -> x2, Pallas kernels: 24.1 us -> 23 us  [the longest x1 12 us: local_stage(): pl.pallas_call(functools.partial(second_kernel, number, parts), in_specs=...]
    pallas_call x1, Pallas kernels: 5.86 us -> 5 us  [finish_stage(): pl.pallas_call(functools.partial(finish_kernel, batch), in_specs=[SMEM, V...]
  transfers between devices with their start and end apart: 5 -> 5, of which waited for: 5 -> 4; matrix products, arithmetic and copies ran while one was open for 0% -> 0% of each run, Pallas kernels for 18% -> 33%
where the time goes in v4:
time: 80.8 us; the launch traced here: 79.6 us
  Pallas kernels  47 us (58%)
  waiting for transfers between devices  18.8 us (23%)
  starting transfers between devices  13.6 us (17%)
    pallas_call x2, Pallas kernels, reading_stage(): pl.pallas_call(functools.partial(reading_kernel, number, index), grid_spe...  15 us
    pallas_call x1, Pallas kernels, local_stage(): pl.pallas_call(functools.partial(second_kernel, number, parts), in_specs=...  12 us
    pallas_call x1, Pallas kernels, local_stage(): pl.pallas_call(functools.partial(first_kernel, number, parts), in_specs=[...  11.1 us
    all_to_all x1, waiting for transfers between devices, per_device(): summary = lax.all_to_all(summary, NEAR, 0, 0, tiled=True)  7.3 us
    ppermute x1, waiting for transfers between devices, entering_state(): return lax.ppermute(total[..., :DK], 'outer', [(0, 1)])  5.86 us
    all_to_all x1, starting transfers between devices, per_device(): lax.all_to_all(starts.reshape(heads, DK, DK), NEAR, 0, 0, tiled=True)  5.01 us
    pallas_call x1, Pallas kernels, finish_stage(): pl.pallas_call(functools.partial(finish_kernel, batch), in_specs=[SMEM, V...  5 us
    ppermute x1, waiting for transfers between devices, per_device(): halo = lax.ppermute(tail, ALL, route)  3.95 us
  transfers between devices with their start and end apart: 5, of which 4 were waited for; matrix products, arithmetic and copies ran while one was open for 0% of the time, Pallas kernels for 33%

profile of v4, /device:TPU:16, one launch (start us, length us, event | category | flops | bytes accessed | tf_op | source)
XLA Modules:
  0.0 79.6 jit_solution(12757189665816216754)
XLA Ops:
  0.0 0.9 %pack_stage.1 = (bf16[8,4096]{1,0:T(8,128)(2,1)S(1)}, f32[1,128,128]{2,1,0:T(8,128)S(1)}, f32[1,128,128]{2,1,0:T(8,128)S(1)}) custom-call(s32[1]{0:T(128)} %bitcast.first_ref, bf16[512,4096]{1,0:T(8,128)(2,1)} %x_ref.7, f32[8,1024]{1,0:T(8,128)} %gate_ref.1, f32[8,1024]{1,0:T(8,128)} %rate_ref.1, bf16[4,2048]{1,0:T(4,128)(2,1)} %taps_ref.1), custom_call_target="tpu_custom_call" | custom-call | tf_op jit(solution)/shard_map/pack_stage/pallas_call | solution.py:161
  0.9 3.4 %collective-permute-start = (bf16[8,4096]{1,0:T(8,128)(2,1)S(1)}, bf16[8,4096]{1,0:T(8,128)(2,1)S(1)}, u32[]{:S(2)}, u32[]{:S(2)}) collective-permute-start(bf16[8,4096]{1,0:T(8,128)(2,1)S(1)} %get-tuple-element.30), channel_id=1, source_target_pairs={{0,1},{1,2},{2,3},{3,4},{4,5},{5,6},{6,7},{7,8},{8,9},{9,10},{10,1... | collective-permute-start | bytes 196616 | tf_op jit(solution)/shard_map/ppermute | solution.py:729
  4.3 0.1 collective-permute-start.1
  4.4 3.9 %collective-permute-done.halo_ref = bf16[8,4096]{1,0:T(8,128)(2,1)S(1)} collective-permute-done((bf16[8,4096]{1,0:T(8,128)(2,1)S(1)}, bf16[8,4096]{1,0:T(8,128)(2,1)S(1)}, u32[]{:S(2)}, u32[]{:S(2)}) %collective-permute-start) | collective-permute-done | bytes 65568 | tf_op jit(solution)/shard_map/ppermute | solution.py:729
  8.3 11.1 %first_stage.1 = (bf16[512,512]{1,0:T(8,128)(2,1)S(1)}, bf16[8,128,256]{2,1,0:T(8,128)(2,1)S(1)}, bf16[4,8,128,256]{3,2,1,0:T(8,128)(2,1)S(1)}, bf16[3,8,128,256...) custom-call(s32[1]{0:T(128)} %bitcast.first_ref, bf16[512,4096]{1,0:T(8,128)(2,1)} %x_ref.7, ...), custom_call_target="tpu_custom_call" | custom-call | tf_op jit(solution)/shard_map/first_stage/pallas_call | solution.py:432
  19.4 0.0 collective-permute-done.1.pack_ref
  19.4 12.0 %second_stage.1 = (bf16[16,128,256]{2,1,0:T(8,128)(2,1)}, bf16[2,4,8,128,256]{4,3,2,1,0:T(8,128)(2,1)}, bf16[2,4,8,128,256]{4,3,2,1,0:T(8,128)(2,1)}, bf16[2,512,512]{2,1,0:T(8,128)(2,1)}, f32[1,4,4,128]{3,2,1,0:T(4,128)S(1)}) custom-call(s32[1]{0:T(128)} %bitcast.first_ref, bf16[8,4096]{1,0:T(8,128)(2,1)S(1)} %collective-permute-done.halo_ref, ...), custom_call_target="tpu_custom_call" | custom-call | tf_op jit(solution)/shard_map/second_stage/pallas_call | solution.py:447
  31.4 3.8 %all-to-all-start = ((bf16[16,128,256]{2,1,0:T(8,128)(2,1)}), bf16[16,128,256]{2,1,0:T(8,128)(2,1)S(1)}, u32[]{:S(2)}, u32[]{:S(2)}) async-start(bf16[16,128,256]{2,1,0:T(8,128)(2,1)} %get-tuple-element.38), calls=%async_computation | async-start | bytes 2097152 | tf_op jit(solution)/shard_map/all_to_all | solution.py:742
  35.3 7.5 %reading_stage.2 = (bf16[8,512,128]{2,1,0:T(8,128)(2,1)}, bf16[8,512,128]{2,1,0:T(8,128)(2,1)}) custom-call(s32[1]{0:T(128)} %bitcast.first_ref, bf16[512,4096]{1,0:T(8,128)(2,1)} %x_ref.7, bf16[8,4096]{1,0:T(8,128)(2,1)S(1)} %collective-permute-done.halo_ref, f32[1,128,128]{2,1,0:T(8,128)S(1)} %get-tuple-element.32.pack_ref, ...), custom_call_target="tpu_custom_call" | custom-call | tf_op jit(solution)/shard_map/reading_stage/pallas_call | solution.py:530
  42.8 7.3 %all-to-all-done = bf16[16,128,256]{2,1,0:T(8,128)(2,1)S(1)} async-done(((bf16[16,128,256]{2,1,0:T(8,128)(2,1)}), bf16[16,128,256]{2,1,0:T(8,128)(2,1)S(1)}, u32[]{:S(2)}, u32[]{:S(2)}) %all-to-all-start) | async-done | bytes 1048608 | tf_op jit(solution)/shard_map/all_to_all | solution.py:742
  50.1 1.4 %chain_stage.1 = (f32[16,1,128,128]{3,2,1,0:T(8,128)S(1)}, bf16[16,1,128,128]{3,2,1,0:T(8,128)(2,1)S(1)}, f32[4,1,128,256]{3,2,1,0:T(8,128)S(1)}, f32[1,128,256]{2,1,0:T(8,128)S(1)}) custom-call(bf16[16,1,128,256]{3,2,1,0:T(8,128)(2,1)S(1)} %bitcast.4), custom_call_target="tpu_custom_call" | custom-call | tf_op jit(solution)/shard_map/chain_stage/pallas_call | solution.py:586
  51.5 1.3 %collective-permute-start.2 = (f32[1,128,128]{2,1,0:T(8,128)S(1)}, f32[1,128,128]{2,1,0:T(8,128)S(1)}, u32[]{:S(2)}, u32[]{:S(2)}) collective-permute-start(f32[1,128,128]{2,1,0:T(8,128)S(1)} %slice.3), channel_id=1, source_target_pairs={{0,16},{1,17},{2,18},{3,19},{4,20},{5,21},{6,22},{7,23},{8,24},{9,... | collective-permute-start | bytes 196616 | tf_op jit(solution)/shard_map/ppermute | solution.py:707
  52.8 5.9 %collective-permute-done.2.entering_ref = f32[1,128,128]{2,1,0:T(8,128)S(1)} collective-permute-done((f32[1,128,128]{2,1,0:T(8,128)S(1)}, f32[1,128,128]{2,1,0:T(8,128)S(1)}, u32[]{:S(2)}, u32[]{:S(2)}) %collective-permute-start.2) | collective-permute-done | bytes 65568 | tf_op jit(solution)/shard_map/ppermute | solution.py:707
  58.7 1.5 %entry_stage.1 = bf16[16,1,128,128]{3,2,1,0:T(8,128)(2,1)} custom-call(f32[16,1,128,128]{3,2,1,0:T(8,128)S(1)} %get-tuple-element.46.state_ref, bf16[16,1,128,128]{3,2,1,0:T(8,128)(2,1)S(1)} %get-tuple-element.47.loss_ref, f32[4,1,128,256]{3,2,1,0:T(8,128)S(1)} %get-tuple-element.48.sub_ref, f32[1,128,128]{2,1,0:T(8,128)S(1)} %collective-permute-done.2.entering_ref), custom_call_target="tpu_custom_call" | custom-call | tf_op jit(solution)/shard_map/entry_stage/pallas_call | solution.py:619
  60.2 5.0 %all-to-all-start.1 = ((bf16[16,128,128]{2,1,0:T(8,128)(2,1)}), bf16[16,128,128]{2,1,0:T(8,128)(2,1)S(1)}, u32[]{:S(2)}, u32[]{:S(2)}) async-start(bf16[16,128,128]{2,1,0:T(8,128)(2,1)} %bitcast.2), calls=%async_computation.1 | async-start | bytes 1048576 | tf_op jit(solution)/shard_map/all_to_all | solution.py:752
  65.3 7.5 %reading_stage.3 = (bf16[8,512,128]{2,1,0:T(8,128)(2,1)}, bf16[8,512,128]{2,1,0:T(8,128)(2,1)}) custom-call(s32[1]{0:T(128)} %bitcast.first_ref, bf16[512,4096]{1,0:T(8,128)(2,1)} %x_ref.7, bf16[8,4096]{1,0:T(8,128)(2,1)S(1)} %collective-permute-done.halo_ref, f32[1,128,128]{2,1,0:T(8,128)S(1)} %collective-permute-done.1.pack_ref, ...), custom_call_target="tpu_custom_call" | custom-call | tf_op jit(solution)/shard_map/reading_stage/pallas_call | solution.py:530
  72.8 1.6 %all-to-all-done.1.start_ref = bf16[16,128,128]{2,1,0:T(8,128)(2,1)S(1)} async-done(((bf16[16,128,128]{2,1,0:T(8,128)(2,1)}), bf16[16,128,128]{2,1,0:T(8,128)(2,1)S(1)}, u32[]{:S(2)}, u32[]{:S(2)}) %all-to-all-start.1) | async-done | bytes 524320 | tf_op jit(solution)/shard_map/all_to_all | solution.py:752
  74.4 5.0 %finish_stage.1 = bf16[512,2048]{1,0:T(8,128)(2,1)} custom-call(s32[1]{0:T(128)} %bitcast.first_ref, bf16[16,128,128]{2,1,0:T(8,128)(2,1)S(1)} %all-to-all-done.1.start_ref, f32[1,128]{1,0:T(1,128)} %bitcast.5, bf16[8,512,128]{2,1,0:T(8,128)(2,1)} %get-tuple-element.50.refs_0_, bf16[8,512,128]{2,1,0:T(8,128)(2,1)} %get-tuple-element.51.refs_1_, ...), custom_call_target="tpu_custom_call" | custom-call | tf_op jit(solution)/shard_map/finish_stage/pallas_call | solution.py:684
  (1 shorter events, 0.0 us)
Async XLA Ops:
  0.9 7.4 %collective-permute-start = (bf16[8,4096]{1,0:T(8,128)(2,1)S(1)}, bf16[8,4096]{1,0:T(8,128)(2,1)S(1)}, u32[]{:S(2)}, u32[]{:S(2)}) collective-permute-start(bf16[8,4096]{1,0:T(8,128)(2,1)S(1)} %get-tuple-element.30), channel_id=1, source_target_pairs={{0,1},{1,2},{2,3},{3,4},{4,5},{5,6},{6,7},{7,8},{8,9},{9,10},{10,1... | collective-permute-start | bytes 196616 | tf_op jit(solution)/shard_map/ppermute | solution.py:729
  4.3 15.1 %collective-permute-start.1 = (f32[1,128,128]{2,1,0:T(8,128)S(1)}, f32[1,128,128]{2,1,0:T(8,128)S(1)}, u32[]{:S(2)}, u32[]{:S(2)}) collective-permute-start(f32[1,128,128]{2,1,0:T(8,128)S(1)} %get-tuple-element.31), channel_id=1, source_target_pairs={{0,1},{1,0},{2,3},{3,2},{4,5},{5,4},{6,7},{7,6},{8,9},{9,8},{10,11... | collective-permute-start | bytes 196616 | tf_op jit(solution)/shard_map/ppermute | solution.py:730
  31.4 18.7 %all-to-all-start = ((bf16[16,128,256]{2,1,0:T(8,128)(2,1)}), bf16[16,128,256]{2,1,0:T(8,128)(2,1)S(1)}, u32[]{:S(2)}, u32[]{:S(2)}) async-start(bf16[16,128,256]{2,1,0:T(8,128)(2,1)} %get-tuple-element.38), calls=%async_computation | async-start | bytes 2097152 | tf_op jit(solution)/shard_map/all_to_all | solution.py:742
  51.5 7.2 %collective-permute-start.2 = (f32[1,128,128]{2,1,0:T(8,128)S(1)}, f32[1,128,128]{2,1,0:T(8,128)S(1)}, u32[]{:S(2)}, u32[]{:S(2)}) collective-permute-start(f32[1,128,128]{2,1,0:T(8,128)S(1)} %slice.3), channel_id=1, source_target_pairs={{0,16},{1,17},{2,18},{3,19},{4,20},{5,21},{6,22},{7,23},{8,24},{9,... | collective-permute-start | bytes 196616 | tf_op jit(solution)/shard_map/ppermute | solution.py:707
  60.2 14.2 %all-to-all-start.1 = ((bf16[16,128,128]{2,1,0:T(8,128)(2,1)}), bf16[16,128,128]{2,1,0:T(8,128)(2,1)S(1)}, u32[]{:S(2)}, u32[]{:S(2)}) async-start(bf16[16,128,128]{2,1,0:T(8,128)(2,1)} %bitcast.2), calls=%async_computation.1 | async-start | bytes 1048576 | tf_op jit(solution)/shard_map/all_to_all | solution.py:752

commit v5 on v4

--- a/solution.py
+++ b/solution.py
@@ -47,6 +47,17 @@
 
 def lanes_of(start):
     return pl.ds(pl.multiple_of(start, DK), DK)
+
+
+def halves(array):
+    high = array.astype(bf16)
+    return high, (array - high.astype(f32)).astype(bf16)
+
+
+def product_left(left, right):
+    high, low = halves(left)
+    both = product(jnp.concatenate([high, low], axis=0), right)
+    return both[: left.shape[0]] + both[left.shape[0] :]
 
 
 def convolved(ext, cols, taps, c):
@@ -233,9 +244,9 @@
         for j, unit in units_of(c, g):
             at = slice(unit, unit + 1)
             by_rate = solved[unit] * rates[at]
-            fresh[unit] = product(by_rate.astype(bf16), channels(c, g, 2 + j))
+            fresh[unit] = product_left(by_rate, channels(c, g, 2 + j))
             by_rate = by_rate * (grown[at] * inverses[c, g])
-            carried[unit] = product(by_rate.astype(bf16), keys[c, g])
+            carried[unit] = product_left(by_rate, keys[c, g])
             scaled[unit] = (turned * tail[at]).astype(bf16)
 
     nothing = jnp.zeros((STRETCH, DK), f32)

time: 80.8 us -> 81.4 us (level)
  no operation moved by 1% of the time
where the time goes in v5:
time: 81.4 us; the launch traced here: 80.2 us
  Pallas kernels  47.5 us (58%)
  waiting for transfers between devices  18.8 us (23%)
  starting transfers between devices  13.6 us (17%)
    pallas_call x2, Pallas kernels, reading_stage(): pl.pallas_call(functools.partial(reading_kernel, number, index), grid_spe...  15 us
    pallas_call x1, Pallas kernels, local_stage(): pl.pallas_call(functools.partial(second_kernel, number, parts), in_specs=...  12.3 us
    pallas_call x1, Pallas kernels, local_stage(): pl.pallas_call(functools.partial(first_kernel, number, parts), in_specs=[...  11.3 us
    all_to_all x1, waiting for transfers between devices, per_device(): summary = lax.all_to_all(summary, NEAR, 0, 0, tiled=True)  7.3 us
    ppermute x1, waiting for transfers between devices, entering_state(): return lax.ppermute(total[..., :DK], 'outer', [(0, 1)])  5.86 us
    all_to_all x1, starting transfers between devices, per_device(): lax.all_to_all(starts.reshape(heads, DK, DK), NEAR, 0, 0, tiled=True)  5.01 us
    pallas_call x1, Pallas kernels, finish_stage(): pl.pallas_call(functools.partial(finish_kernel, batch), in_specs=[SMEM, V...  5 us
    ppermute x1, waiting for transfers between devices, per_device(): halo = lax.ppermute(tail, ALL, route)  3.95 us
  transfers between devices with their start and end apart: 5, of which 4 were waited for; matrix products, arithmetic and copies ran while one was open for 0% of the time, Pallas kernels for 33%

profile of v5, /device:TPU:16, one launch (start us, length us, event | category | flops | bytes accessed | tf_op | source)
XLA Modules:
  0.0 80.2 jit_solution(4623033986607199544)
XLA Ops:
  0.0 0.9 %pack_stage.1 = (bf16[8,4096]{1,0:T(8,128)(2,1)S(1)}, f32[1,128,128]{2,1,0:T(8,128)S(1)}, f32[1,128,128]{2,1,0:T(8,128)S(1)}) custom-call(s32[1]{0:T(128)} %bitcast.first_ref, bf16[512,4096]{1,0:T(8,128)(2,1)} %x_ref.7, f32[8,1024]{1,0:T(8,128)} %gate_ref.1, f32[8,1024]{1,0:T(8,128)} %rate_ref.1, bf16[4,2048]{1,0:T(4,128)(2,1)} %taps_ref.1), custom_call_target="tpu_custom_call" | custom-call | tf_op jit(solution)/shard_map/pack_stage/pallas_call | solution.py:172
  0.9 3.4 %collective-permute-start = (bf16[8,4096]{1,0:T(8,128)(2,1)S(1)}, bf16[8,4096]{1,0:T(8,128)(2,1)S(1)}, u32[]{:S(2)}, u32[]{:S(2)}) collective-permute-start(bf16[8,4096]{1,0:T(8,128)(2,1)S(1)} %get-tuple-element.30), channel_id=1, source_target_pairs={{0,1},{1,2},{2,3},{3,4},{4,5},{5,6},{6,7},{7,8},{8,9},{9,10},{10,1... | collective-permute-start | bytes 196616 | tf_op jit(solution)/shard_map/ppermute | solution.py:740
  4.3 0.1 collective-permute-start.1
  4.4 3.9 %collective-permute-done.halo_ref = bf16[8,4096]{1,0:T(8,128)(2,1)S(1)} collective-permute-done((bf16[8,4096]{1,0:T(8,128)(2,1)S(1)}, bf16[8,4096]{1,0:T(8,128)(2,1)S(1)}, u32[]{:S(2)}, u32[]{:S(2)}) %collective-permute-start) | collective-permute-done | bytes 65568 | tf_op jit(solution)/shard_map/ppermute | solution.py:740
  8.3 11.3 %first_stage.1 = (bf16[512,512]{1,0:T(8,128)(2,1)S(1)}, bf16[8,128,256]{2,1,0:T(8,128)(2,1)S(1)}, bf16[4,8,128,256]{3,2,1,0:T(8,128)(2,1)S(1)}, bf16[3,8,128,256...) custom-call(s32[1]{0:T(128)} %bitcast.first_ref, bf16[512,4096]{1,0:T(8,128)(2,1)} %x_ref.7, ...), custom_call_target="tpu_custom_call" | custom-call | tf_op jit(solution)/shard_map/first_stage/pallas_call | solution.py:443
  19.6 0.0 collective-permute-done.1.pack_ref
  19.6 12.3 %second_stage.1 = (bf16[16,128,256]{2,1,0:T(8,128)(2,1)}, bf16[2,4,8,128,256]{4,3,2,1,0:T(8,128)(2,1)}, bf16[2,4,8,128,256]{4,3,2,1,0:T(8,128)(2,1)}, bf16[2,512,512]{2,1,0:T(8,128)(2,1)}, f32[1,4,4,128]{3,2,1,0:T(4,128)S(1)}) custom-call(s32[1]{0:T(128)} %bitcast.first_ref, bf16[8,4096]{1,0:T(8,128)(2,1)S(1)} %collective-permute-done.halo_ref, ...), custom_call_target="tpu_custom_call" | custom-call | tf_op jit(solution)/shard_map/second_stage/pallas_call | solution.py:458
  32.0 3.8 %all-to-all-start = ((bf16[16,128,256]{2,1,0:T(8,128)(2,1)}), bf16[16,128,256]{2,1,0:T(8,128)(2,1)S(1)}, u32[]{:S(2)}, u32[]{:S(2)}) async-start(bf16[16,128,256]{2,1,0:T(8,128)(2,1)} %get-tuple-element.38), calls=%async_computation | async-start | bytes 2097152 | tf_op jit(solution)/shard_map/all_to_all | solution.py:753
  35.8 7.5 %reading_stage.2 = (bf16[8,512,128]{2,1,0:T(8,128)(2,1)}, bf16[8,512,128]{2,1,0:T(8,128)(2,1)}) custom-call(s32[1]{0:T(128)} %bitcast.first_ref, bf16[512,4096]{1,0:T(8,128)(2,1)} %x_ref.7, bf16[8,4096]{1,0:T(8,128)(2,1)S(1)} %collective-permute-done.halo_ref, f32[1,128,128]{2,1,0:T(8,128)S(1)} %get-tuple-element.32.pack_ref, ...), custom_call_target="tpu_custom_call" | custom-call | tf_op jit(solution)/shard_map/reading_stage/pallas_call | solution.py:541
  43.3 7.3 %all-to-all-done = bf16[16,128,256]{2,1,0:T(8,128)(2,1)S(1)} async-done(((bf16[16,128,256]{2,1,0:T(8,128)(2,1)}), bf16[16,128,256]{2,1,0:T(8,128)(2,1)S(1)}, u32[]{:S(2)}, u32[]{:S(2)}) %all-to-all-start) | async-done | bytes 1048608 | tf_op jit(solution)/shard_map/all_to_all | solution.py:753
  50.6 1.5 %chain_stage.1 = (f32[16,1,128,128]{3,2,1,0:T(8,128)S(1)}, bf16[16,1,128,128]{3,2,1,0:T(8,128)(2,1)S(1)}, f32[4,1,128,256]{3,2,1,0:T(8,128)S(1)}, f32[1,128,256]{2,1,0:T(8,128)S(1)}) custom-call(bf16[16,1,128,256]{3,2,1,0:T(8,128)(2,1)S(1)} %bitcast.4), custom_call_target="tpu_custom_call" | custom-call | tf_op jit(solution)/shard_map/chain_stage/pallas_call | solution.py:597
  52.1 1.3 %collective-permute-start.2 = (f32[1,128,128]{2,1,0:T(8,128)S(1)}, f32[1,128,128]{2,1,0:T(8,128)S(1)}, u32[]{:S(2)}, u32[]{:S(2)}) collective-permute-start(f32[1,128,128]{2,1,0:T(8,128)S(1)} %slice.3), channel_id=1, source_target_pairs={{0,16},{1,17},{2,18},{3,19},{4,20},{5,21},{6,22},{7,23},{8,24},{9,... | collective-permute-start | bytes 196616 | tf_op jit(solution)/shard_map/ppermute | solution.py:718
  53.4 5.9 %collective-permute-done.2.entering_ref = f32[1,128,128]{2,1,0:T(8,128)S(1)} collective-permute-done((f32[1,128,128]{2,1,0:T(8,128)S(1)}, f32[1,128,128]{2,1,0:T(8,128)S(1)}, u32[]{:S(2)}, u32[]{:S(2)}) %collective-permute-start.2) | collective-permute-done | bytes 65568 | tf_op jit(solution)/shard_map/ppermute | solution.py:718
  59.3 1.5 %entry_stage.1 = bf16[16,1,128,128]{3,2,1,0:T(8,128)(2,1)} custom-call(f32[16,1,128,128]{3,2,1,0:T(8,128)S(1)} %get-tuple-element.46.state_ref, bf16[16,1,128,128]{3,2,1,0:T(8,128)(2,1)S(1)} %get-tuple-element.47.loss_ref, f32[4,1,128,256]{3,2,1,0:T(8,128)S(1)} %get-tuple-element.48.sub_ref, f32[1,128,128]{2,1,0:T(8,128)S(1)} %collective-permute-done.2.entering_ref), custom_call_target="tpu_custom_call" | custom-call | tf_op jit(solution)/shard_map/entry_stage/pallas_call | solution.py:630
  60.8 5.0 %all-to-all-start.1 = ((bf16[16,128,128]{2,1,0:T(8,128)(2,1)}), bf16[16,128,128]{2,1,0:T(8,128)(2,1)S(1)}, u32[]{:S(2)}, u32[]{:S(2)}) async-start(bf16[16,128,128]{2,1,0:T(8,128)(2,1)} %bitcast.2), calls=%async_computation.1 | async-start | bytes 1048576 | tf_op jit(solution)/shard_map/all_to_all | solution.py:763
  65.8 7.5 %reading_stage.3 = (bf16[8,512,128]{2,1,0:T(8,128)(2,1)}, bf16[8,512,128]{2,1,0:T(8,128)(2,1)}) custom-call(s32[1]{0:T(128)} %bitcast.first_ref, bf16[512,4096]{1,0:T(8,128)(2,1)} %x_ref.7, bf16[8,4096]{1,0:T(8,128)(2,1)S(1)} %collective-permute-done.halo_ref, f32[1,128,128]{2,1,0:T(8,128)S(1)} %collective-permute-done.1.pack_ref, ...), custom_call_target="tpu_custom_call" | custom-call | tf_op jit(solution)/shard_map/reading_stage/pallas_call | solution.py:541
  73.3 1.6 %all-to-all-done.1.start_ref = bf16[16,128,128]{2,1,0:T(8,128)(2,1)S(1)} async-done(((bf16[16,128,128]{2,1,0:T(8,128)(2,1)}), bf16[16,128,128]{2,1,0:T(8,128)(2,1)S(1)}, u32[]{:S(2)}, u32[]{:S(2)}) %all-to-all-start.1) | async-done | bytes 524320 | tf_op jit(solution)/shard_map/all_to_all | solution.py:763
  75.0 5.0 %finish_stage.1 = bf16[512,2048]{1,0:T(8,128)(2,1)} custom-call(s32[1]{0:T(128)} %bitcast.first_ref, bf16[16,128,128]{2,1,0:T(8,128)(2,1)S(1)} %all-to-all-done.1.start_ref, f32[1,128]{1,0:T(1,128)} %bitcast.5, bf16[8,512,128]{2,1,0:T(8,128)(2,1)} %get-tuple-element.50.refs_0_, bf16[8,512,128]{2,1,0:T(8,128)(2,1)} %get-tuple-element.51.refs_1_, ...), custom_call_target="tpu_custom_call" | custom-call | tf_op jit(solution)/shard_map/finish_stage/pallas_call | solution.py:695
  (1 shorter events, 0.0 us)
Async XLA Ops:
  0.9 7.4 %collective-permute-start = (bf16[8,4096]{1,0:T(8,128)(2,1)S(1)}, bf16[8,4096]{1,0:T(8,128)(2,1)S(1)}, u32[]{:S(2)}, u32[]{:S(2)}) collective-permute-start(bf16[8,4096]{1,0:T(8,128)(2,1)S(1)} %get-tuple-element.30), channel_id=1, source_target_pairs={{0,1},{1,2},{2,3},{3,4},{4,5},{5,6},{6,7},{7,8},{8,9},{9,10},{10,1... | collective-permute-start | bytes 196616 | tf_op jit(solution)/shard_map/ppermute | solution.py:740
  4.3 15.3 %collective-permute-start.1 = (f32[1,128,128]{2,1,0:T(8,128)S(1)}, f32[1,128,128]{2,1,0:T(8,128)S(1)}, u32[]{:S(2)}, u32[]{:S(2)}) collective-permute-start(f32[1,128,128]{2,1,0:T(8,128)S(1)} %get-tuple-element.31), channel_id=1, source_target_pairs={{0,1},{1,0},{2,3},{3,2},{4,5},{5,4},{6,7},{7,6},{8,9},{9,8},{10,11... | collective-permute-start | bytes 196616 | tf_op jit(solution)/shard_map/ppermute | solution.py:741
  32.0 18.7 %all-to-all-start = ((bf16[16,128,256]{2,1,0:T(8,128)(2,1)}), bf16[16,128,256]{2,1,0:T(8,128)(2,1)S(1)}, u32[]{:S(2)}, u32[]{:S(2)}) async-start(bf16[16,128,256]{2,1,0:T(8,128)(2,1)} %get-tuple-element.38), calls=%async_computation | async-start | bytes 2097152 | tf_op jit(solution)/shard_map/all_to_all | solution.py:753
  52.1 7.2 %collective-permute-start.2 = (f32[1,128,128]{2,1,0:T(8,128)S(1)}, f32[1,128,128]{2,1,0:T(8,128)S(1)}, u32[]{:S(2)}, u32[]{:S(2)}) collective-permute-start(f32[1,128,128]{2,1,0:T(8,128)S(1)} %slice.3), channel_id=1, source_target_pairs={{0,16},{1,17},{2,18},{3,19},{4,20},{5,21},{6,22},{7,23},{8,24},{9,... | collective-permute-start | bytes 196616 | tf_op jit(solution)/shard_map/ppermute | solution.py:718
  60.8 14.2 %all-to-all-start.1 = ((bf16[16,128,128]{2,1,0:T(8,128)(2,1)}), bf16[16,128,128]{2,1,0:T(8,128)(2,1)S(1)}, u32[]{:S(2)}, u32[]{:S(2)}) async-start(bf16[16,128,128]{2,1,0:T(8,128)(2,1)} %bitcast.2), calls=%async_computation.1 | async-start | bytes 1048576 | tf_op jit(solution)/shard_map/all_to_all | solution.py:763

commit v6 on v5

--- a/solution.py
+++ b/solution.py
@@ -691,7 +691,7 @@
 def finish_stage(first, reads, starts, gain):
     heads, length, _ = reads[0][0].shape
     all_heads = starts.shape[0]
-    batch = 2
+    batch = min(4, heads)
     return pl.pallas_call(
         functools.partial(finish_kernel, batch),
         in_specs=[SMEM, VMEM, FAR] + [FAR] * (2 * len(reads)),

time: 81.4 us -> 80.6 us (level)
  no operation moved by 1% of the time
where the time goes in v6:
time: 80.6 us; the launch traced here: 79.4 us
  Pallas kernels  46.8 us (58%)
  waiting for transfers between devices  18.8 us (23%)
  starting transfers between devices  13.6 us (17%)
    pallas_call x2, Pallas kernels, reading_stage(): pl.pallas_call(functools.partial(reading_kernel, number, index), grid_spe...  15 us
    pallas_call x1, Pallas kernels, local_stage(): pl.pallas_call(functools.partial(second_kernel, number, parts), in_specs=...  12.3 us
    pallas_call x1, Pallas kernels, local_stage(): pl.pallas_call(functools.partial(first_kernel, number, parts), in_specs=[...  11.3 us
    all_to_all x1, waiting for transfers between devices, per_device(): summary = lax.all_to_all(summary, NEAR, 0, 0, tiled=True)  7.3 us
    ppermute x1, waiting for transfers between devices, entering_state(): return lax.ppermute(total[..., :DK], 'outer', [(0, 1)])  5.86 us
    all_to_all x1, starting transfers between devices, per_device(): lax.all_to_all(starts.reshape(heads, DK, DK), NEAR, 0, 0, tiled=True)  5 us
    pallas_call x1, Pallas kernels, finish_stage(): pl.pallas_call(functools.partial(finish_kernel, batch), in_specs=[SMEM, V...  4.25 us
    ppermute x1, waiting for transfers between devices, per_device(): halo = lax.ppermute(tail, ALL, route)  3.95 us
  transfers between devices with their start and end apart: 5, of which 4 were waited for; matrix products, arithmetic and copies ran while one was open for 0% of the time, Pallas kernels for 33%

profile of v6, /device:TPU:16, one launch (start us, length us, event | category | flops | bytes accessed | tf_op | source)
XLA Modules:
  0.0 79.4 jit_solution(18272737573391476156)
XLA Ops:
  0.0 0.9 %pack_stage.1 = (bf16[8,4096]{1,0:T(8,128)(2,1)S(1)}, f32[1,128,128]{2,1,0:T(8,128)S(1)}, f32[1,128,128]{2,1,0:T(8,128)S(1)}) custom-call(s32[1]{0:T(128)} %bitcast.first_ref, bf16[512,4096]{1,0:T(8,128)(2,1)} %x_ref.7, f32[8,1024]{1,0:T(8,128)} %gate_ref.1, f32[8,1024]{1,0:T(8,128)} %rate_ref.1, bf16[4,2048]{1,0:T(4,128)(2,1)} %taps_ref.1), custom_call_target="tpu_custom_call" | custom-call | tf_op jit(solution)/shard_map/pack_stage/pallas_call | solution.py:172
  0.9 3.4 %collective-permute-start = (bf16[8,4096]{1,0:T(8,128)(2,1)S(1)}, bf16[8,4096]{1,0:T(8,128)(2,1)S(1)}, u32[]{:S(2)}, u32[]{:S(2)}) collective-permute-start(bf16[8,4096]{1,0:T(8,128)(2,1)S(1)} %get-tuple-element.30), channel_id=1, source_target_pairs={{0,1},{1,2},{2,3},{3,4},{4,5},{5,6},{6,7},{7,8},{8,9},{9,10},{10,1... | collective-permute-start | bytes 196616 | tf_op jit(solution)/shard_map/ppermute | solution.py:740
  4.3 0.1 collective-permute-start.1
  4.4 3.9 %collective-permute-done.halo_ref = bf16[8,4096]{1,0:T(8,128)(2,1)S(1)} collective-permute-done((bf16[8,4096]{1,0:T(8,128)(2,1)S(1)}, bf16[8,4096]{1,0:T(8,128)(2,1)S(1)}, u32[]{:S(2)}, u32[]{:S(2)}) %collective-permute-start) | collective-permute-done | bytes 65568 | tf_op jit(solution)/shard_map/ppermute | solution.py:740
  8.3 11.3 %first_stage.1 = (bf16[512,512]{1,0:T(8,128)(2,1)S(1)}, bf16[8,128,256]{2,1,0:T(8,128)(2,1)S(1)}, bf16[4,8,128,256]{3,2,1,0:T(8,128)(2,1)S(1)}, bf16[3,8,128,256...) custom-call(s32[1]{0:T(128)} %bitcast.first_ref, bf16[512,4096]{1,0:T(8,128)(2,1)} %x_ref.7, ...), custom_call_target="tpu_custom_call" | custom-call | tf_op jit(solution)/shard_map/first_stage/pallas_call | solution.py:443
  19.6 0.0 collective-permute-done.1.pack_ref
  19.6 12.3 %second_stage.1 = (bf16[16,128,256]{2,1,0:T(8,128)(2,1)}, bf16[2,4,8,128,256]{4,3,2,1,0:T(8,128)(2,1)}, bf16[2,4,8,128,256]{4,3,2,1,0:T(8,128)(2,1)}, bf16[2,512,512]{2,1,0:T(8,128)(2,1)}, f32[1,4,4,128]{3,2,1,0:T(4,128)S(1)}) custom-call(s32[1]{0:T(128)} %bitcast.first_ref, bf16[8,4096]{1,0:T(8,128)(2,1)S(1)} %collective-permute-done.halo_ref, ...), custom_call_target="tpu_custom_call" | custom-call | tf_op jit(solution)/shard_map/second_stage/pallas_call | solution.py:458
  32.0 3.8 %all-to-all-start = ((bf16[16,128,256]{2,1,0:T(8,128)(2,1)}), bf16[16,128,256]{2,1,0:T(8,128)(2,1)S(1)}, u32[]{:S(2)}, u32[]{:S(2)}) async-start(bf16[16,128,256]{2,1,0:T(8,128)(2,1)} %get-tuple-element.38), calls=%async_computation | async-start | bytes 2097152 | tf_op jit(solution)/shard_map/all_to_all | solution.py:753
  35.8 7.5 %reading_stage.2 = (bf16[8,512,128]{2,1,0:T(8,128)(2,1)}, bf16[8,512,128]{2,1,0:T(8,128)(2,1)}) custom-call(s32[1]{0:T(128)} %bitcast.first_ref, bf16[512,4096]{1,0:T(8,128)(2,1)} %x_ref.7, bf16[8,4096]{1,0:T(8,128)(2,1)S(1)} %collective-permute-done.halo_ref, f32[1,128,128]{2,1,0:T(8,128)S(1)} %get-tuple-element.32.pack_ref, ...), custom_call_target="tpu_custom_call" | custom-call | tf_op jit(solution)/shard_map/reading_stage/pallas_call | solution.py:541
  43.3 7.3 %all-to-all-done = bf16[16,128,256]{2,1,0:T(8,128)(2,1)S(1)} async-done(((bf16[16,128,256]{2,1,0:T(8,128)(2,1)}), bf16[16,128,256]{2,1,0:T(8,128)(2,1)S(1)}, u32[]{:S(2)}, u32[]{:S(2)}) %all-to-all-start) | async-done | bytes 1048608 | tf_op jit(solution)/shard_map/all_to_all | solution.py:753
  50.6 1.5 %chain_stage.1 = (f32[16,1,128,128]{3,2,1,0:T(8,128)S(1)}, bf16[16,1,128,128]{3,2,1,0:T(8,128)(2,1)S(1)}, f32[4,1,128,256]{3,2,1,0:T(8,128)S(1)}, f32[1,128,256]{2,1,0:T(8,128)S(1)}) custom-call(bf16[16,1,128,256]{3,2,1,0:T(8,128)(2,1)S(1)} %bitcast.4), custom_call_target="tpu_custom_call" | custom-call | tf_op jit(solution)/shard_map/chain_stage/pallas_call | solution.py:597
  52.1 1.3 %collective-permute-start.2 = (f32[1,128,128]{2,1,0:T(8,128)S(1)}, f32[1,128,128]{2,1,0:T(8,128)S(1)}, u32[]{:S(2)}, u32[]{:S(2)}) collective-permute-start(f32[1,128,128]{2,1,0:T(8,128)S(1)} %slice.3), channel_id=1, source_target_pairs={{0,16},{1,17},{2,18},{3,19},{4,20},{5,21},{6,22},{7,23},{8,24},{9,... | collective-permute-start | bytes 196616 | tf_op jit(solution)/shard_map/ppermute | solution.py:718
  53.4 5.9 %collective-permute-done.2.entering_ref = f32[1,128,128]{2,1,0:T(8,128)S(1)} collective-permute-done((f32[1,128,128]{2,1,0:T(8,128)S(1)}, f32[1,128,128]{2,1,0:T(8,128)S(1)}, u32[]{:S(2)}, u32[]{:S(2)}) %collective-permute-start.2) | collective-permute-done | bytes 65568 | tf_op jit(solution)/shard_map/ppermute | solution.py:718
  59.3 1.5 %entry_stage.1 = bf16[16,1,128,128]{3,2,1,0:T(8,128)(2,1)} custom-call(f32[16,1,128,128]{3,2,1,0:T(8,128)S(1)} %get-tuple-element.46.state_ref, bf16[16,1,128,128]{3,2,1,0:T(8,128)(2,1)S(1)} %get-tuple-element.47.loss_ref, f32[4,1,128,256]{3,2,1,0:T(8,128)S(1)} %get-tuple-element.48.sub_ref, f32[1,128,128]{2,1,0:T(8,128)S(1)} %collective-permute-done.2.entering_ref), custom_call_target="tpu_custom_call" | custom-call | tf_op jit(solution)/shard_map/entry_stage/pallas_call | solution.py:630
  60.8 5.0 %all-to-all-start.1 = ((bf16[16,128,128]{2,1,0:T(8,128)(2,1)}), bf16[16,128,128]{2,1,0:T(8,128)(2,1)S(1)}, u32[]{:S(2)}, u32[]{:S(2)}) async-start(bf16[16,128,128]{2,1,0:T(8,128)(2,1)} %bitcast.2), calls=%async_computation.1 | async-start | bytes 1048576 | tf_op jit(solution)/shard_map/all_to_all | solution.py:763
  65.8 7.5 %reading_stage.3 = (bf16[8,512,128]{2,1,0:T(8,128)(2,1)}, bf16[8,512,128]{2,1,0:T(8,128)(2,1)}) custom-call(s32[1]{0:T(128)} %bitcast.first_ref, bf16[512,4096]{1,0:T(8,128)(2,1)} %x_ref.7, bf16[8,4096]{1,0:T(8,128)(2,1)S(1)} %collective-permute-done.halo_ref, f32[1,128,128]{2,1,0:T(8,128)S(1)} %collective-permute-done.1.pack_ref, ...), custom_call_target="tpu_custom_call" | custom-call | tf_op jit(solution)/shard_map/reading_stage/pallas_call | solution.py:541
  73.3 1.7 %all-to-all-done.1.start_ref = bf16[16,128,128]{2,1,0:T(8,128)(2,1)S(1)} async-done(((bf16[16,128,128]{2,1,0:T(8,128)(2,1)}), bf16[16,128,128]{2,1,0:T(8,128)(2,1)S(1)}, u32[]{:S(2)}, u32[]{:S(2)}) %all-to-all-start.1) | async-done | bytes 524320 | tf_op jit(solution)/shard_map/all_to_all | solution.py:763
  75.0 4.3 %finish_stage.1 = bf16[512,2048]{1,0:T(8,128)(2,1)} custom-call(s32[1]{0:T(128)} %bitcast.first_ref, bf16[16,128,128]{2,1,0:T(8,128)(2,1)S(1)} %all-to-all-done.1.start_ref, f32[1,128]{1,0:T(1,128)} %bitcast.5, bf16[8,512,128]{2,1,0:T(8,128)(2,1)} %get-tuple-element.50.refs_0_, bf16[8,512,128]{2,1,0:T(8,128)(2,1)} %get-tuple-element.51.refs_1_, ...), custom_call_target="tpu_custom_call" | custom-call | tf_op jit(solution)/shard_map/finish_stage/pallas_call | solution.py:695
  (1 shorter events, 0.0 us)
Async XLA Ops:
  0.9 7.4 %collective-permute-start = (bf16[8,4096]{1,0:T(8,128)(2,1)S(1)}, bf16[8,4096]{1,0:T(8,128)(2,1)S(1)}, u32[]{:S(2)}, u32[]{:S(2)}) collective-permute-start(bf16[8,4096]{1,0:T(8,128)(2,1)S(1)} %get-tuple-element.30), channel_id=1, source_target_pairs={{0,1},{1,2},{2,3},{3,4},{4,5},{5,6},{6,7},{7,8},{8,9},{9,10},{10,1... | collective-permute-start | bytes 196616 | tf_op jit(solution)/shard_map/ppermute | solution.py:740
  4.3 15.3 %collective-permute-start.1 = (f32[1,128,128]{2,1,0:T(8,128)S(1)}, f32[1,128,128]{2,1,0:T(8,128)S(1)}, u32[]{:S(2)}, u32[]{:S(2)}) collective-permute-start(f32[1,128,128]{2,1,0:T(8,128)S(1)} %get-tuple-element.31), channel_id=1, source_target_pairs={{0,1},{1,0},{2,3},{3,2},{4,5},{5,4},{6,7},{7,6},{8,9},{9,8},{10,11... | collective-permute-start | bytes 196616 | tf_op jit(solution)/shard_map/ppermute | solution.py:741
  32.0 18.7 %all-to-all-start = ((bf16[16,128,256]{2,1,0:T(8,128)(2,1)}), bf16[16,128,256]{2,1,0:T(8,128)(2,1)S(1)}, u32[]{:S(2)}, u32[]{:S(2)}) async-start(bf16[16,128,256]{2,1,0:T(8,128)(2,1)} %get-tuple-element.38), calls=%async_computation | async-start | bytes 2097152 | tf_op jit(solution)/shard_map/all_to_all | solution.py:753
  52.1 7.2 %collective-permute-start.2 = (f32[1,128,128]{2,1,0:T(8,128)S(1)}, f32[1,128,128]{2,1,0:T(8,128)S(1)}, u32[]{:S(2)}, u32[]{:S(2)}) collective-permute-start(f32[1,128,128]{2,1,0:T(8,128)S(1)} %slice.3), channel_id=1, source_target_pairs={{0,16},{1,17},{2,18},{3,19},{4,20},{5,21},{6,22},{7,23},{8,24},{9,... | collective-permute-start | bytes 196616 | tf_op jit(solution)/shard_map/ppermute | solution.py:718
  60.8 14.2 %all-to-all-start.1 = ((bf16[16,128,128]{2,1,0:T(8,128)(2,1)}), bf16[16,128,128]{2,1,0:T(8,128)(2,1)S(1)}, u32[]{:S(2)}, u32[]{:S(2)}) async-start(bf16[16,128,128]{2,1,0:T(8,128)(2,1)} %bitcast.2), calls=%async_computation.1 | async-start | bytes 1048576 | tf_op jit(solution)/shard_map/all_to_all | solution.py:763
